TPU v7x, 256 devices: a whole 4x4x8 slice. The times are simulated.
256 devices in a mesh: lev: 16 (over y, x_hi, core), lat: 16 (over z, x_lo).
Axes of the slice: x: 4 (x_hi: 2, x_lo: 2; x = x_hi * 2 + x_lo), y: 4, z: 8, core: 2. Of those that a mesh axis runs over, the one named last changes fastest.
Arguments:
- adjoint_in: float32 [8, 128, 64, 2048], P(None, 'lev', 'lat'), may hold values from -6 to 6
- courant_lon: float32 [128, 64, 2048], P('lev', 'lat'), may hold values from -0.24 to 0.24
- courant_lat: float32 [128, 64, 2048], P('lev', 'lat'), may hold values from -0.24 to 0.24, as said below
- mass_flux: float32 [64, 2048], P('lat'), may hold values from 0.1 to 0.9
- conv_band: int32 [2, 64, 2048], P(None, 'lat'), may hold values from 48 to 128, as said below
- diff_inverse: float32 [64, 8, 16, 16], P('lat'), may hold values from 0 to 1
- obs_values: float32 [16, 16, 16, 16, 128], P('lev', 'lat'), may hold values from -6 to 6
- obs_column: int32 [16, 16, 16, 16], P('lev', 'lat'), may hold values from 0 to 511
- obs_count: int32 [16, 16, 16], P('lev', 'lat'), may hold values from 0 to 16, as said below
Outputs:
- adjoint_out: float32 [8, 128, 64, 2048], P(None, 'lev', 'lat')
Inputs may be any that keep to these rules, and one draw needn't show every extreme that they name: `courant_lat`: the south face of the first latitude row carries no flow. `conv_band`: bands hold 4 to 64 levels. `obs_count`: slots at and after the count hold padding. `obs_column`: several soundings may share a column.
All inputs are finite; a program needn't handle non-finite values.
Results may differ from a plain program's by a relative error of at most 0.00007.
Values sent between devices are 32-bit elements; how exact they have to be, the bound alone decides.
No kernel may reach another device: no remote copies, remote signals or barrier semaphores. Data moves between devices by JAX's collectives and lax.ppermute only.
A program may use at most 128 MiB of HBM per device.

v0:
```python
import jax
import jax.numpy as jnp
from jax import lax
from jax.sharding import PartitionSpec as P

ADV_STEPS = 2


def from_behind(value, axis, steps):
    count = lax.axis_size(axis)
    initial, last = (max(0, -steps), min(count, count - steps))
    return lax.ppermute(value, axis, [(source, source + steps) for source in range(initial, last)])


def padded_2(cells, sides, width):
    for axis, dim in sides:
        count = lax.axis_size(axis)
        ends = count - 1
        head = lax.slice_in_dim(cells, 0, width, axis=dim)
        tail = lax.slice_in_dim(cells, cells.shape[dim] - width, cells.shape[dim], axis=dim)
        cells = jnp.concatenate(
            [
                lax.ppermute(tail, axis, [(i, (i + 1) % count) for i in range(ends)]),
                cells,
                lax.ppermute(head, axis, [((i + 1) % count, i) for i in range(ends)]),
            ],
            axis=dim,
        )
    return cells


def advect(padded_rows, lat_faces, lon_faces):
    row_total = lon_faces.shape[-2]
    center_rows = padded_rows[..., 1 : row_total + 1, :]
    northern = padded_rows[..., 2 : row_total + 2, :]
    southern = padded_rows[..., 0:row_total, :]
    face_south = lat_faces[..., 0:row_total, :]
    face_north = lat_faces[..., 1 : row_total + 1, :]
    face_east = jnp.roll(lon_faces, -1, axis=-1)
    eastern = jnp.roll(center_rows, -1, axis=-1)
    western = jnp.roll(center_rows, 1, axis=-1)
    flow_east = jnp.maximum(face_east, 0.0)
    flow_west = jnp.minimum(lon_faces, 0.0)
    flow_north = jnp.maximum(face_north, 0.0)
    flow_south = jnp.minimum(face_south, 0.0)
    center = 1.0 - flow_east + flow_west - flow_north + flow_south
    return (
        center_rows * center
        + eastern * flow_east
        - western * flow_west
        + northern * flow_north
        - southern * flow_south
    )


def body(
    adjoint_in,
    courant_lon,
    courant_lat,
    mass_flux,
    conv_band,
    diff_inverse,
    obs_values,
    obs_column,
    obs_count,
):
    tracer_count, level_count, row_count, lon_count = adjoint_in.shape
    lev_count = lax.axis_size("lev")
    lev_index = lax.axis_index("lev")
    north_faces = from_behind(courant_lat[:, :1], "lat", -1)
    lat_faces = jnp.concatenate([courant_lat, north_faces], axis=1)
    state = adjoint_in
    for substep in range(ADV_STEPS):
        padded = padded_2(state, (("lat", 2),), 1)
        state = advect(padded, lat_faces, courant_lon)
    received_values, received_column, received_count = (
        lax.all_to_all(obs_values, "lat", split_axis=2, concat_axis=2, tiled=True),
        lax.all_to_all(obs_column, "lat", split_axis=2, concat_axis=2, tiled=True),
        lax.all_to_all(obs_count, "lat", split_axis=2, concat_axis=2, tiled=True),
    )
    all_level_count = received_values.shape[-1]
    block_width = row_count * lon_count // lev_count
    slot_ids = lax.broadcasted_iota(jnp.int32, received_column.shape, 3)
    valid_slot = (slot_ids < received_count[..., None]).reshape(-1)
    column_ids = lax.broadcasted_iota(jnp.int32, (1, block_width), 1)
    one_hot = ((received_column.reshape(-1)[:, None] == column_ids) & valid_slot[:, None]).astype(
        jnp.float32
    )
    forcing = jnp.einsum(
        "sl,sc->lc",
        received_values.reshape(-1, all_level_count),
        one_hot,
        precision=lax.Precision.HIGHEST,
    )
    block_start = lev_index * block_width
    row_here = block_start // lon_count
    band_here = lax.dynamic_slice_in_dim(
        conv_band.reshape(2, row_count * lon_count), block_start, block_width, axis=1
    )
    kappa_here = lax.dynamic_slice_in_dim(
        mass_flux.reshape(row_count * lon_count), block_start, block_width, axis=0
    )
    inverse_here = lax.dynamic_index_in_dim(diff_inverse, row_here, axis=0, keepdims=False)
    block_count, block_size = (inverse_here.shape[0], inverse_here.shape[1])
    all_levels = lax.broadcasted_iota(jnp.int32, (all_level_count, 1), 0)
    inside = ((all_levels >= band_here[0][None]) & (all_levels < band_here[1][None])).astype(
        jnp.float32
    )
    counted = (band_here[1] - band_here[0]).astype(jnp.float32)
    flattened = state.reshape(tracer_count, level_count, row_count * lon_count)
    columns = lax.all_to_all(flattened, "lev", split_axis=2, concat_axis=1, tiled=True)
    item_count = columns.shape[0]
    band_mean = jnp.sum(columns * inside[None], axis=1) / counted
    mixed = columns + kappa_here * inside[None] * (band_mean[:, None] - columns)
    blocked = mixed.reshape(item_count, block_count, block_size, block_width)
    diffused = jnp.einsum("bij,tbjc->tbic", inverse_here, blocked, precision=lax.Precision.HIGHEST)
    diffused = diffused.reshape(item_count, all_level_count, block_width) + forcing[None]
    result = lax.all_to_all(diffused, "lev", split_axis=1, concat_axis=2, tiled=True)
    result = result.reshape(tracer_count, level_count, row_count, lon_count)
    return result


def solution(mesh):
    placed = (
        P(None, "lev", "lat", None),
        P("lev", "lat", None),
        P("lev", "lat", None),
        P("lat", None),
        P(None, "lat", None),
        P("lat", None, None, None),
        P("lev", "lat", None, None, None),
        P("lev", "lat", None, None),
        P("lev", "lat", None),
    )
    return jax.shard_map(
        body, mesh=mesh, in_specs=placed, out_specs=P(None, "lev", "lat", None), check_vma=False
    )
```

profile of v0, /device:TPU:1, one launch (start us, length us, event | category | flops | bytes accessed | tf_op | source)
XLA Modules:
  0.0 275.3 jit_solution(9481989879173830036)
XLA Ops:
  0.0 1.0 slice.87
  1.0 1.3 collective-permute-start
  2.3 2.8 %copy.42 = f32[8,8,4,2048]{3,1,2,0:T(8,128)S(1)} copy(f32[8,8,4,2048]{3,2,1,0:T(4,128)} %param.9) | data formatting | bytes 4194304 | tf_op args[0]
  5.2 1.0 fusion.33
  6.2 1.3 collective-permute-start.1
  7.5 6.0 %collective-permute-start.2 = (f32[8,8,1,2048]{3,1,2,0:T(8,128)}, f32[8,8,1,2048]{3,1,2,0:T(8,128)}, u32[]{:S(2)}, u32[]{:S(2)}) collective-permute-start(f32[8,8,1,2048]{3,1,2,0:T(8,128)} %get-tuple-element.22), channel_id=1, source_target_pairs={{0,1},{1,2},{2,3},{3,4},{4,5},{5,6},{6,7},{7,8},{8,9},{9,10},{10,1... | collective-permute-start | bytes 1572872 | tf_op jit(solution)/shard_map/ppermute | solution.py:23
  13.5 0.7 copy.62
  14.2 9.8 %all-to-all-start.2 = ((s32[1,1,16]{1,0,2:T(1,128)}), s32[1,1,16]{1,0,2:T(1,128)S(1)}, u32[]{:S(2)}, u32[]{:S(2)}) async-start(s32[1,1,16]{1,0,2:T(1,128)} %copy.62), calls=%async_computation.2 | async-start | bytes 16384 | tf_op jit(solution)/shard_map/all_to_all | solution.py:79
  24.0 0.8 fusion.32
  24.8 0.1 fusion.31
  24.9 0.1 copy-done.4
  24.9 0.2 slice.85
  25.2 0.4 subtract_add_fusion
  25.6 0.2 copy.41
  25.7 0.2 copy.45
  25.9 0.2 copy.48
  26.1 0.2 copy.51
  26.2 0.2 copy.54
  26.4 8.5 %collective-permute-done.2 = f32[8,8,1,2048]{3,1,2,0:T(8,128)} collective-permute-done((f32[8,8,1,2048]{3,1,2,0:T(8,128)}, f32[8,8,1,2048]{3,1,2,0:T(8,128)}, u32[]{:S(2)}, u32[]{:S(2)}) %collective-permute-start.2) | collective-permute-done | bytes 524320 | tf_op jit(solution)/shard_map/ppermute | solution.py:23
  34.9 2.7 fusion.5
  37.7 0.1 fusion.30
  37.8 1.3 collective-permute-start.3
  39.1 4.8 %collective-permute-start.4 = (f32[8,8,1,2048]{3,1,2,0:T(8,128)S(1)}, f32[8,8,1,2048]{3,1,2,0:T(8,128)S(1)}, u32[]{:S(2)}, u32[]{:S(2)}) collective-permute-start(f32[8,8,1,2048]{3,1,2,0:T(8,128)S(1)} %get-tuple-element.16), channel_id=1, source_target_pairs={{0,1},{1,2},{2,3},{3,4},{4,5},{5,6},{6,7},{7,8},{8,9},{9,10},{10,1... | collective-permute-start | bytes 1572872 | tf_op jit(solution)/shard_map/ppermute | solution.py:23
  43.9 2.7 fusion.29
  46.6 10.6 %all-to-all-start.1 = ((s32[1,1,16,16]{3,1,0,2:T(1,128)}), s32[1,1,16,16]{3,1,0,2:T(1,128)S(1)}, u32[]{:S(2)}, u32[]{:S(2)}) async-start(s32[1,1,16,16]{3,1,0,2:T(1,128)} %bitcast.14), calls=%async_computation.1 | async-start | bytes 16384 | tf_op jit(solution)/shard_map/all_to_all | solution.py:78
  57.2 1.6 fusion.28
  58.8 7.0 %all-to-all-done.1 = s32[1,1,16,16]{3,1,0,2:T(1,128)S(1)} async-done(((s32[1,1,16,16]{3,1,0,2:T(1,128)}), s32[1,1,16,16]{3,1,0,2:T(1,128)S(1)}, u32[]{:S(2)}, u32[]{:S(2)}) %all-to-all-start.1) | async-done | bytes 1056 | tf_op jit(solution)/shard_map/all_to_all | solution.py:78
  65.8 10.5 %all-to-all-start.3 = ((f32[1,1,16,16,128]{4,3,1,0,2:T(8,128)}), f32[1,1,16,16,128]{4,3,1,0,2:T(8,128)}, u32[]{:S(2)}, u32[]{:S(2)}) async-start(f32[1,1,16,16,128]{4,3,1,0,2:T(8,128)} %bitcast.53), calls=%async_computation.3 | async-start | bytes 262144 | tf_op jit(solution)/shard_map/all_to_all | solution.py:77
  76.3 0.8 copy-done.5
  77.1 0.2 copy-done.6
  77.3 5.5 %fusion.1 = f32[8,8,4,2048]{3,1,2,0:T(8,128)S(1)} fusion(f32[8,8,4,2048]{3,1,2,0:T(8,128)} %copy-done.1, f32[8,8,1,2048]{3,1,2,0:T(8,128)} %copy-done.6, f32[8,8,1,2048]{3,1,2,0:T(8,128)} %copy-done.5, f32[8,8,4,1]{3,1,2,0:T(8,128)} %get-tuple-element.12, f32[8,8,4,2047]{3,1,2,0:T(8,128)} %get-tuple-element.14, f32[8,8,4,2047]{3,1,2,0:T(8,128)} %get-tuple-element.13, ...), kind=kLoop, calls=%fused_computation.2 | loop fusion | flops 6815744 | bytes 10747904 | tf_op jit(solution)/shard_map/sub | solution.py:48
  82.8 15.9 %copy.56 = f32[8,8,8192]{1,0,2:T(8,128)} copy(f32[8,8,8192]{2,1,0:T(8,128)S(1)} %bitcast.51) | data formatting | bytes 4194304 | tf_op jit(solution)/shard_map/reshape | solution.py:110
  98.7 24.3 %reshape.209 = f32[16,1,32768]{2,1,0:T(1,128)} reshape(f32[8192,8,8]{2,1,0:T(8,128)} %bitcast.49) | data formatting | bytes 4194304
  123.0 7.9 %all-to-all-start = ((f32[16,1,32768]{2,1,0:T(1,128)}), f32[16,1,32768]{2,1,0:T(1,128)S(1)}, u32[]{:S(2)}, u32[]{:S(2)}) async-start(f32[16,1,32768]{2,1,0:T(1,128)} %reshape.209), calls=%async_computation | async-start | bytes 4194304 | tf_op jit(solution)/shard_map/all_to_all | solution.py:111
  130.9 0.1 copy.72
  131.0 0.1 iota.43
  131.1 0.1 dynamic_slice.11
  131.2 0.1 subtract_convert_fusion
  131.3 0.1 and_convert_fusion
  131.4 0.1 and_select_fusion
  131.5 0.4 reduce.2
  131.9 0.1 broadcast_reduce_fusion
  132.0 0.1 lt.53
  132.1 0.6 broadcast.151
  132.7 0.7 reduce.9
  133.4 0.1 eq.15
  133.5 1.6 convolution_bitcast_fusion
  135.1 0.1 copy.64
  135.2 24.0 %all-to-all-done = f32[16,1,32768]{2,1,0:T(1,128)S(1)} async-done(((f32[16,1,32768]{2,1,0:T(1,128)}), f32[16,1,32768]{2,1,0:T(1,128)S(1)}, u32[]{:S(2)}, u32[]{:S(2)}) %all-to-all-start) | async-done | bytes 2097184 | tf_op jit(solution)/shard_map/all_to_all | solution.py:111
  159.3 1.3 copy-done.2
  160.6 0.6 broadcast.154
  161.2 7.3 %reduce.10 = f32[16,32768]{1,0:T(8,128)S(1)} reduce(f32[16,1,32768]{2,1,0:T(1,128)} %copy-done.2, f32[]{:T(128)} %broadcast.154), dimensions={1}, to_apply=%all_to_all.35.reduce_sub_computation | reduce | bytes 4194308 | tf_op jit(solution)/shard_map/all_to_all | solution.py:111
  168.5 29.8 %reshape.210 = f32[8192,8,8]{2,1,0:T(8,128)} reshape(f32[16,32768]{1,0:T(8,128)S(1)} %reduce.10) | data formatting | bytes 4194304
  198.3 16.2 %copy.69 = f32[8,8,16,512]{3,2,1,0:T(8,128)} copy(f32[8,8,16,512]{1,0,3,2:T(8,128)} %bitcast.47) | data formatting | bytes 4194304 | tf_op jit(solution)/shard_map/all_to_all | solution.py:111
  214.6 19.3 %copy.58 = f32[8,16,8,512]{3,2,1,0:T(8,128)S(1)} copy(f32[8,16,8,512]{2,0,3,1:T(8,128)} %bitcast.48) | data formatting | bytes 4194304 | tf_op jit(solution)/shard_map/all_to_all | solution.py:111
  233.9 1.9 fusion.13
  235.8 0.3 bitcast_add_fusion.1
  236.1 1.9 fusion.16
  238.0 0.3 copy.60
  238.4 0.3 bitcast_add_fusion
  238.7 1.2 copy.65
  239.9 31.9 %all_to_all.51 = f32[8,128,512]{2,0,1:T(8,128)S(1)} all-to-all(f32[8,128,512]{2,0,1:T(8,128)S(1)} %copy.65), channel_id=1, replica_groups=mesh['lev'=16,'lat'=16] {'lev'}, dimensions={1} | all-to-all | bytes 4194304 | tf_op jit(solution)/shard_map/all_to_all | solution.py:118
  271.8 1.2 copy.67
  273.0 2.3 reshape.192
  (32 shorter events, 0.1 us)
Async XLA Ops:
  0.0 236.1 %copy-start = (f32[4,8,16,16]{3,2,1,0:T(8,128)S(1)}, f32[4,8,16,16]{3,2,1,0:T(8,128)}, u32[]{:S(2)}) copy-start(f32[4,8,16,16]{3,2,1,0:T(8,128)} %param.14) | copy-start | bytes 98308
  1.0 24.1 %collective-permute-start = (f32[8,1,2048]{2,1,0:T(1,128)S(1)}, f32[8,1,2048]{2,1,0:T(1,128)S(1)}, u32[]{:S(2)}, u32[]{:S(2)}) collective-permute-start(f32[8,1,2048]{2,1,0:T(1,128)S(1)} %slice.87), channel_id=1, source_target_pairs={{1,0},{2,1},{3,2},{4,3},{5,4},{6,5},{7,6},{8,7},{9,8},{10,9},{11,1... | collective-permute-start | bytes 196616 | tf_op jit(solution)/shard_map/ppermute | solution.py:12
  5.1 8.3 %copy-start.10 = (s32[1,1,16]{2,1,0:T(1,128)S(1)}, s32[1,1,16]{2,1,0:T(1,128)}, u32[]{:S(2)}) copy-start(s32[1,1,16]{2,1,0:T(1,128)} %param.17) | copy-start | bytes 196
  6.2 20.2 %collective-permute-start.1 = (f32[8,8,1,2048]{3,1,2,0:T(8,128)}, f32[8,8,1,2048]{3,1,2,0:T(8,128)}, u32[]{:S(2)}, u32[]{:S(2)}) collective-permute-start(f32[8,8,1,2048]{3,1,2,0:T(8,128)} %get-tuple-element.21), channel_id=1, source_target_pairs={{1,0},{2,1},{3,2},{4,3},{5,4},{6,5},{7,6},{8,7},{9,8},{10,9},{11,1... | collective-permute-start | bytes 1572872 | tf_op jit(solution)/shard_map/ppermute | solution.py:25
  7.5 27.4 %collective-permute-start.2 = (f32[8,8,1,2048]{3,1,2,0:T(8,128)}, f32[8,8,1,2048]{3,1,2,0:T(8,128)}, u32[]{:S(2)}, u32[]{:S(2)}) collective-permute-start(f32[8,8,1,2048]{3,1,2,0:T(8,128)} %get-tuple-element.22), channel_id=1, source_target_pairs={{0,1},{1,2},{2,3},{3,4},{4,5},{5,6},{6,7},{7,8},{8,9},{9,10},{10,1... | collective-permute-start | bytes 1572872 | tf_op jit(solution)/shard_map/ppermute | solution.py:23
  14.2 32.4 %all-to-all-start.2 = ((s32[1,1,16]{1,0,2:T(1,128)}), s32[1,1,16]{1,0,2:T(1,128)S(1)}, u32[]{:S(2)}, u32[]{:S(2)}) async-start(s32[1,1,16]{1,0,2:T(1,128)} %copy.62), calls=%async_computation.2 | async-start | bytes 16384 | tf_op jit(solution)/shard_map/all_to_all | solution.py:79
  24.0 1.0 copy-start.4
  24.0 1.2 slice-start
  24.0 1.2 copy-start.7
  26.4 11.3 %copy-start.3 = (f32[8,4,2048]{2,0,1:T(8,128)}, f32[8,4,2048]{2,0,1:T(8,128)S(1)}, u32[]{:S(2)}) copy-start(f32[8,4,2048]{2,0,1:T(8,128)S(1)} %copy.54) | copy-start | bytes 786436
  37.7 6.2 %copy-start.1 = (f32[8,8,4,2048]{3,1,2,0:T(8,128)}, f32[8,8,4,2048]{3,1,2,0:T(8,128)S(1)}, u32[]{:S(2)}) copy-start(f32[8,8,4,2048]{3,1,2,0:T(8,128)S(1)} %fusion.5) | copy-start | bytes 6291460
  37.8 38.5 %collective-permute-start.3 = (f32[8,8,1,2048]{3,1,2,0:T(8,128)S(1)}, f32[8,8,1,2048]{3,1,2,0:T(8,128)S(1)}, u32[]{:S(2)}, u32[]{:S(2)}) collective-permute-start(f32[8,8,1,2048]{3,1,2,0:T(8,128)S(1)} %get-tuple-element.15), channel_id=1, source_target_pairs={{1,0},{2,1},{3,2},{4,3},{5,4},{6,5},{7,6},{8,7},{9,8},{10,9},{11,1... | collective-permute-start | bytes 1572872 | tf_op jit(solution)/shard_map/ppermute | solution.py:25
  39.1 37.2 %collective-permute-start.4 = (f32[8,8,1,2048]{3,1,2,0:T(8,128)S(1)}, f32[8,8,1,2048]{3,1,2,0:T(8,128)S(1)}, u32[]{:S(2)}, u32[]{:S(2)}) collective-permute-start(f32[8,8,1,2048]{3,1,2,0:T(8,128)S(1)} %get-tuple-element.16), channel_id=1, source_target_pairs={{0,1},{1,2},{2,3},{3,4},{4,5},{5,6},{6,7},{7,8},{8,9},{9,10},{10,1... | collective-permute-start | bytes 1572872 | tf_op jit(solution)/shard_map/ppermute | solution.py:23
  46.6 19.2 %all-to-all-start.1 = ((s32[1,1,16,16]{3,1,0,2:T(1,128)}), s32[1,1,16,16]{3,1,0,2:T(1,128)S(1)}, u32[]{:S(2)}, u32[]{:S(2)}) async-start(s32[1,1,16,16]{3,1,0,2:T(1,128)} %bitcast.14), calls=%async_computation.1 | async-start | bytes 16384 | tf_op jit(solution)/shard_map/all_to_all | solution.py:78
  65.8 57.2 %all-to-all-start.3 = ((f32[1,1,16,16,128]{4,3,1,0,2:T(8,128)}), f32[1,1,16,16,128]{4,3,1,0,2:T(8,128)}, u32[]{:S(2)}, u32[]{:S(2)}) async-start(f32[1,1,16,16,128]{4,3,1,0,2:T(8,128)} %bitcast.53), calls=%async_computation.3 | async-start | bytes 262144 | tf_op jit(solution)/shard_map/all_to_all | solution.py:77
  76.3 0.8 copy-start.5
  76.3 1.0 copy-start.6
  123.0 8.0 %copy-start.8 = (s32[2,4,2048]{2,1,0:T(4,128)S(1)}, s32[2,4,2048]{2,1,0:T(4,128)}, u32[]{:S(2)}) copy-start(s32[2,4,2048]{2,1,0:T(4,128)} %param.13) | copy-start | bytes 196612
  123.0 8.0 %copy-start.9 = (f32[4,2048]{1,0:T(4,128)S(1)}, f32[4,2048]{1,0:T(4,128)}, u32[]{:S(2)}) copy-start(f32[4,2048]{1,0:T(4,128)} %param.12) | copy-start | bytes 98308
  123.0 36.3 %all-to-all-start = ((f32[16,1,32768]{2,1,0:T(1,128)}), f32[16,1,32768]{2,1,0:T(1,128)S(1)}, u32[]{:S(2)}, u32[]{:S(2)}) async-start(f32[16,1,32768]{2,1,0:T(1,128)} %reshape.209), calls=%async_computation | async-start | bytes 4194304 | tf_op jit(solution)/shard_map/all_to_all | solution.py:111
  159.3 1.3 copy-start.2
where the time goes:
time: 277 us; the launch traced here: 275 us
  local copies, waits for them, and re-layouts  127 us (46%)
  starting transfers between devices  53.4 us (19%)
  waiting for transfers between devices  39.5 us (14%)
  blocking collectives  31.9 us (12%)
  other arithmetic  20 us (7%)
  matrix products  3.51 us (1%)
    unnamed x28, local copies, waits for them, and re-layouts  60 us
    all_to_all x3, local copies, waits for them, and re-layouts, body(): lax.all_to_all(flattened, 'lev', split_axis=2, concat_axis=1, tiled=True)  36.1 us
    all_to_all x1, blocking collectives, body(): lax.all_to_all(diffused, 'lev', split_axis=1, concat_axis=2, tiled=True)  31.9 us
    all_to_all x1, waiting for transfers between devices, body(): lax.all_to_all(flattened, 'lev', split_axis=2, concat_axis=1, tiled=True)  24 us
    reshape x1, local copies, waits for them, and re-layouts, body(): flattened = state.reshape(tracer_count, level_count, row_count * lon_count)  15.9 us
    ppermute x2, starting transfers between devices, padded_2(): lax.ppermute(tail, axis, [(i, (i + 1) % count) for i in range(ends)])  10.8 us
    all_to_all x1, starting transfers between devices, body(): lax.all_to_all(obs_column, 'lat', split_axis=2, concat_axis=2, tiled=True)  10.6 us
    all_to_all x1, starting transfers between devices, body(): lax.all_to_all(obs_values, 'lat', split_axis=2, concat_axis=2, tiled=True)  10.5 us
  transfers between devices with their start and end apart: 9, of which 3 were waited for; matrix products, arithmetic and copies ran while one was open for 23% of the time, Pallas kernels for 0%

commit v1 on v0

v1 whole, which is shorter than its diff:
```python
import jax
import jax.numpy as jnp
from jax import lax
from jax.experimental import pallas as pl
from jax.experimental.pallas import tpu as pltpu
from jax.sharding import PartitionSpec as P


F32 = jnp.float32
LANES = 128


def split_rows(x):
    lead = x.shape[:-2]
    rows, lons = x.shape[-2:]
    x = x.reshape(*lead, rows, lons // LANES, LANES).swapaxes(-3, -2)
    return x.reshape(*lead, rows * lons // LANES, LANES)


def join_rows(x, rows, lons):
    lead = x.shape[:-2]
    x = x.reshape(*lead, lons // LANES, rows, LANES).swapaxes(-3, -2)
    return x.reshape(*lead, rows, lons)


def lane_slice(j):
    return pl.ds(j * LANES, LANES)


def swap_axes8(tiles):
    row = lax.broadcasted_iota(jnp.int32, (8, LANES), 0)
    tiles = list(tiles)
    for step in (4, 2, 1):
        low_half = (row & step) == 0
        for i in range(8):
            if i & step == 0:
                low, high = tiles[i], tiles[i + step]
                tiles[i] = jnp.where(low_half, low, pltpu.roll(high, step, 0))
                tiles[i + step] = jnp.where(low_half, pltpu.roll(low, 8 - step, 0), high)
    return tiles


def unpack_rows(source, target):
    for k in range(8):
        tiles = swap_axes8([source(level * 64 + k * 8) for level in range(8)])
        for half in range(2):
            for r in range(4):
                target[r, :, lane_slice(2 * k + half)] = tiles[4 * half + r]


def east_tiles(tiles):
    lane = lax.broadcasted_iota(jnp.int32, tiles[0].shape, 1)
    turned = [pltpu.roll(x, LANES - 1, 1) for x in tiles]
    count = len(tiles)
    return [jnp.where(lane == LANES - 1, turned[(j + 1) % count], turned[j]) for j in range(count)]


def west_tiles(tiles):
    lane = lax.broadcasted_iota(jnp.int32, tiles[0].shape, 1)
    turned = [pltpu.roll(x, 1, 1) for x in tiles]
    return [jnp.where(lane == 0, turned[j - 1], turned[j]) for j in range(len(tiles))]


def flow_coefficients(u_ref, v_ref, u_rows, v_rows, coef_ref):
    unpack_rows(lambda start: u_ref[pl.ds(start, 8), :], u_rows)
    unpack_rows(lambda start: v_ref[pl.ds(start, 8), :], v_rows)
    for r in range(4):
        u = [u_rows[r, :, lane_slice(j)] for j in range(16)]
        ue = east_tiles(u)
        for j in range(16):
            s = lane_slice(j)
            east = jnp.maximum(ue[j], 0.0)
            west = jnp.minimum(u[j], 0.0)
            south = jnp.minimum(v_rows[r, :, s], 0.0)
            center = 1.0 - east + west + south
            if r < 3:
                north = jnp.maximum(v_rows[r + 1, :, s], 0.0)
                center = center - north
                coef_ref[2, r, :, s] = north
            coef_ref[0, r, :, s] = east
            coef_ref[1, r, :, s] = west
            coef_ref[3, r, :, s] = south
            coef_ref[4, r, :, s] = center


def prep_kernel(
    a_hbm, u_hbm, v_hbm, part_hbm, north_hbm, south_hbm, coef_hbm,
    a_ref, u_ref, v_ref, rows_ref, v_rows, part_ref, north_ref, south_ref, coef_ref, sems,
):
    faces = [
        pltpu.make_async_copy(u_hbm, u_ref, sems.at[8, 2]),
        pltpu.make_async_copy(v_hbm, v_ref, sems.at[8, 3]),
    ]
    for copy in faces:
        copy.start()

    def incoming(t):
        return pltpu.make_async_copy(a_hbm.at[t], a_ref.at[t], sems.at[t, 3])

    @pl.loop(0, 8)
    def _(t):
        incoming(t).start()

    def copies(t):
        pair = pl.ds(2 * t, 2)
        return [
            pltpu.make_async_copy(part_ref.at[t], part_hbm.at[t], sems.at[t, 0]),
            pltpu.make_async_copy(north_ref.at[pair], north_hbm.at[pair], sems.at[t, 1]),
            pltpu.make_async_copy(south_ref.at[pair], south_hbm.at[pair], sems.at[t, 2]),
        ]

    for copy in faces:
        copy.wait()
    flow_coefficients(u_ref, v_ref, rows_ref, v_rows, coef_ref)
    south_ref[16] = v_rows[0]
    coef_copy = pltpu.make_async_copy(coef_ref, coef_hbm, sems.at[8, 0])
    face_copy = pltpu.make_async_copy(south_ref.at[pl.ds(16, 1)], south_hbm.at[pl.ds(16, 1)], sems.at[8, 1])
    coef_copy.start()
    face_copy.start()

    @pl.loop(0, 8)
    def _(t):
        incoming(t).wait()
        unpack_rows(lambda start: a_ref[t, pl.ds(start, 8), :], rows_ref)
        for r in range(4):
            row = [rows_ref[r, :, lane_slice(j)] for j in range(16)]
            e = east_tiles(row)
            w = west_tiles(row)
            for j in range(16):
                s = lane_slice(j)
                out = row[j] * coef_ref[4, r, :, s] + e[j] * coef_ref[0, r, :, s] - w[j] * coef_ref[1, r, :, s]
                if r < 3:
                    out = out + rows_ref[r + 1, :, s] * coef_ref[2, r, :, s]
                if r > 0:
                    out = out - rows_ref[r - 1, :, s] * coef_ref[3, r, :, s]
                part_ref[t, r, :, s] = out
                if r == 3:
                    north_ref[2 * t, :, s] = row[j]
                    north_ref[2 * t + 1, :, s] = out
                if r == 0:
                    south_ref[2 * t, :, s] = row[j]
                    south_ref[2 * t + 1, :, s] = out
        for copy in copies(t):
            copy.start()

    @pl.loop(0, 8)
    def _(t):
        for copy in copies(t):
            copy.wait()

    coef_copy.wait()
    face_copy.wait()


def advect_kernel(
    lev_ref, part_hbm, own_north_hbm, own_south_hbm, from_south_hbm, from_north_hbm, coef_hbm, band_ref,
    adv_hbm, keep_ref, send_ref,
    adv_ref, edge_ref, sum_ref, inside_ref, part_ref, own_north_ref, own_south_ref, from_south_ref, from_north_ref, coef_ref, sems,
):
    tiles = range(16)

    def copies(t):
        pair = pl.ds(2 * t, 2)
        first = pl.ds(2 * t, 1)
        return [
            pltpu.make_async_copy(part_hbm.at[t], part_ref.at[t], sems.at[t, 0]),
            pltpu.make_async_copy(own_north_hbm.at[first], own_north_ref.at[pl.ds(t, 1)], sems.at[t, 1]),
            pltpu.make_async_copy(own_south_hbm.at[first], own_south_ref.at[pl.ds(t, 1)], sems.at[t, 2]),
            pltpu.make_async_copy(from_south_hbm.at[pair], from_south_ref.at[pair], sems.at[t, 3]),
            pltpu.make_async_copy(from_north_hbm.at[pair], from_north_ref.at[pair], sems.at[t, 4]),
        ]

    fixed = [
        pltpu.make_async_copy(coef_hbm, coef_ref, sems.at[8, 0]),
        pltpu.make_async_copy(own_south_hbm.at[pl.ds(16, 1)], own_south_ref.at[pl.ds(8, 1)], sems.at[8, 1]),
        pltpu.make_async_copy(from_north_hbm.at[pl.ds(16, 1)], from_north_ref.at[pl.ds(16, 1)], sems.at[8, 2]),
    ]
    for copy in fixed:
        copy.start()

    @pl.loop(0, 8)
    def _(t):
        for copy in copies(t):
            copy.start()

    def outgoing(t):
        return pltpu.make_async_copy(adv_ref.at[:, t], adv_hbm.at[:, t], sems.at[t, 5])

    level = lax.broadcasted_iota(jnp.int32, (8, 2048), 0) + lev_ref[0] * 8
    for r in range(4):
        first = band_ref[0, r : r + 1, :]
        last = band_ref[1, r : r + 1, :]
        inside_ref[r] = jnp.where((level >= first) & (level < last), 1.0, 0.0).astype(F32)

    for copy in fixed:
        copy.wait()
    north_face = jnp.maximum(from_north_ref[16], 0.0)
    edge_ref[0] = jnp.maximum(own_south_ref[8], 0.0)
    edge_ref[1] = jnp.minimum(from_north_ref[16], 0.0)
    edge_ref[2] = north_face
    edge_ref[3] = coef_ref[4, 3] - north_face

    @pl.loop(0, 8)
    def _(t):
        for copy in copies(t):
            copy.wait()
        this_tracer = lax.broadcasted_iota(jnp.int32, (8, LANES), 0) == t
        rows = [[] for _ in range(6)]
        for j in tiles:
            s = lane_slice(j)
            a_south = from_south_ref[2 * t, :, s]
            a_last = own_north_ref[t, :, s]
            a_first = own_south_ref[t, :, s]
            rows[0].append(from_south_ref[2 * t + 1, :, s] + edge_ref[0, :, s] * (a_first - a_south))
            rows[1].append(part_ref[t, 0, :, s] - coef_ref[3, 0, :, s] * a_south)
            rows[2].append(part_ref[t, 1, :, s])
            rows[3].append(part_ref[t, 2, :, s])
            rows[4].append(part_ref[t, 3, :, s] + edge_ref[2, :, s] * (from_north_ref[2 * t, :, s] - a_last))
            rows[5].append(from_north_ref[2 * t + 1, :, s] - edge_ref[1, :, s] * a_last)
        for r in range(4):
            x = rows[r + 1]
            e = east_tiles(x)
            w = west_tiles(x)
            for j in tiles:
                s = lane_slice(j)
                center = coef_ref[4, r, :, s] if r < 3 else edge_ref[3, :, s]
                north = coef_ref[2, r, :, s] if r < 3 else edge_ref[2, :, s]
                out = (
                    x[j] * center
                    + e[j] * coef_ref[0, r, :, s]
                    - w[j] * coef_ref[1, r, :, s]
                    + rows[r + 2][j] * north
                    - rows[r][j] * coef_ref[3, r, :, s]
                )
                adv_ref[r, t, :, s] = out
                band = jnp.sum(out * inside_ref[r, :, s], axis=0, keepdims=True)
                sum_ref[r, :, s] = jnp.where(this_tracer, band, sum_ref[r, :, s])
        outgoing(t).start()

    @pl.loop(0, 8)
    def _(t):
        outgoing(t).wait()

    core = lax.rem(lev_ref[0], 2)
    keep_ref[...] = sum_ref[pl.ds(2 * core, 2)]
    send_ref[...] = sum_ref[pl.ds(2 - 2 * core, 2)]


def halves_of(x):
    high = x.astype(jnp.bfloat16)
    return high, (x - high.astype(F32)).astype(jnp.bfloat16)


def column_kernel(lev_ref, band_ref, flux_ref, inv_ref, gain_ref, matrix_ref):
    lev = lev_ref[0]
    core = lax.rem(lev, 2)
    block = lax.div(lev, 2)
    wide = (64, 128)
    row_pick = (lax.broadcasted_iota(jnp.int32, (64, 8), 0) & 7) == lax.broadcasted_iota(jnp.int32, (64, 8), 1)
    lane = lax.broadcasted_iota(jnp.int32, (16, 128), 1)
    half = jnp.where(lane < 64, core, 1 - core)
    lane_pick = half * 8 + (lane & 7) == lax.broadcasted_iota(jnp.int32, (16, 128), 0)
    same_tracer = (lax.broadcasted_iota(jnp.int32, wide, 0) >> 3) == ((lax.broadcasted_iota(jnp.int32, wide, 1) & 63) >> 3)
    row_pick = jnp.where(row_pick, 1.0, 0.0).astype(F32)
    lane_pick = jnp.where(lane_pick, 1.0, 0.0).astype(F32)
    exact = dict(precision=lax.Precision.HIGHEST, preferred_element_type=F32)
    for r in range(4):
        first = band_ref[0, r : r + 1, :]
        last = band_ref[1, r : r + 1, :]
        scaled = flux_ref[r : r + 1, :] / (last - first).astype(F32)
        inv = inv_ref[r, block, pl.ds(pl.multiple_of(core * 8, 8), 8), :]
        gain = jnp.zeros((8, 2048), F32)
        for k in range(16):
            level_k = block * 16 + k
            weight = jnp.where((first <= level_k) & (level_k < last), scaled, 0.0)
            gain = gain + inv[:, k : k + 1] * weight
        gain_ref[r] = gain
        spread = lax.dot(lax.dot(row_pick, inv, **exact), lane_pick, **exact)
        high, low = halves_of(jnp.where(same_tracer, spread, 0.0))
        matrix_ref[r, 0:64, 0:128] = high
        matrix_ref[r, 0:64, 128:256] = high
        matrix_ref[r, 64:128, 0:128] = low
        matrix_ref[r, 64:128, 128:256] = jnp.zeros_like(low)


def diffuse_kernel(lev_ref, adv_hbm, other_hbm, band_ref, flux_ref, matrix_ref, out_ref, adv_ref, other_ref, sems):
    def copies(r):
        return [
            pltpu.make_async_copy(adv_hbm.at[r], adv_ref.at[r], sems.at[r, 0]),
            pltpu.make_async_copy(other_hbm.at[r], other_ref.at[r], sems.at[r, 1]),
        ]

    for r in range(4):
        for copy in copies(r):
            copy.start()
    lev = lev_ref[0]
    level = lax.broadcasted_iota(jnp.int32, (8, 2048), 0)
    own_level = level + lev * 8
    other_level = level + (lev + 1 - 2 * lax.rem(lev, 2)) * 8
    for r in range(4):
        first = band_ref[0, r : r + 1, :]
        last = band_ref[1, r : r + 1, :]
        flux = flux_ref[r : r + 1, :]

        def rest(values, levels):
            kept = 1.0 - jnp.where((levels >= first) & (levels < last), flux, 0.0)
            return halves_of((values * kept[None]).reshape(64, 2048))

        for copy in copies(r):
            copy.wait()
        own_high, own_low = rest(adv_ref[r], own_level)
        other_high, other_low = rest(other_ref[r], other_level)
        stacked = jnp.concatenate([own_high, other_high, own_low, other_low], axis=0)
        both = lax.dot(matrix_ref[r], stacked, preferred_element_type=F32)
        out_ref[r] = both[:64] + both[64:]


def finish_kernel(lev_ref, base_ref, gain_ref, own_ref, other_ref, forcing_ref, out_ref, sum_ref, done_ref, sems):
    core = lax.rem(lev_ref[0], 2)
    for q in range(2):
        for j in range(16):
            sum_ref[2 * core + q, j] = own_ref[q, :, lane_slice(j)]
            sum_ref[2 - 2 * core + q, j] = other_ref[q, :, lane_slice(j)]

    @pl.loop(0, 8)
    def _(t):
        for k in range(8):
            tiles = []
            for j in (2 * k, 2 * k + 1):
                s = lane_slice(j)
                for r in range(4):
                    total = sum_ref[r, j, pl.ds(t, 8, stride=0), :]
                    forcing = forcing_ref[4 * r + j // 4, :, lane_slice(j % 4)]
                    tiles.append(base_ref[r, t, :, s] + gain_ref[r, :, s] * total + forcing)
            tiles = swap_axes8(tiles)
            for level in range(8):
                done_ref[t, pl.ds(level * 64 + k * 8, 8), :] = tiles[level]
        pltpu.make_async_copy(done_ref.at[t], out_ref.at[t], sems.at[t]).start()

    @pl.loop(0, 8)
    def _(t):
        pltpu.make_async_copy(done_ref.at[t], out_ref.at[t], sems.at[t]).wait()


def pack_kernel(lat_ref, count_ref, values_ref, column_ref, out_ref, line_ref):
    lat = lat_ref[0]
    slot = lax.broadcasted_iota(jnp.int32, (16, LANES), 0)
    line_ref[...] = jnp.zeros((16, LANES), F32)
    line_ref[:, 0:16] = column_ref[...].astype(F32)
    placed = pltpu.roll(line_ref[...], lax.rem(lat, 8) * 16, 1)
    low = jnp.where(lat < 8, placed, 0.0)
    high = jnp.where(lat < 8, 0.0, placed)
    for d in range(16):
        out_ref[d, 0:16, :] = jnp.where(slot < count_ref[d], values_ref[d], 0.0)
        out_ref[d, 16:24, :] = jnp.zeros((8, LANES), F32)
        out_ref[d, 16:17, :] = low[d : d + 1]
        out_ref[d, 17:18, :] = high[d : d + 1]


def forcing_kernel(packed_ref, out_ref):
    lines = packed_ref[0, 16:18, :]
    for source in range(1, 16):
        lines = lines + packed_ref[source, 16:18, :]
    total = jnp.zeros((512, LANES), F32)
    column = lax.broadcasted_iota(jnp.int32, (512, LANES), 0).astype(F32)
    for part in range(2):
        hit = jnp.where(column == lines[part : part + 1], 1.0, 0.0).astype(F32)
        values = jnp.concatenate([packed_ref[8 * part + n, 0:16, :] for n in range(8)], axis=0)
        total = total + lax.dot(hit, values, precision=lax.Precision.HIGHEST, preferred_element_type=F32)
    out_ref[...] = total.T.reshape(16, 8, 512)


def body(adjoint_in, courant_lon, courant_lat, mass_flux, conv_band, diff_inverse, obs_values, obs_column, obs_count):
    tracers, levels, rows, lons = adjoint_in.shape
    lev = lax.axis_index("lev").astype(jnp.int32).reshape(1)
    lat = lax.axis_index("lat").astype(jnp.int32).reshape(1)
    lev_count = lax.axis_size("lev")
    lat_count = lax.axis_size("lat")
    smem = pl.BlockSpec(memory_space=pltpu.SMEM)
    shape = lambda *dims: jax.ShapeDtypeStruct(dims, F32)

    a_view = split_rows(adjoint_in).reshape(tracers, 512, LANES)
    u_view = split_rows(courant_lon).reshape(512, LANES)
    v_view = split_rows(courant_lat).reshape(512, LANES)

    vmem = pl.BlockSpec(memory_space=pltpu.VMEM)
    hbm = pl.BlockSpec(memory_space=pltpu.HBM)
    small = pltpu.CompilerParams(vmem_limit_bytes=16 << 20)
    row_scratch = pltpu.VMEM((4, 8, lons), F32)

    def far(*dims):
        return pltpu.HBM(dims, F32)

    def keep_far(x):
        return pltpu.with_memory_space_constraint(x, pltpu.HBM)

    part, to_north, to_south, coef = pl.pallas_call(
        prep_kernel,
        in_specs=[hbm] * 3,
        out_specs=[hbm] * 4,
        out_shape=[far(8, 4, 8, lons), far(16, 8, lons), far(17, 8, lons), far(5, 4, 8, lons)],
        scratch_shapes=[
            pltpu.VMEM((8, 512, LANES), F32), pltpu.VMEM((512, LANES), F32), pltpu.VMEM((512, LANES), F32),
            row_scratch, row_scratch, pltpu.VMEM((8, 4, 8, lons), F32), pltpu.VMEM((16, 8, lons), F32),
            pltpu.VMEM((17, 8, lons), F32), pltpu.VMEM((5, 4, 8, lons), F32), pltpu.SemaphoreType.DMA((9, 4)),
        ],
        compiler_params=small,
    )(keep_far(a_view), keep_far(u_view), keep_far(v_view))
    from_south = lax.ppermute(to_north, "lat", [(i, i + 1) for i in range(lat_count - 1)])
    from_north = lax.ppermute(to_south, "lat", [(i + 1, i) for i in range(lat_count - 1)])

    packed = pl.pallas_call(
        pack_kernel,
        in_specs=[smem, smem, vmem, vmem],
        out_specs=vmem,
        out_shape=shape(16, 24, LANES),
        scratch_shapes=[pltpu.VMEM((16, LANES), F32)],
        compiler_params=small,
    )(lat, obs_count.reshape(16), obs_values.reshape(16, 16, LANES), obs_column.reshape(16, 16))
    packed = lax.all_to_all(packed, "lat", split_axis=0, concat_axis=0, tiled=True)

    forcing = pl.pallas_call(
        forcing_kernel, in_specs=[vmem], out_specs=vmem, out_shape=shape(16, 8, 512), compiler_params=small
    )(packed)
    forcing = lax.all_to_all(forcing, "lev", split_axis=0, concat_axis=0, tiled=True)

    gain, matrix = pl.pallas_call(
        column_kernel,
        in_specs=[smem] + [vmem] * 3,
        out_specs=[vmem] * 2,
        out_shape=[shape(4, 8, lons), jax.ShapeDtypeStruct((4, 128, 256), jnp.bfloat16)],
        compiler_params=small,
    )(lev, conv_band, mass_flux, diff_inverse)

    adv, keep, send = pl.pallas_call(
        advect_kernel,
        in_specs=[smem] + [hbm] * 6 + [vmem],
        out_specs=[hbm, vmem, vmem],
        out_shape=[far(4, 8, 8, lons), shape(2, 8, lons), shape(2, 8, lons)],
        scratch_shapes=[
            pltpu.VMEM((4, 8, 8, lons), F32), row_scratch, row_scratch, row_scratch, pltpu.VMEM((8, 4, 8, lons), F32), pltpu.VMEM((8, 8, lons), F32),
            pltpu.VMEM((9, 8, lons), F32), pltpu.VMEM((16, 8, lons), F32), pltpu.VMEM((17, 8, lons), F32),
            pltpu.VMEM((5, 4, 8, lons), F32), pltpu.SemaphoreType.DMA((9, 6)),
        ],
        compiler_params=small,
    )(lev, keep_far(part), keep_far(to_north), keep_far(to_south), from_south, from_north, keep_far(coef), conv_band)

    swap = [(i, i ^ 1) for i in range(lev_count)]
    swapped = lax.ppermute(send, "lev", swap)
    chip_sum = keep + swapped
    blocks = lev_count // 2
    pairs = [(2 * n + c, 2 * (n ^ 1) + c) for n in range(2, blocks) for c in range(2)]
    total = chip_sum + lax.ppermute(chip_sum, "lev", pairs)
    adv_out, _ = lax.optimization_barrier((adv, swapped))
    adv_other = lax.ppermute(adv_out, "lev", swap)
    lines = blocks // 2 - 1
    moved = []
    for shift in range(1, lines):
        pairs = []
        for y in range(lines):
            for n in range(4):
                pairs.append((4 * (y + 1) + n, 4 * ((y + shift) % lines + 1) + n))
        moved.append(lax.ppermute(total, "lev", pairs))
    total = sum(moved, total)
    total_other = lax.ppermute(total, "lev", swap)

    base = pl.pallas_call(
        diffuse_kernel,
        in_specs=[smem, hbm, hbm] + [vmem] * 3,
        out_specs=vmem,
        out_shape=shape(4, 64, lons),
        scratch_shapes=[pltpu.VMEM((4, 8, 8, lons), F32), pltpu.VMEM((4, 8, 8, lons), F32), pltpu.SemaphoreType.DMA((4, 2))],
        compiler_params=small,
    )(lev, keep_far(adv), keep_far(adv_other), conv_band, mass_flux, matrix)

    out = pl.pallas_call(
        finish_kernel,
        in_specs=[smem] + [vmem] * 5,
        out_specs=hbm,
        out_shape=shape(tracers, 512, LANES),
        scratch_shapes=[
            pltpu.VMEM((4, 16, 8, LANES), F32), pltpu.VMEM((8, 512, LANES), F32), pltpu.SemaphoreType.DMA((8,))
        ],
        compiler_params=small,
    )(lev, base.reshape(4, 8, 8, lons), gain, total, total_other, forcing)
    return join_rows(out.reshape(tracers, levels, 64, LANES), rows, lons)


def solution(mesh):
    placed = (
        P(None, "lev", "lat", None),
        P("lev", "lat", None),
        P("lev", "lat", None),
        P("lat", None),
        P(None, "lat", None),
        P("lat", None, None, None),
        P("lev", "lat", None, None, None),
        P("lev", "lat", None, None),
        P("lev", "lat", None),
    )

    def step(*args):
        return body(*args)

    step = jax.shard_map(
        step, mesh=mesh, in_specs=placed, out_specs=P(None, "lev", "lat", None), check_vma=False
    )
    return step
```

time: 277 us -> 111 us (0.40)
  local copies, waits for them, and re-layouts: 127 us -> 0.03 us
  blocking collectives: 31.9 us -> 0 us
  starting transfers between devices: 53.4 us -> 32.2 us
  waiting for transfers between devices: 39.5 us -> 59.6 us
  other arithmetic: 20 us -> 0.06 us
  Pallas kernels: 0 us -> 18.5 us
  matrix products: 3.51 us -> 0 us
    unnamed x28 -> x12, local copies, waits for them, and re-layouts: 60 us -> 0.03 us
    ppermute x5 -> x8, waiting for transfers between devices: 8.5 us -> 47 us  [the longest x1 46 us: body(): lax.ppermute(to_north, 'lat', [(i, i + 1) for i in range(lat_count - 1)])]
    all_to_all x5 -> x0, local copies, waits for them, and re-layouts: 37.9 us -> none  [the longest x3 36.1 us: body(): lax.all_to_all(flattened, 'lev', split_axis=2, concat_axis=1, tiled=True)]
    all_to_all x1 -> x0, blocking collectives: 31.9 us -> none  [body(): lax.all_to_all(diffused, 'lev', split_axis=1, concat_axis=2, tiled=True)]
    pallas_call x0 -> x7, Pallas kernels: none -> 18.5 us  [the longest x1 6.48 us: body(): pl.pallas_call(advect_kernel, in_specs=[smem] + [hbm] * 6 + [vmem], out_s...]
    all_to_all x4 -> x2, waiting for transfers between devices: 31 us -> 12.7 us  [the longest x1 7.83 us: body(): lax.all_to_all(packed, 'lat', split_axis=0, concat_axis=0, tiled=True)]
    reshape x2 -> x0, local copies, waits for them, and re-layouts: 18.2 us -> none  [the longest x1 15.9 us: body(): flattened = state.reshape(tracer_count, level_count, row_count * lon_count)]
    all_to_all x4 -> x2, starting transfers between devices: 38.8 us -> 23.1 us  [the longest x1 13 us: body(): lax.all_to_all(forcing, 'lev', split_axis=0, concat_axis=0, tiled=True)]
  transfers between devices with their start and end apart: 9 -> 10, of which waited for: 3 -> 4; matrix products, arithmetic and copies ran while one was open for 23% -> 0% of each run, Pallas kernels for 0% -> 6%
where the time goes in v1:
time: 111 us
  waiting for transfers between devices  59.6 us (54%)
  starting transfers between devices  32.2 us (29%)
  Pallas kernels  18.5 us (17%)
    ppermute x1, waiting for transfers between devices, body(): lax.ppermute(to_north, 'lat', [(i, i + 1) for i in range(lat_count - 1)])  46 us
    all_to_all x1, starting transfers between devices, body(): lax.all_to_all(forcing, 'lev', split_axis=0, concat_axis=0, tiled=True)  13 us
    all_to_all x1, starting transfers between devices, body(): lax.all_to_all(packed, 'lat', split_axis=0, concat_axis=0, tiled=True)  10.1 us
    all_to_all x1, waiting for transfers between devices, body(): lax.all_to_all(packed, 'lat', split_axis=0, concat_axis=0, tiled=True)  7.83 us
    pallas_call x1, Pallas kernels, body(): pl.pallas_call(advect_kernel, in_specs=[smem] + [hbm] * 6 + [vmem], out_s...  6.48 us
    all_to_all x1, waiting for transfers between devices, body(): lax.all_to_all(forcing, 'lev', split_axis=0, concat_axis=0, tiled=True)  4.83 us
    ppermute x1, starting transfers between devices, body(): lax.ppermute(to_north, 'lat', [(i, i + 1) for i in range(lat_count - 1)])  4.63 us
    pallas_call x1, Pallas kernels, body(): pl.pallas_call(prep_kernel, in_specs=[hbm] * 3, out_specs=[hbm] * 4, out_...  4.2 us
  transfers between devices with their start and end apart: 10, of which 4 were waited for; matrix products, arithmetic and copies ran while one was open for 0% of the time, Pallas kernels for 6%

profile of v1, /device:TPU:1, one launch (start us, length us, event | category | flops | bytes accessed | tf_op | source)
XLA Modules:
  0.0 110.5 jit_solution(16273325713045049983)
XLA Ops:
  0.0 0.0 copy-start
  0.0 4.2 %shard_map.91 = (f32[8,4,8,2048]{3,2,1,0:T(8,128)}, f32[16,8,2048]{2,1,0:T(8,128)}, f32[17,8,2048]{2,1,0:T(8,128)}, f32[5,4,8,2048]{3,2,1,0:T(8,128)}) custom-call(f32[8,512,128]{2,1,0:T(8,128)} %bitcast.30, f32[512,128]{1,0:T(8,128)} %bitcast.31, f32[512,128]{1,0:T(8,128)} %bitcast.32), custom_call_target="tpu_custom_call" | custom-call | tf_op jit(solution)/shard_map/pallas_call | solution.py:397
  4.2 1.3 %collective-permute-start.1 = (f32[17,8,2048]{2,1,0:T(8,128)}, f32[17,8,2048]{2,1,0:T(8,128)S(1)}, u32[]{:S(2)}, u32[]{:S(2)}) collective-permute-start(f32[17,8,2048]{2,1,0:T(8,128)} %get-tuple-element.17.own_south_hbm), channel_id=1, source_target_pairs={{1,0},{2,1},{3,2},{4,3},{5,4},{6,5},{7,6},{8,7},{9,8},{10,9},{11,1... | collective-permute-start | bytes 3342344 | tf_op jit(solution)/shard_map/ppermute | solution.py:410
  5.5 4.6 %collective-permute-start = (f32[16,8,2048]{2,1,0:T(8,128)}, f32[16,8,2048]{2,1,0:T(8,128)S(1)}, u32[]{:S(2)}, u32[]{:S(2)}) collective-permute-start(f32[16,8,2048]{2,1,0:T(8,128)} %get-tuple-element.16.own_north_hbm), channel_id=1, source_target_pairs={{0,1},{1,2},{2,3},{3,4},{4,5},{5,6},{6,7},{7,8},{8,9},{9,10},{10,1... | collective-permute-start | bytes 3145736 | tf_op jit(solution)/shard_map/ppermute | solution.py:409
  10.2 46.0 %collective-permute-done.from_south_hbm = f32[16,8,2048]{2,1,0:T(8,128)S(1)} collective-permute-done((f32[16,8,2048]{2,1,0:T(8,128)}, f32[16,8,2048]{2,1,0:T(8,128)S(1)}, u32[]{:S(2)}, u32[]{:S(2)}) %collective-permute-start) | collective-permute-done | bytes 1048608 | tf_op jit(solution)/shard_map/ppermute | solution.py:409
  56.1 0.0 collective-permute-done.1.from_north_hbm
  56.1 0.0 copy-done
  56.1 0.0 copy-start.3
  56.1 0.0 copy-start.4
  56.1 0.0 copy-start.5
  56.1 6.5 %shard_map.92 = (f32[4,8,8,2048]{3,2,1,0:T(8,128)}, f32[2,8,2048]{2,1,0:T(8,128)S(1)}, f32[2,8,2048]{2,1,0:T(8,128)S(1)}) custom-call(s32[1]{0:T(128)} %bitcast.lev_ref, f32[8,4,8,2048]{3,2,1,0:T(8,128)} %get-tuple-element.15.part_hbm, f32[16,8,2048]{2,1,0:T(8,128)} %get-tuple-element.16.own_north_hbm, f32[17,8,2048]{2,1,0:T(8,128)} %get-tuple-element.17.own_south_hbm, ...), custom_call_target="tpu_custom_call" | custom-call | tf_op jit(solution)/shard_map/pallas_call | solution.py:435
  62.6 0.0 copy-start.1
  62.6 0.0 copy-start.2
  62.6 0.6 collective-permute-start.2
  63.2 1.0 collective-permute-done.2
  64.2 0.4 collective-permute-start.3
  64.6 0.0 copy-done.3
  64.6 0.0 copy-done.4
  64.6 0.0 copy-done.5
  64.6 1.3 %shard_map.95 = f32[16,24,128]{2,1,0:T(8,128)} custom-call(s32[1]{0:T(128)} %bitcast.11.lat_ref, s32[16]{0:T(128)S(1)} %bitcast.29, f32[16,16,128]{2,1,0:T(8,128)S(1)} %bitcast.27, s32[16,16]{1,0:T(8,128)S(1)} %bitcast.28), custom_call_target="tpu_custom_call" | custom-call | tf_op jit(solution)/shard_map/pallas_call | solution.py:412
  65.9 10.1 %all-to-all-start = ((f32[16,24,128]{2,1,0:T(8,128)}), f32[16,24,128]{2,1,0:T(8,128)S(1)}, u32[]{:S(2)}, u32[]{:S(2)}) async-start(f32[16,24,128]{2,1,0:T(8,128)} %shard_map.95), calls=%async_computation | async-start | bytes 393216 | tf_op jit(solution)/shard_map/all_to_all | solution.py:420
  76.0 0.7 collective-permute-start.4
  76.7 0.0 collective-permute-done.4
  76.7 0.7 collective-permute-start.5
  77.4 0.7 collective-permute-start.6
  78.1 7.8 %all-to-all-done.packed_ref = f32[16,24,128]{2,1,0:T(8,128)S(1)} async-done(((f32[16,24,128]{2,1,0:T(8,128)}), f32[16,24,128]{2,1,0:T(8,128)S(1)}, u32[]{:S(2)}, u32[]{:S(2)}) %all-to-all-start) | async-done | bytes 196640 | tf_op jit(solution)/shard_map/all_to_all | solution.py:420
  85.9 1.4 %shard_map.96 = f32[16,8,512]{2,1,0:T(8,128)} custom-call(f32[16,24,128]{2,1,0:T(8,128)S(1)} %all-to-all-done.packed_ref), custom_call_target="tpu_custom_call" | custom-call | tf_op jit(solution)/shard_map/pallas_call | solution.py:422
  87.3 13.0 %all-to-all-start.1 = ((f32[16,8,512]{2,1,0:T(8,128)}), f32[16,8,512]{2,1,0:T(8,128)S(1)}, u32[]{:S(2)}, u32[]{:S(2)}) async-start(f32[16,8,512]{2,1,0:T(8,128)} %shard_map.96), calls=%async_computation.1 | async-start | bytes 524288 | tf_op jit(solution)/shard_map/all_to_all | solution.py:425
  100.3 0.0 collective-permute-done.5
  100.3 0.0 collective-permute-done.6
  100.4 0.2 collective-permute-start.7
  100.6 0.0 copy-done.1
  100.6 0.0 copy-done.2
  100.6 0.8 shard_map.93
  101.4 0.0 collective-permute-done.3.other_hbm
  101.4 2.8 %shard_map.94 = f32[4,64,2048]{2,1,0:T(8,128)S(1)} custom-call(s32[1]{0:T(128)} %bitcast.lev_ref, f32[4,8,8,2048]{3,2,1,0:T(8,128)} %get-tuple-element.21.adv_hbm, f32[4,8,8,2048]{3,2,1,0:T(8,128)} %collective-permute-done.3.other_hbm, s32[2,4,2048]{2,1,0:T(4,128)S(1)} %copy-done, f32[4,2048]{1,0:T(4,128)S(1)} %copy-done.2, ...), custom_call_target="tpu_custom_call" | custom-call | tf_op jit(solution)/shard_map/pallas_call | solution.py:467
  104.2 4.8 %all-to-all-done.1.forcing_ref = f32[16,8,512]{2,1,0:T(8,128)S(1)} async-done(((f32[16,8,512]{2,1,0:T(8,128)}), f32[16,8,512]{2,1,0:T(8,128)S(1)}, u32[]{:S(2)}, u32[]{:S(2)}) %all-to-all-start.1) | async-done | bytes 262176 | tf_op jit(solution)/shard_map/all_to_all | solution.py:425
  109.0 0.0 collective-permute-done.7.other_ref
  109.0 1.5 %shard_map.97 = f32[8,512,128]{2,1,0:T(8,128)} custom-call(s32[1]{0:T(128)} %bitcast.lev_ref, f32[4,8,8,2048]{3,2,1,0:T(8,128)S(1)} %bitcast.26, f32[4,8,2048]{2,1,0:T(8,128)S(1)} %get-tuple-element.23.gain_ref, f32[2,8,2048]{2,1,0:T(8,128)S(1)} %add_add_fusion.own_ref, f32[2,8,2048]{2,1,0:T(8,128)S(1)} %collective-permute-done.7.other_ref, ...), custom_call_target="tpu_custom_call" | custom-call | tf_op jit(solution)/shard_map/pallas_call | solution.py:476
  (3 shorter events, 0.1 us)
Async XLA Ops:
  0.0 56.1 %copy-start = (s32[2,4,2048]{2,1,0:T(4,128)S(1)}, s32[2,4,2048]{2,1,0:T(4,128)}, u32[]{:S(2)}) copy-start(s32[2,4,2048]{2,1,0:T(4,128)} %band_ref.5) | copy-start | bytes 196612
  4.2 51.9 %collective-permute-start.1 = (f32[17,8,2048]{2,1,0:T(8,128)}, f32[17,8,2048]{2,1,0:T(8,128)S(1)}, u32[]{:S(2)}, u32[]{:S(2)}) collective-permute-start(f32[17,8,2048]{2,1,0:T(8,128)} %get-tuple-element.17.own_south_hbm), channel_id=1, source_target_pairs={{1,0},{2,1},{3,2},{4,3},{5,4},{6,5},{7,6},{8,7},{9,8},{10,9},{11,1... | collective-permute-start | bytes 3342344 | tf_op jit(solution)/shard_map/ppermute | solution.py:410
  5.5 50.6 %collective-permute-start = (f32[16,8,2048]{2,1,0:T(8,128)}, f32[16,8,2048]{2,1,0:T(8,128)S(1)}, u32[]{:S(2)}, u32[]{:S(2)}) collective-permute-start(f32[16,8,2048]{2,1,0:T(8,128)} %get-tuple-element.16.own_north_hbm), channel_id=1, source_target_pairs={{0,1},{1,2},{2,3},{3,4},{4,5},{5,6},{6,7},{7,8},{8,9},{9,10},{10,1... | collective-permute-start | bytes 3145736 | tf_op jit(solution)/shard_map/ppermute | solution.py:409
  56.1 8.5 %copy-start.3 = (f32[1,1,16,16,128]{4,3,2,1,0:T(8,128)S(1)}, f32[1,1,16,16,128]{4,3,2,1,0:T(8,128)}, u32[]{:S(2)}) copy-start(f32[1,1,16,16,128]{4,3,2,1,0:T(8,128)} %param.15) | copy-start | bytes 393220
  56.1 8.5 %copy-start.4 = (s32[1,1,16,16]{3,2,1,0:T(8,128)S(1)}, s32[1,1,16,16]{3,2,1,0:T(8,128)}, u32[]{:S(2)}) copy-start(s32[1,1,16,16]{3,2,1,0:T(8,128)} %param.16) | copy-start | bytes 3076
  56.1 8.5 %copy-start.5 = (s32[1,1,16]{2,1,0:T(1,128)S(1)}, s32[1,1,16]{2,1,0:T(1,128)}, u32[]{:S(2)}) copy-start(s32[1,1,16]{2,1,0:T(1,128)} %param.17) | copy-start | bytes 196
  62.6 38.0 %copy-start.1 = (f32[4,8,16,16]{3,2,1,0:T(8,128)S(1)}, f32[4,8,16,16]{3,2,1,0:T(8,128)}, u32[]{:S(2)}) copy-start(f32[4,8,16,16]{3,2,1,0:T(8,128)} %inv_ref.1) | copy-start | bytes 98308
  62.6 37.9 %copy-start.2 = (f32[4,2048]{1,0:T(4,128)S(1)}, f32[4,2048]{1,0:T(4,128)}, u32[]{:S(2)}) copy-start(f32[4,2048]{1,0:T(4,128)} %flux_ref.3) | copy-start | bytes 98308
  62.6 1.6 %collective-permute-start.2 = (f32[2,8,2048]{2,1,0:T(8,128)S(1)}, f32[2,8,2048]{2,1,0:T(8,128)S(1)}, u32[]{:S(2)}, u32[]{:S(2)}) collective-permute-start(f32[2,8,2048]{2,1,0:T(8,128)S(1)} %get-tuple-element.20), channel_id=1, source_target_pairs={{0,16},{16,0},{32,48},{48,32},{64,80},{80,64},{96,112},{112,96},{1... | collective-permute-start | bytes 393224 | tf_op jit(solution)/shard_map/ppermute | solution.py:449
  64.2 37.2 %collective-permute-start.3 = (f32[4,8,8,2048]{3,2,1,0:T(8,128)}, f32[4,8,8,2048]{3,2,1,0:T(8,128)}, u32[]{:S(2)}, u32[]{:S(2)}) collective-permute-start(f32[4,8,8,2048]{3,2,1,0:T(8,128)} %get-tuple-element.21.adv_hbm), channel_id=1, source_target_pairs={{0,16},{16,0},{32,48},{48,32},{64,80},{80,64},{96,112},{112,96},{1... | collective-permute-start | bytes 6291464 | tf_op jit(solution)/shard_map/ppermute | solution.py:455
  65.9 20.0 %all-to-all-start = ((f32[16,24,128]{2,1,0:T(8,128)}), f32[16,24,128]{2,1,0:T(8,128)S(1)}, u32[]{:S(2)}, u32[]{:S(2)}) async-start(f32[16,24,128]{2,1,0:T(8,128)} %shard_map.95), calls=%async_computation | async-start | bytes 393216 | tf_op jit(solution)/shard_map/all_to_all | solution.py:420
  76.0 0.7 collective-permute-start.4
  76.7 23.6 %collective-permute-start.5 = (f32[2,8,2048]{2,1,0:T(8,128)S(1)}, f32[2,8,2048]{2,1,0:T(8,128)S(1)}, u32[]{:S(2)}, u32[]{:S(2)}) collective-permute-start(f32[2,8,2048]{2,1,0:T(8,128)S(1)} %add.13), channel_id=1, source_target_pairs={{64,128},{80,144},{96,160},{112,176},{128,192},{144,208},{160,224}... | collective-permute-start | bytes 393224 | tf_op jit(solution)/shard_map/ppermute | solution.py:463
  77.4 22.9 %collective-permute-start.6 = (f32[2,8,2048]{2,1,0:T(8,128)S(1)}, f32[2,8,2048]{2,1,0:T(8,128)S(1)}, u32[]{:S(2)}, u32[]{:S(2)}) collective-permute-start(f32[2,8,2048]{2,1,0:T(8,128)S(1)} %add.13), channel_id=1, source_target_pairs={{64,192},{80,208},{96,224},{112,240},{128,64},{144,80},{160,96},{1... | collective-permute-start | bytes 393224 | tf_op jit(solution)/shard_map/ppermute | solution.py:463
  87.3 21.7 %all-to-all-start.1 = ((f32[16,8,512]{2,1,0:T(8,128)}), f32[16,8,512]{2,1,0:T(8,128)S(1)}, u32[]{:S(2)}, u32[]{:S(2)}) async-start(f32[16,8,512]{2,1,0:T(8,128)} %shard_map.96), calls=%async_computation.1 | async-start | bytes 524288 | tf_op jit(solution)/shard_map/all_to_all | solution.py:425
  100.4 8.7 %collective-permute-start.7 = (f32[2,8,2048]{2,1,0:T(8,128)S(1)}, f32[2,8,2048]{2,1,0:T(8,128)S(1)}, u32[]{:S(2)}, u32[]{:S(2)}) collective-permute-start(f32[2,8,2048]{2,1,0:T(8,128)S(1)} %add_add_fusion.own_ref), channel_id=1, source_target_pairs={{0,16},{16,0},{32,48},{48,32},{64,80},{80,64},{96,112},{112,96},{1... | collective-permute-start | bytes 393224 | tf_op jit(solution)/shard_map/ppermute | solution.py:465

commit v2 on v1

--- a/solution.py
+++ b/solution.py
@@ -83,9 +83,40 @@
             coef_ref[4, r, :, s] = center
 
 
+def edge_kernel(a_hbm, last_hbm, first_hbm, a_ref, last_ref, first_ref, sems):
+    def incoming(t):
+        return pltpu.make_async_copy(a_hbm.at[t], a_ref.at[t], sems.at[t, 0])
+
+    def outgoing(t):
+        return [
+            pltpu.make_async_copy(last_ref.at[t], last_hbm.at[t], sems.at[t, 1]),
+            pltpu.make_async_copy(first_ref.at[t], first_hbm.at[t], sems.at[t, 2]),
+        ]
+
+    @pl.loop(0, 8)
+    def _(t):
+        incoming(t).start()
+
+    @pl.loop(0, 8)
+    def _(t):
+        incoming(t).wait()
+        for k in range(8):
+            tiles = swap_axes8([a_ref[t, pl.ds(level * 64 + k * 8, 8), :] for level in range(8)])
+            for half in range(2):
+                first_ref[t, :, lane_slice(2 * k + half)] = tiles[4 * half]
+                last_ref[t, :, lane_slice(2 * k + half)] = tiles[4 * half + 3]
+        for copy in outgoing(t):
+            copy.start()
+
+    @pl.loop(0, 8)
+    def _(t):
+        for copy in outgoing(t):
+            copy.wait()
+
+
 def prep_kernel(
     a_hbm, u_hbm, v_hbm, part_hbm, north_hbm, south_hbm, coef_hbm,
-    a_ref, u_ref, v_ref, rows_ref, v_rows, part_ref, north_ref, south_ref, coef_ref, sems,
+    a_ref, u_ref, v_ref, rows_ref, v_rows, part_ref, coef_ref, sems,
 ):
     faces = [
         pltpu.make_async_copy(u_hbm, u_ref, sems.at[8, 2]),
@@ -102,19 +133,17 @@
         incoming(t).start()
 
     def copies(t):
-        pair = pl.ds(2 * t, 2)
         return [
             pltpu.make_async_copy(part_ref.at[t], part_hbm.at[t], sems.at[t, 0]),
-            pltpu.make_async_copy(north_ref.at[pair], north_hbm.at[pair], sems.at[t, 1]),
-            pltpu.make_async_copy(south_ref.at[pair], south_hbm.at[pair], sems.at[t, 2]),
+            pltpu.make_async_copy(part_ref.at[t, 3], north_hbm.at[t], sems.at[t, 1]),
+            pltpu.make_async_copy(part_ref.at[t, 0], south_hbm.at[t], sems.at[t, 2]),
         ]
 
     for copy in faces:
         copy.wait()
     flow_coefficients(u_ref, v_ref, rows_ref, v_rows, coef_ref)
-    south_ref[16] = v_rows[0]
     coef_copy = pltpu.make_async_copy(coef_ref, coef_hbm, sems.at[8, 0])
-    face_copy = pltpu.make_async_copy(south_ref.at[pl.ds(16, 1)], south_hbm.at[pl.ds(16, 1)], sems.at[8, 1])
+    face_copy = pltpu.make_async_copy(v_rows.at[0], south_hbm.at[8], sems.at[8, 1])
     coef_copy.start()
     face_copy.start()
 
@@ -134,12 +163,6 @@
                 if r > 0:
                     out = out - rows_ref[r - 1, :, s] * coef_ref[3, r, :, s]
                 part_ref[t, r, :, s] = out
-                if r == 3:
-                    north_ref[2 * t, :, s] = row[j]
-                    north_ref[2 * t + 1, :, s] = out
-                if r == 0:
-                    south_ref[2 * t, :, s] = row[j]
-                    south_ref[2 * t + 1, :, s] = out
         for copy in copies(t):
             copy.start()
 
@@ -153,27 +176,22 @@
 
 
 def advect_kernel(
-    lev_ref, part_hbm, own_north_hbm, own_south_hbm, from_south_hbm, from_north_hbm, coef_hbm, band_ref,
-    adv_hbm, keep_ref, send_ref,
-    adv_ref, edge_ref, sum_ref, inside_ref, part_ref, own_north_ref, own_south_ref, from_south_ref, from_north_ref, coef_ref, sems,
+    lev_ref, part_hbm, own_last_hbm, own_first_hbm, own_face_hbm, south_row_ref, south_part_ref, north_row_ref, north_part_ref,
+    coef_hbm, band_ref, adv_ref, keep_ref, send_ref,
+    edge_ref, sum_ref, inside_ref, part_ref, own_last_ref, own_first_ref, coef_ref, sems,
 ):
     tiles = range(16)
 
     def copies(t):
-        pair = pl.ds(2 * t, 2)
-        first = pl.ds(2 * t, 1)
         return [
             pltpu.make_async_copy(part_hbm.at[t], part_ref.at[t], sems.at[t, 0]),
-            pltpu.make_async_copy(own_north_hbm.at[first], own_north_ref.at[pl.ds(t, 1)], sems.at[t, 1]),
-            pltpu.make_async_copy(own_south_hbm.at[first], own_south_ref.at[pl.ds(t, 1)], sems.at[t, 2]),
-            pltpu.make_async_copy(from_south_hbm.at[pair], from_south_ref.at[pair], sems.at[t, 3]),
-            pltpu.make_async_copy(from_north_hbm.at[pair], from_north_ref.at[pair], sems.at[t, 4]),
+            pltpu.make_async_copy(own_last_hbm.at[t], own_last_ref.at[t], sems.at[t, 1]),
+            pltpu.make_async_copy(own_first_hbm.at[t], own_first_ref.at[t], sems.at[t, 2]),
         ]
 
     fixed = [
         pltpu.make_async_copy(coef_hbm, coef_ref, sems.at[8, 0]),
-        pltpu.make_async_copy(own_south_hbm.at[pl.ds(16, 1)], own_south_ref.at[pl.ds(8, 1)], sems.at[8, 1]),
-        pltpu.make_async_copy(from_north_hbm.at[pl.ds(16, 1)], from_north_ref.at[pl.ds(16, 1)], sems.at[8, 2]),
+        pltpu.make_async_copy(own_face_hbm.at[8], own_first_ref.at[8], sems.at[8, 1]),
     ]
     for copy in fixed:
         copy.start()
@@ -182,9 +200,6 @@
     def _(t):
         for copy in copies(t):
             copy.start()
-
-    def outgoing(t):
-        return pltpu.make_async_copy(adv_ref.at[:, t], adv_hbm.at[:, t], sems.at[t, 5])
 
     level = lax.broadcasted_iota(jnp.int32, (8, 2048), 0) + lev_ref[0] * 8
     for r in range(4):
@@ -194,9 +209,9 @@
 
     for copy in fixed:
         copy.wait()
-    north_face = jnp.maximum(from_north_ref[16], 0.0)
-    edge_ref[0] = jnp.maximum(own_south_ref[8], 0.0)
-    edge_ref[1] = jnp.minimum(from_north_ref[16], 0.0)
+    north_face = jnp.maximum(north_part_ref[8], 0.0)
+    edge_ref[0] = jnp.maximum(own_first_ref[8], 0.0)
+    edge_ref[1] = jnp.minimum(north_part_ref[8], 0.0)
     edge_ref[2] = north_face
     edge_ref[3] = coef_ref[4, 3] - north_face
 
@@ -208,15 +223,15 @@
         rows = [[] for _ in range(6)]
         for j in tiles:
             s = lane_slice(j)
-            a_south = from_south_ref[2 * t, :, s]
-            a_last = own_north_ref[t, :, s]
-            a_first = own_south_ref[t, :, s]
-            rows[0].append(from_south_ref[2 * t + 1, :, s] + edge_ref[0, :, s] * (a_first - a_south))
+            a_south = south_row_ref[t, :, s]
+            a_last = own_last_ref[t, :, s]
+            a_first = own_first_ref[t, :, s]
+            rows[0].append(south_part_ref[t, :, s] + edge_ref[0, :, s] * (a_first - a_south))
             rows[1].append(part_ref[t, 0, :, s] - coef_ref[3, 0, :, s] * a_south)
             rows[2].append(part_ref[t, 1, :, s])
             rows[3].append(part_ref[t, 2, :, s])
-            rows[4].append(part_ref[t, 3, :, s] + edge_ref[2, :, s] * (from_north_ref[2 * t, :, s] - a_last))
-            rows[5].append(from_north_ref[2 * t + 1, :, s] - edge_ref[1, :, s] * a_last)
+            rows[4].append(part_ref[t, 3, :, s] + edge_ref[2, :, s] * (north_row_ref[t, :, s] - a_last))
+            rows[5].append(north_part_ref[t, :, s] - edge_ref[1, :, s] * a_last)
         for r in range(4):
             x = rows[r + 1]
             e = east_tiles(x)
@@ -235,11 +250,6 @@
                 adv_ref[r, t, :, s] = out
                 band = jnp.sum(out * inside_ref[r, :, s], axis=0, keepdims=True)
                 sum_ref[r, :, s] = jnp.where(this_tracer, band, sum_ref[r, :, s])
-        outgoing(t).start()
-
-    @pl.loop(0, 8)
-    def _(t):
-        outgoing(t).wait()
 
     core = lax.rem(lev_ref[0], 2)
     keep_ref[...] = sum_ref[pl.ds(2 * core, 2)]
@@ -283,16 +293,7 @@
         matrix_ref[r, 64:128, 128:256] = jnp.zeros_like(low)
 
 
-def diffuse_kernel(lev_ref, adv_hbm, other_hbm, band_ref, flux_ref, matrix_ref, out_ref, adv_ref, other_ref, sems):
-    def copies(r):
-        return [
-            pltpu.make_async_copy(adv_hbm.at[r], adv_ref.at[r], sems.at[r, 0]),
-            pltpu.make_async_copy(other_hbm.at[r], other_ref.at[r], sems.at[r, 1]),
-        ]
-
-    for r in range(4):
-        for copy in copies(r):
-            copy.start()
+def diffuse_kernel(lev_ref, adv_ref, other_ref, band_ref, flux_ref, matrix_ref, out_ref):
     lev = lev_ref[0]
     level = lax.broadcasted_iota(jnp.int32, (8, 2048), 0)
     own_level = level + lev * 8
@@ -306,8 +307,6 @@
             kept = 1.0 - jnp.where((levels >= first) & (levels < last), flux, 0.0)
             return halves_of((values * kept[None]).reshape(64, 2048))
 
-        for copy in copies(r):
-            copy.wait()
         own_high, own_low = rest(adv_ref[r], own_level)
         other_high, other_low = rest(other_ref[r], other_level)
         stacked = jnp.concatenate([own_high, other_high, own_low, other_low], axis=0)
@@ -394,20 +393,35 @@
     def keep_far(x):
         return pltpu.with_memory_space_constraint(x, pltpu.HBM)
 
+    last_row, first_row = pl.pallas_call(
+        edge_kernel,
+        in_specs=[hbm],
+        out_specs=[hbm] * 2,
+        out_shape=[far(8, 8, lons), far(8, 8, lons)],
+        scratch_shapes=[
+            pltpu.VMEM((8, 512, LANES), F32), pltpu.VMEM((8, 8, lons), F32), pltpu.VMEM((8, 8, lons), F32),
+            pltpu.SemaphoreType.DMA((8, 3)),
+        ],
+        compiler_params=small,
+    )(keep_far(a_view))
     part, to_north, to_south, coef = pl.pallas_call(
         prep_kernel,
         in_specs=[hbm] * 3,
         out_specs=[hbm] * 4,
-        out_shape=[far(8, 4, 8, lons), far(16, 8, lons), far(17, 8, lons), far(5, 4, 8, lons)],
+        out_shape=[far(8, 4, 8, lons), far(8, 8, lons), far(9, 8, lons), far(5, 4, 8, lons)],
         scratch_shapes=[
             pltpu.VMEM((8, 512, LANES), F32), pltpu.VMEM((512, LANES), F32), pltpu.VMEM((512, LANES), F32),
-            row_scratch, row_scratch, pltpu.VMEM((8, 4, 8, lons), F32), pltpu.VMEM((16, 8, lons), F32),
-            pltpu.VMEM((17, 8, lons), F32), pltpu.VMEM((5, 4, 8, lons), F32), pltpu.SemaphoreType.DMA((9, 4)),
+            row_scratch, row_scratch, pltpu.VMEM((8, 4, 8, lons), F32), pltpu.VMEM((5, 4, 8, lons), F32),
+            pltpu.SemaphoreType.DMA((9, 4)),
         ],
         compiler_params=small,
     )(keep_far(a_view), keep_far(u_view), keep_far(v_view))
-    from_south = lax.ppermute(to_north, "lat", [(i, i + 1) for i in range(lat_count - 1)])
-    from_north = lax.ppermute(to_south, "lat", [(i + 1, i) for i in range(lat_count - 1)])
+    north = [(i, i + 1) for i in range(lat_count - 1)]
+    south = [(i + 1, i) for i in range(lat_count - 1)]
+    south_row = lax.ppermute(last_row, "lat", north)
+    north_row = lax.ppermute(first_row, "lat", south)
+    south_part = lax.ppermute(to_north, "lat", north)
+    north_part = lax.ppermute(to_south, "lat", south)
 
     packed = pl.pallas_call(
         pack_kernel,
@@ -434,16 +448,18 @@
 
     adv, keep, send = pl.pallas_call(
         advect_kernel,
-        in_specs=[smem] + [hbm] * 6 + [vmem],
-        out_specs=[hbm, vmem, vmem],
-        out_shape=[far(4, 8, 8, lons), shape(2, 8, lons), shape(2, 8, lons)],
+        in_specs=[smem] + [hbm] * 4 + [vmem] * 4 + [hbm, vmem],
+        out_specs=[vmem] * 3,
+        out_shape=[shape(4, 8, 8, lons), shape(2, 8, lons), shape(2, 8, lons)],
         scratch_shapes=[
-            pltpu.VMEM((4, 8, 8, lons), F32), row_scratch, row_scratch, row_scratch, pltpu.VMEM((8, 4, 8, lons), F32), pltpu.VMEM((8, 8, lons), F32),
-            pltpu.VMEM((9, 8, lons), F32), pltpu.VMEM((16, 8, lons), F32), pltpu.VMEM((17, 8, lons), F32),
-            pltpu.VMEM((5, 4, 8, lons), F32), pltpu.SemaphoreType.DMA((9, 6)),
+            row_scratch, row_scratch, row_scratch, pltpu.VMEM((8, 4, 8, lons), F32), pltpu.VMEM((8, 8, lons), F32),
+            pltpu.VMEM((9, 8, lons), F32), pltpu.VMEM((5, 4, 8, lons), F32), pltpu.SemaphoreType.DMA((9, 3)),
         ],
         compiler_params=small,
-    )(lev, keep_far(part), keep_far(to_north), keep_far(to_south), from_south, from_north, keep_far(coef), conv_band)
+    )(
+        lev, keep_far(part), keep_far(last_row), keep_far(first_row), keep_far(to_south),
+        south_row, south_part, north_row, north_part, keep_far(coef), conv_band,
+    )
 
     swap = [(i, i ^ 1) for i in range(lev_count)]
     swapped = lax.ppermute(send, "lev", swap)
@@ -466,12 +482,11 @@
 
     base = pl.pallas_call(
         diffuse_kernel,
-        in_specs=[smem, hbm, hbm] + [vmem] * 3,
+        in_specs=[smem] + [vmem] * 5,
         out_specs=vmem,
         out_shape=shape(4, 64, lons),
-        scratch_shapes=[pltpu.VMEM((4, 8, 8, lons), F32), pltpu.VMEM((4, 8, 8, lons), F32), pltpu.SemaphoreType.DMA((4, 2))],
-        compiler_params=small,
-    )(lev, keep_far(adv), keep_far(adv_other), conv_band, mass_flux, matrix)
+        compiler_params=small,
+    )(lev, adv, adv_other, conv_band, mass_flux, matrix)
 
     out = pl.pallas_call(
         finish_kernel,

time: 111 us -> 113 us (1.018)
  waiting for transfers between devices: 59.6 us -> 49.4 us
  starting transfers between devices: 32.2 us -> 38.2 us
  local copies, waits for them, and re-layouts: 0.03 us -> 5.94 us
    ppermute x2 -> x4, waiting for transfers between devices: 46 us -> 38 us  [the longest x1 26.8 us: body(): south_part = lax.ppermute(to_north, 'lat', north)]
    unnamed x12 -> x26, local copies, waits for them, and re-layouts: 0.03 us -> 5.94 us
    ppermute x2 -> x4, starting transfers between devices: 5.92 us -> 11.4 us  [the longest x1 4.59 us: body(): south_part = lax.ppermute(to_north, 'lat', north)]
    all_to_all x1, waiting for transfers between devices: 4.83 us -> 3.45 us  [body(): lax.all_to_all(forcing, 'lev', split_axis=0, concat_axis=0, tiled=True)]
    pallas_call x2 -> x3, Pallas kernels: 9.25 us -> 8.8 us  [the longest x1 3.85 us: body(): pl.pallas_call(advect_kernel, in_specs=[smem] + [hbm] * 4 + [vmem] * 4 +...]
  transfers between devices with their start and end apart: 10 -> 12, of which waited for: 4 -> 5; matrix products, arithmetic and copies ran while one was open for 0% -> 1% of each run, Pallas kernels for 6% -> 8%
where the time goes in v2:
time: 113 us
  waiting for transfers between devices  49.4 us (44%)
  starting transfers between devices  38.2 us (34%)
  Pallas kernels  18 us (16%)
  local copies, waits for them, and re-layouts  5.94 us (5%)
    ppermute x1, waiting for transfers between devices, body(): south_part = lax.ppermute(to_north, 'lat', north)  26.8 us
    all_to_all x1, starting transfers between devices, body(): lax.all_to_all(forcing, 'lev', split_axis=0, concat_axis=0, tiled=True)  13.6 us
    ppermute x1, waiting for transfers between devices, body(): south_row = lax.ppermute(last_row, 'lat', north)  11.2 us
    all_to_all x1, starting transfers between devices, body(): lax.all_to_all(packed, 'lat', split_axis=0, concat_axis=0, tiled=True)  10.1 us
    all_to_all x1, waiting for transfers between devices, body(): lax.all_to_all(packed, 'lat', split_axis=0, concat_axis=0, tiled=True)  6.93 us
    unnamed x26, local copies, waits for them, and re-layouts  5.94 us
    ppermute x1, starting transfers between devices, body(): south_part = lax.ppermute(to_north, 'lat', north)  4.59 us
    ppermute x1, starting transfers between devices, body(): south_row = lax.ppermute(last_row, 'lat', north)  4.26 us
  transfers between devices with their start and end apart: 12, of which 5 were waited for; matrix products, arithmetic and copies ran while one was open for 1% of the time, Pallas kernels for 8%

profile of v2, /device:TPU:1, one launch (start us, length us, event | category | flops | bytes accessed | tf_op | source)
XLA Modules:
  0.0 112.6 jit_solution(12545393625921160844)
XLA Ops:
  0.0 0.0 copy-start.2
  0.0 4.2 %shard_map.91 = (f32[8,4,8,2048]{3,2,1,0:T(8,128)}, f32[8,8,2048]{2,1,0:T(8,128)}, f32[9,8,2048]{2,1,0:T(8,128)}, f32[5,4,8,2048]{3,2,1,0:T(8,128)}) custom-call(f32[8,512,128]{2,1,0:T(8,128)} %bitcast.30, f32[512,128]{1,0:T(8,128)} %bitcast.32, f32[512,128]{1,0:T(8,128)} %bitcast.33), custom_call_target="tpu_custom_call" | custom-call | tf_op jit(solution)/shard_map/pallas_call | solution.py:407
  4.2 1.3 %collective-permute-start.3 = (f32[9,8,2048]{2,1,0:T(8,128)}, f32[9,8,2048]{2,1,0:T(8,128)S(1)}, u32[]{:S(2)}, u32[]{:S(2)}) collective-permute-start(f32[9,8,2048]{2,1,0:T(8,128)} %get-tuple-element.20.own_face_hbm), channel_id=1, source_target_pairs={{1,0},{2,1},{3,2},{4,3},{5,4},{6,5},{7,6},{8,7},{9,8},{10,9},{11,1... | collective-permute-start | bytes 1769480 | tf_op jit(solution)/shard_map/ppermute | solution.py:424
  5.5 4.6 %collective-permute-start.1 = (f32[8,8,2048]{2,1,0:T(8,128)}, f32[8,8,2048]{2,1,0:T(8,128)S(1)}, u32[]{:S(2)}, u32[]{:S(2)}) collective-permute-start(f32[8,8,2048]{2,1,0:T(8,128)} %get-tuple-element.21), channel_id=1, source_target_pairs={{0,1},{1,2},{2,3},{3,4},{4,5},{5,6},{6,7},{7,8},{8,9},{9,10},{10,1... | collective-permute-start | bytes 1572872 | tf_op jit(solution)/shard_map/ppermute | solution.py:423
  10.1 2.4 %shard_map.92 = (f32[8,8,2048]{2,1,0:T(8,128)}, f32[8,8,2048]{2,1,0:T(8,128)}) custom-call(f32[8,512,128]{2,1,0:T(8,128)} %bitcast.31), custom_call_target="tpu_custom_call" | custom-call | tf_op jit(solution)/shard_map/pallas_call | solution.py:396
  12.5 4.3 %collective-permute-start = (f32[8,8,2048]{2,1,0:T(8,128)}, f32[8,8,2048]{2,1,0:T(8,128)S(1)}, u32[]{:S(2)}, u32[]{:S(2)}) collective-permute-start(f32[8,8,2048]{2,1,0:T(8,128)} %get-tuple-element.18.own_last_hbm), channel_id=1, source_target_pairs={{0,1},{1,2},{2,3},{3,4},{4,5},{5,6},{6,7},{7,8},{8,9},{9,10},{10,1... | collective-permute-start | bytes 1572872 | tf_op jit(solution)/shard_map/ppermute | solution.py:421
  16.8 1.3 %collective-permute-start.2 = (f32[8,8,2048]{2,1,0:T(8,128)}, f32[8,8,2048]{2,1,0:T(8,128)S(1)}, u32[]{:S(2)}, u32[]{:S(2)}) collective-permute-start(f32[8,8,2048]{2,1,0:T(8,128)} %get-tuple-element.19.own_first_hbm), channel_id=1, source_target_pairs={{1,0},{2,1},{3,2},{4,3},{5,4},{6,5},{7,6},{8,7},{9,8},{10,9},{11,1... | collective-permute-start | bytes 1572872 | tf_op jit(solution)/shard_map/ppermute | solution.py:422
  18.1 26.8 %collective-permute-done.1.south_part_ref = f32[8,8,2048]{2,1,0:T(8,128)S(1)} collective-permute-done((f32[8,8,2048]{2,1,0:T(8,128)}, f32[8,8,2048]{2,1,0:T(8,128)S(1)}, u32[]{:S(2)}, u32[]{:S(2)}) %collective-permute-start.1) | collective-permute-done | bytes 524320 | tf_op jit(solution)/shard_map/ppermute | solution.py:423
  44.8 11.2 %collective-permute-done.south_row_ref = f32[8,8,2048]{2,1,0:T(8,128)S(1)} collective-permute-done((f32[8,8,2048]{2,1,0:T(8,128)}, f32[8,8,2048]{2,1,0:T(8,128)S(1)}, u32[]{:S(2)}, u32[]{:S(2)}) %collective-permute-start) | collective-permute-done | bytes 524320 | tf_op jit(solution)/shard_map/ppermute | solution.py:421
  56.1 0.0 copy-start.3
  56.1 0.8 copy-done.3
  56.9 0.0 collective-permute-done.2.north_row_ref
  56.9 0.0 copy-start.5
  56.9 0.8 copy-done.5
  57.7 0.0 collective-permute-done.3.north_part_ref
  57.7 0.0 copy-done.2
  57.7 0.0 copy-start.4
  57.7 1.0 copy-done.4
  58.7 0.0 copy-start.6
  58.7 1.0 copy-done.6
  59.7 0.0 copy-start.10
  59.7 0.0 copy-start.11
  59.7 0.0 copy-start.12
  59.8 3.8 %shard_map.93 = (f32[4,8,8,2048]{3,2,1,0:T(8,128)S(1)}, f32[2,8,2048]{2,1,0:T(8,128)S(1)}, f32[2,8,2048]{2,1,0:T(8,128)S(1)}) custom-call(s32[1]{0:T(128)} %bitcast.lev_ref, f32[8,4,8,2048]{3,2,1,0:T(8,128)} %get-tuple-element.17.part_hbm, f32[8,8,2048]{2,1,0:T(8,128)} %get-tuple-element.18.own_last_hbm, f32[8,8,2048]{2,1,0:T(8,128)} %get-tuple-element.19.own_first_hbm, ...), custom_call_target="tpu_custom_call" | custom-call | tf_op jit(solution)/shard_map/pallas_call | solution.py:449
  63.6 0.0 copy-start.9
  63.6 0.6 copy-done.9
  64.3 0.0 copy-start
  64.3 0.0 copy-start.7
  64.3 0.0 copy-start.8
  64.3 0.5 collective-permute-start.4
  64.8 1.0 collective-permute-done.4
  65.7 0.4 collective-permute-start.5
  66.1 0.0 copy-done.10
  66.1 0.0 copy-done.11
  66.1 0.0 copy-done.12
  66.1 1.3 %shard_map.96 = f32[16,24,128]{2,1,0:T(8,128)} custom-call(s32[1]{0:T(128)} %bitcast.13.lat_ref, s32[16]{0:T(128)S(1)} %bitcast.29, f32[16,16,128]{2,1,0:T(8,128)S(1)} %bitcast.27, s32[16,16]{1,0:T(8,128)S(1)} %bitcast.28), custom_call_target="tpu_custom_call" | custom-call | tf_op jit(solution)/shard_map/pallas_call | solution.py:426
  67.4 10.1 %all-to-all-start = ((f32[16,24,128]{2,1,0:T(8,128)}), f32[16,24,128]{2,1,0:T(8,128)S(1)}, u32[]{:S(2)}, u32[]{:S(2)}) async-start(f32[16,24,128]{2,1,0:T(8,128)} %shard_map.96), calls=%async_computation | async-start | bytes 393216 | tf_op jit(solution)/shard_map/all_to_all | solution.py:434
  77.5 0.9 add.12
  78.5 0.7 collective-permute-start.6
  79.1 0.0 collective-permute-done.6
  79.2 0.7 collective-permute-start.7
  79.8 0.7 collective-permute-start.8
  80.5 6.9 %all-to-all-done.packed_ref = f32[16,24,128]{2,1,0:T(8,128)S(1)} async-done(((f32[16,24,128]{2,1,0:T(8,128)}), f32[16,24,128]{2,1,0:T(8,128)S(1)}, u32[]{:S(2)}, u32[]{:S(2)}) %all-to-all-start) | async-done | bytes 196640 | tf_op jit(solution)/shard_map/all_to_all | solution.py:434
  87.4 1.4 %shard_map.97 = f32[16,8,512]{2,1,0:T(8,128)} custom-call(f32[16,24,128]{2,1,0:T(8,128)S(1)} %all-to-all-done.packed_ref), custom_call_target="tpu_custom_call" | custom-call | tf_op jit(solution)/shard_map/pallas_call | solution.py:436
  88.9 13.6 %all-to-all-start.1 = ((f32[16,8,512]{2,1,0:T(8,128)}), f32[16,8,512]{2,1,0:T(8,128)S(1)}, u32[]{:S(2)}, u32[]{:S(2)}) async-start(f32[16,8,512]{2,1,0:T(8,128)} %shard_map.97), calls=%async_computation.1 | async-start | bytes 524288 | tf_op jit(solution)/shard_map/all_to_all | solution.py:439
  102.5 0.0 collective-permute-done.7
  102.5 0.0 collective-permute-done.8
  102.5 0.2 collective-permute-start.9
  102.7 0.0 copy-done.7
  102.7 0.0 copy-done.8
  102.7 0.8 shard_map.94
  103.5 0.0 collective-permute-done.5.other_ref
  103.6 0.0 copy-done
  103.6 0.0 copy-start.1
  103.6 1.6 %copy-done.1 = f32[4,8,8,2048]{3,2,1,0:T(8,128)S(1)} copy-done((f32[4,8,8,2048]{3,2,1,0:T(8,128)S(1)}, f32[4,8,8,2048]{3,2,1,0:T(8,128)}, u32[]{:S(2)}) %copy-start.1) | copy-done | bytes 2097176
  105.2 2.5 %shard_map.95 = f32[4,64,2048]{2,1,0:T(8,128)S(1)} custom-call(s32[1]{0:T(128)} %bitcast.lev_ref, f32[4,8,8,2048]{3,2,1,0:T(8,128)S(1)} %copy-done.1, f32[4,8,8,2048]{3,2,1,0:T(8,128)} %collective-permute-done.5.other_ref, s32[2,4,2048]{2,1,0:T(4,128)S(1)} %copy-done.2, f32[4,2048]{1,0:T(4,128)S(1)} %copy-done.8, ...), custom_call_target="tpu_custom_call" | custom-call | tf_op jit(solution)/shard_map/pallas_call | solution.py:483
  107.7 3.4 %all-to-all-done.1.forcing_ref = f32[16,8,512]{2,1,0:T(8,128)S(1)} async-done(((f32[16,8,512]{2,1,0:T(8,128)}), f32[16,8,512]{2,1,0:T(8,128)S(1)}, u32[]{:S(2)}, u32[]{:S(2)}) %all-to-all-start.1) | async-done | bytes 262176 | tf_op jit(solution)/shard_map/all_to_all | solution.py:439
  111.2 0.0 collective-permute-done.9.other_ref
  111.2 1.5 %shard_map.98 = f32[8,512,128]{2,1,0:T(8,128)} custom-call(s32[1]{0:T(128)} %bitcast.lev_ref, f32[4,8,8,2048]{3,2,1,0:T(8,128)S(1)} %bitcast.26, f32[4,8,2048]{2,1,0:T(8,128)S(1)} %get-tuple-element.27.gain_ref, f32[2,8,2048]{2,1,0:T(8,128)S(1)} %add_add_fusion.own_ref, f32[2,8,2048]{2,1,0:T(8,128)S(1)} %collective-permute-done.9.other_ref, ...), custom_call_target="tpu_custom_call" | custom-call | tf_op jit(solution)/shard_map/pallas_call | solution.py:491
  (2 shorter events, 0.0 us)
Async XLA Ops:
  0.0 57.7 %copy-start.2 = (s32[2,4,2048]{2,1,0:T(4,128)S(1)}, s32[2,4,2048]{2,1,0:T(4,128)}, u32[]{:S(2)}) copy-start(s32[2,4,2048]{2,1,0:T(4,128)} %band_ref.5) | copy-start | bytes 196612
  4.2 53.5 %collective-permute-start.3 = (f32[9,8,2048]{2,1,0:T(8,128)}, f32[9,8,2048]{2,1,0:T(8,128)S(1)}, u32[]{:S(2)}, u32[]{:S(2)}) collective-permute-start(f32[9,8,2048]{2,1,0:T(8,128)} %get-tuple-element.20.own_face_hbm), channel_id=1, source_target_pairs={{1,0},{2,1},{3,2},{4,3},{5,4},{6,5},{7,6},{8,7},{9,8},{10,9},{11,1... | collective-permute-start | bytes 1769480 | tf_op jit(solution)/shard_map/ppermute | solution.py:424
  5.5 39.4 %collective-permute-start.1 = (f32[8,8,2048]{2,1,0:T(8,128)}, f32[8,8,2048]{2,1,0:T(8,128)S(1)}, u32[]{:S(2)}, u32[]{:S(2)}) collective-permute-start(f32[8,8,2048]{2,1,0:T(8,128)} %get-tuple-element.21), channel_id=1, source_target_pairs={{0,1},{1,2},{2,3},{3,4},{4,5},{5,6},{6,7},{7,8},{8,9},{9,10},{10,1... | collective-permute-start | bytes 1572872 | tf_op jit(solution)/shard_map/ppermute | solution.py:423
  12.5 43.6 %collective-permute-start = (f32[8,8,2048]{2,1,0:T(8,128)}, f32[8,8,2048]{2,1,0:T(8,128)S(1)}, u32[]{:S(2)}, u32[]{:S(2)}) collective-permute-start(f32[8,8,2048]{2,1,0:T(8,128)} %get-tuple-element.18.own_last_hbm), channel_id=1, source_target_pairs={{0,1},{1,2},{2,3},{3,4},{4,5},{5,6},{6,7},{7,8},{8,9},{9,10},{10,1... | collective-permute-start | bytes 1572872 | tf_op jit(solution)/shard_map/ppermute | solution.py:421
  16.8 40.1 %collective-permute-start.2 = (f32[8,8,2048]{2,1,0:T(8,128)}, f32[8,8,2048]{2,1,0:T(8,128)S(1)}, u32[]{:S(2)}, u32[]{:S(2)}) collective-permute-start(f32[8,8,2048]{2,1,0:T(8,128)} %get-tuple-element.19.own_first_hbm), channel_id=1, source_target_pairs={{1,0},{2,1},{3,2},{4,3},{5,4},{6,5},{7,6},{8,7},{9,8},{10,9},{11,1... | collective-permute-start | bytes 1572872 | tf_op jit(solution)/shard_map/ppermute | solution.py:422
  56.1 0.8 copy-start.3
  56.9 0.8 copy-start.5
  57.7 1.0 copy-start.4
  58.7 1.0 copy-start.6
  59.7 6.4 %copy-start.10 = (f32[1,1,16,16,128]{4,3,2,1,0:T(8,128)S(1)}, f32[1,1,16,16,128]{4,3,2,1,0:T(8,128)}, u32[]{:S(2)}) copy-start(f32[1,1,16,16,128]{4,3,2,1,0:T(8,128)} %param.15) | copy-start | bytes 393220
  59.7 6.4 %copy-start.11 = (s32[1,1,16,16]{3,2,1,0:T(8,128)S(1)}, s32[1,1,16,16]{3,2,1,0:T(8,128)}, u32[]{:S(2)}) copy-start(s32[1,1,16,16]{3,2,1,0:T(8,128)} %param.16) | copy-start | bytes 3076
  59.7 6.4 %copy-start.12 = (s32[1,1,16]{2,1,0:T(1,128)S(1)}, s32[1,1,16]{2,1,0:T(1,128)}, u32[]{:S(2)}) copy-start(s32[1,1,16]{2,1,0:T(1,128)} %param.17) | copy-start | bytes 196
  63.6 0.7 copy-start.9
  64.3 39.3 %copy-start = (f32[4,8,8,2048]{3,2,1,0:T(8,128)}, f32[4,8,8,2048]{3,2,1,0:T(8,128)S(1)}, u32[]{:S(2)}) copy-start(f32[4,8,8,2048]{3,2,1,0:T(8,128)S(1)} %get-tuple-element.25.adv_ref) | copy-start | bytes 6291460
  64.3 38.4 %copy-start.7 = (f32[4,8,16,16]{3,2,1,0:T(8,128)S(1)}, f32[4,8,16,16]{3,2,1,0:T(8,128)}, u32[]{:S(2)}) copy-start(f32[4,8,16,16]{3,2,1,0:T(8,128)} %inv_ref.1) | copy-start | bytes 98308
  64.3 38.4 %copy-start.8 = (f32[4,2048]{1,0:T(4,128)S(1)}, f32[4,2048]{1,0:T(4,128)}, u32[]{:S(2)}) copy-start(f32[4,2048]{1,0:T(4,128)} %flux_ref.3) | copy-start | bytes 98308
  64.3 1.5 %collective-permute-start.4 = (f32[2,8,2048]{2,1,0:T(8,128)S(1)}, f32[2,8,2048]{2,1,0:T(8,128)S(1)}, u32[]{:S(2)}, u32[]{:S(2)}) collective-permute-start(f32[2,8,2048]{2,1,0:T(8,128)S(1)} %get-tuple-element.24), channel_id=1, source_target_pairs={{0,16},{16,0},{32,48},{48,32},{64,80},{80,64},{96,112},{112,96},{1... | collective-permute-start | bytes 393224 | tf_op jit(solution)/shard_map/ppermute | solution.py:465
  65.7 37.8 %collective-permute-start.5 = (f32[4,8,8,2048]{3,2,1,0:T(8,128)S(1)}, f32[4,8,8,2048]{3,2,1,0:T(8,128)}, u32[]{:S(2)}, u32[]{:S(2)}) collective-permute-start(f32[4,8,8,2048]{3,2,1,0:T(8,128)S(1)} %get-tuple-element.25.adv_ref), channel_id=1, source_target_pairs={{0,16},{16,0},{32,48},{48,32},{64,80},{80,64},{96,112},{112,96},{1... | collective-permute-start | bytes 6291464 | tf_op jit(solution)/shard_map/ppermute | solution.py:471
  67.4 20.0 %all-to-all-start = ((f32[16,24,128]{2,1,0:T(8,128)}), f32[16,24,128]{2,1,0:T(8,128)S(1)}, u32[]{:S(2)}, u32[]{:S(2)}) async-start(f32[16,24,128]{2,1,0:T(8,128)} %shard_map.96), calls=%async_computation | async-start | bytes 393216 | tf_op jit(solution)/shard_map/all_to_all | solution.py:434
  78.5 0.7 collective-permute-start.6
  79.2 23.3 %collective-permute-start.7 = (f32[2,8,2048]{2,1,0:T(8,128)S(1)}, f32[2,8,2048]{2,1,0:T(8,128)S(1)}, u32[]{:S(2)}, u32[]{:S(2)}) collective-permute-start(f32[2,8,2048]{2,1,0:T(8,128)S(1)} %add.13), channel_id=1, source_target_pairs={{64,128},{80,144},{96,160},{112,176},{128,192},{144,208},{160,224}... | collective-permute-start | bytes 393224 | tf_op jit(solution)/shard_map/ppermute | solution.py:479
  79.8 22.6 %collective-permute-start.8 = (f32[2,8,2048]{2,1,0:T(8,128)S(1)}, f32[2,8,2048]{2,1,0:T(8,128)S(1)}, u32[]{:S(2)}, u32[]{:S(2)}) collective-permute-start(f32[2,8,2048]{2,1,0:T(8,128)S(1)} %add.13), channel_id=1, source_target_pairs={{64,192},{80,208},{96,224},{112,240},{128,64},{144,80},{160,96},{1... | collective-permute-start | bytes 393224 | tf_op jit(solution)/shard_map/ppermute | solution.py:479
  88.9 22.3 %all-to-all-start.1 = ((f32[16,8,512]{2,1,0:T(8,128)}), f32[16,8,512]{2,1,0:T(8,128)S(1)}, u32[]{:S(2)}, u32[]{:S(2)}) async-start(f32[16,8,512]{2,1,0:T(8,128)} %shard_map.97), calls=%async_computation.1 | async-start | bytes 524288 | tf_op jit(solution)/shard_map/all_to_all | solution.py:439
  102.5 8.7 %collective-permute-start.9 = (f32[2,8,2048]{2,1,0:T(8,128)S(1)}, f32[2,8,2048]{2,1,0:T(8,128)S(1)}, u32[]{:S(2)}, u32[]{:S(2)}) collective-permute-start(f32[2,8,2048]{2,1,0:T(8,128)S(1)} %add_add_fusion.own_ref), channel_id=1, source_target_pairs={{0,16},{16,0},{32,48},{48,32},{64,80},{80,64},{96,112},{112,96},{1... | collective-permute-start | bytes 393224 | tf_op jit(solution)/shard_map/ppermute | solution.py:481
  103.6 1.6 %copy-start.1 = (f32[4,8,8,2048]{3,2,1,0:T(8,128)S(1)}, f32[4,8,8,2048]{3,2,1,0:T(8,128)}, u32[]{:S(2)}) copy-start(f32[4,8,8,2048]{3,2,1,0:T(8,128)} %copy-done) | copy-start | bytes 6291460

commit v3 on v2

--- a/solution.py
+++ b/solution.py
@@ -38,6 +38,16 @@
                 tiles[i] = jnp.where(low_half, low, pltpu.roll(high, step, 0))
                 tiles[i + step] = jnp.where(low_half, pltpu.roll(low, 8 - step, 0), high)
     return tiles
+
+
+def level_sums(tiles):
+    row = lax.broadcasted_iota(jnp.int32, (8, LANES), 0)
+    for step in (1, 2, 4):
+        low = (row & step) == 0
+        tiles = [
+            jnp.where(low, a, b) + pltpu.roll(jnp.where(low, b, a), step, 0) for a, b in zip(tiles[::2], tiles[1::2])
+        ]
+    return tiles[0]
 
 
 def unpack_rows(source, target):
@@ -219,7 +229,6 @@
     def _(t):
         for copy in copies(t):
             copy.wait()
-        this_tracer = lax.broadcasted_iota(jnp.int32, (8, LANES), 0) == t
         rows = [[] for _ in range(6)]
         for j in tiles:
             s = lane_slice(j)
@@ -248,8 +257,13 @@
                     - rows[r][j] * coef_ref[3, r, :, s]
                 )
                 adv_ref[r, t, :, s] = out
-                band = jnp.sum(out * inside_ref[r, :, s], axis=0, keepdims=True)
-                sum_ref[r, :, s] = jnp.where(this_tracer, band, sum_ref[r, :, s])
+
+    @pl.loop(0, 4)
+    def _(r):
+        for j in tiles:
+            s = lane_slice(j)
+            inside = inside_ref[r, :, s]
+            sum_ref[r, :, s] = level_sums([adv_ref[r, t, :, s] * inside for t in range(8)])
 
     core = lax.rem(lev_ref[0], 2)
     keep_ref[...] = sum_ref[pl.ds(2 * core, 2)]
@@ -465,10 +479,6 @@
     swapped = lax.ppermute(send, "lev", swap)
     chip_sum = keep + swapped
     blocks = lev_count // 2
-    pairs = [(2 * n + c, 2 * (n ^ 1) + c) for n in range(2, blocks) for c in range(2)]
-    total = chip_sum + lax.ppermute(chip_sum, "lev", pairs)
-    adv_out, _ = lax.optimization_barrier((adv, swapped))
-    adv_other = lax.ppermute(adv_out, "lev", swap)
     lines = blocks // 2 - 1
     moved = []
     for shift in range(1, lines):
@@ -476,8 +486,11 @@
         for y in range(lines):
             for n in range(4):
                 pairs.append((4 * (y + 1) + n, 4 * ((y + shift) % lines + 1) + n))
-        moved.append(lax.ppermute(total, "lev", pairs))
-    total = sum(moved, total)
+        moved.append(lax.ppermute(chip_sum, "lev", pairs))
+    total = sum(moved, chip_sum)
+    adv_other = lax.ppermute(adv, "lev", swap)
+    pairs = [(2 * n + c, 2 * (n ^ 1) + c) for n in range(2, blocks) for c in range(2)]
+    total = total + lax.ppermute(total, "lev", pairs)
     total_other = lax.ppermute(total, "lev", swap)
 
     base = pl.pallas_call(

time: 113 us -> 116 us (1.027)
  waiting for transfers between devices: 49.4 us -> 54.2 us
    ppermute x1, waiting for transfers between devices: 0.99 us -> 3.87 us  [body(): swapped = lax.ppermute(send, 'lev', swap)]
    all_to_all x1, waiting for transfers between devices: 6.93 us -> 8.87 us  [body(): lax.all_to_all(packed, 'lat', split_axis=0, concat_axis=0, tiled=True)]
    unnamed x26 -> x24, local copies, waits for them, and re-layouts: 5.94 us -> 5.3 us
  transfers between devices with their start and end apart: 12 -> 12, of which waited for: 5 -> 5; matrix products, arithmetic and copies ran while one was open for 1% -> 0% of each run, Pallas kernels for 8% -> 7%
where the time goes in v3:
time: 116 us; the launch traced here: 115 us
  waiting for transfers between devices  54.2 us (47%)
  starting transfers between devices  37.2 us (32%)
  Pallas kernels  18 us (16%)
  local copies, waits for them, and re-layouts  5.3 us (5%)
    ppermute x1, waiting for transfers between devices, body(): south_part = lax.ppermute(to_north, 'lat', north)  26.8 us
    all_to_all x1, starting transfers between devices, body(): lax.all_to_all(forcing, 'lev', split_axis=0, concat_axis=0, tiled=True)  12.8 us
    ppermute x1, waiting for transfers between devices, body(): south_row = lax.ppermute(last_row, 'lat', north)  11.2 us
    all_to_all x1, starting transfers between devices, body(): lax.all_to_all(packed, 'lat', split_axis=0, concat_axis=0, tiled=True)  10.1 us
    all_to_all x1, waiting for transfers between devices, body(): lax.all_to_all(packed, 'lat', split_axis=0, concat_axis=0, tiled=True)  8.87 us
    unnamed x24, local copies, waits for them, and re-layouts  5.3 us
    ppermute x1, starting transfers between devices, body(): south_part = lax.ppermute(to_north, 'lat', north)  4.59 us
    ppermute x1, starting transfers between devices, body(): south_row = lax.ppermute(last_row, 'lat', north)  4.26 us
  transfers between devices with their start and end apart: 12, of which 5 were waited for; matrix products, arithmetic and copies ran while one was open for 0% of the time, Pallas kernels for 7%

profile of v3, /device:TPU:1, one launch (start us, length us, event | category | flops | bytes accessed | tf_op | source)
XLA Modules:
  0.0 115.0 jit_solution(11719340998556279297)
XLA Ops:
  0.0 0.0 copy-start.2
  0.0 4.1 %shard_map.91 = (f32[8,4,8,2048]{3,2,1,0:T(8,128)}, f32[8,8,2048]{2,1,0:T(8,128)}, f32[9,8,2048]{2,1,0:T(8,128)}, f32[5,4,8,2048]{3,2,1,0:T(8,128)}) custom-call(f32[8,512,128]{2,1,0:T(8,128)} %bitcast.30, f32[512,128]{1,0:T(8,128)} %bitcast.32, f32[512,128]{1,0:T(8,128)} %bitcast.33), custom_call_target="tpu_custom_call" | custom-call | tf_op jit(solution)/shard_map/pallas_call | solution.py:421
  4.2 1.3 %collective-permute-start.3 = (f32[9,8,2048]{2,1,0:T(8,128)}, f32[9,8,2048]{2,1,0:T(8,128)S(1)}, u32[]{:S(2)}, u32[]{:S(2)}) collective-permute-start(f32[9,8,2048]{2,1,0:T(8,128)} %get-tuple-element.19.own_face_hbm), channel_id=1, source_target_pairs={{1,0},{2,1},{3,2},{4,3},{5,4},{6,5},{7,6},{8,7},{9,8},{10,9},{11,1... | collective-permute-start | bytes 1769480 | tf_op jit(solution)/shard_map/ppermute | solution.py:438
  5.5 4.6 %collective-permute-start.1 = (f32[8,8,2048]{2,1,0:T(8,128)}, f32[8,8,2048]{2,1,0:T(8,128)S(1)}, u32[]{:S(2)}, u32[]{:S(2)}) collective-permute-start(f32[8,8,2048]{2,1,0:T(8,128)} %get-tuple-element.20), channel_id=1, source_target_pairs={{0,1},{1,2},{2,3},{3,4},{4,5},{5,6},{6,7},{7,8},{8,9},{9,10},{10,1... | collective-permute-start | bytes 1572872 | tf_op jit(solution)/shard_map/ppermute | solution.py:437
  10.1 2.4 %shard_map.92 = (f32[8,8,2048]{2,1,0:T(8,128)}, f32[8,8,2048]{2,1,0:T(8,128)}) custom-call(f32[8,512,128]{2,1,0:T(8,128)} %bitcast.31), custom_call_target="tpu_custom_call" | custom-call | tf_op jit(solution)/shard_map/pallas_call | solution.py:410
  12.5 4.3 %collective-permute-start = (f32[8,8,2048]{2,1,0:T(8,128)}, f32[8,8,2048]{2,1,0:T(8,128)S(1)}, u32[]{:S(2)}, u32[]{:S(2)}) collective-permute-start(f32[8,8,2048]{2,1,0:T(8,128)} %get-tuple-element.17.own_last_hbm), channel_id=1, source_target_pairs={{0,1},{1,2},{2,3},{3,4},{4,5},{5,6},{6,7},{7,8},{8,9},{9,10},{10,1... | collective-permute-start | bytes 1572872 | tf_op jit(solution)/shard_map/ppermute | solution.py:435
  16.7 1.3 %collective-permute-start.2 = (f32[8,8,2048]{2,1,0:T(8,128)}, f32[8,8,2048]{2,1,0:T(8,128)S(1)}, u32[]{:S(2)}, u32[]{:S(2)}) collective-permute-start(f32[8,8,2048]{2,1,0:T(8,128)} %get-tuple-element.18.own_first_hbm), channel_id=1, source_target_pairs={{1,0},{2,1},{3,2},{4,3},{5,4},{6,5},{7,6},{8,7},{9,8},{10,9},{11,1... | collective-permute-start | bytes 1572872 | tf_op jit(solution)/shard_map/ppermute | solution.py:436
  18.0 26.8 %collective-permute-done.1.south_part_ref = f32[8,8,2048]{2,1,0:T(8,128)S(1)} collective-permute-done((f32[8,8,2048]{2,1,0:T(8,128)}, f32[8,8,2048]{2,1,0:T(8,128)S(1)}, u32[]{:S(2)}, u32[]{:S(2)}) %collective-permute-start.1) | collective-permute-done | bytes 524320 | tf_op jit(solution)/shard_map/ppermute | solution.py:437
  44.8 11.2 %collective-permute-done.south_row_ref = f32[8,8,2048]{2,1,0:T(8,128)S(1)} collective-permute-done((f32[8,8,2048]{2,1,0:T(8,128)}, f32[8,8,2048]{2,1,0:T(8,128)S(1)}, u32[]{:S(2)}, u32[]{:S(2)}) %collective-permute-start) | collective-permute-done | bytes 524320 | tf_op jit(solution)/shard_map/ppermute | solution.py:435
  56.0 0.0 copy-start.3
  56.0 0.8 copy-done.3
  56.8 0.0 collective-permute-done.2.north_row_ref
  56.8 0.0 copy-start.5
  56.8 0.8 copy-done.5
  57.6 0.0 collective-permute-done.3.north_part_ref
  57.7 0.0 copy-done.2
  57.7 0.0 copy-start.4
  57.7 1.0 copy-done.4
  58.7 0.0 copy-start.6
  58.7 1.0 copy-done.6
  59.7 0.0 copy-start.9
  59.7 0.0 copy-start.10
  59.7 0.0 copy-start.11
  59.7 3.9 %shard_map.93 = (f32[4,8,8,2048]{3,2,1,0:T(8,128)S(1)}, f32[2,8,2048]{2,1,0:T(8,128)S(1)}, f32[2,8,2048]{2,1,0:T(8,128)S(1)}) custom-call(s32[1]{0:T(128)} %bitcast.lev_ref, f32[8,4,8,2048]{3,2,1,0:T(8,128)} %get-tuple-element.16.part_hbm, f32[8,8,2048]{2,1,0:T(8,128)} %get-tuple-element.17.own_last_hbm, f32[8,8,2048]{2,1,0:T(8,128)} %get-tuple-element.18.own_first_hbm, ...), custom_call_target="tpu_custom_call" | custom-call | tf_op jit(solution)/shard_map/pallas_call | solution.py:463
  63.6 0.0 copy-start
  63.6 0.0 copy-start.7
  63.6 0.0 copy-start.8
  63.7 0.6 collective-permute-start.4
  64.2 0.1 collective-permute-start.5
  64.3 3.9 %collective-permute-done.5 = f32[2,8,2048]{2,1,0:T(8,128)S(1)} collective-permute-done((f32[2,8,2048]{2,1,0:T(8,128)S(1)}, f32[2,8,2048]{2,1,0:T(8,128)S(1)}, u32[]{:S(2)}, u32[]{:S(2)}) %collective-permute-start.5) | collective-permute-done | bytes 131104 | tf_op jit(solution)/shard_map/ppermute | solution.py:479
  68.2 0.7 collective-permute-start.6
  68.9 0.7 collective-permute-start.7
  69.6 0.0 copy-done.9
  69.6 0.0 copy-done.10
  69.6 0.0 copy-done.11
  69.6 1.3 %shard_map.96 = f32[16,24,128]{2,1,0:T(8,128)} custom-call(s32[1]{0:T(128)} %bitcast.13.lat_ref, s32[16]{0:T(128)S(1)} %bitcast.29, f32[16,16,128]{2,1,0:T(8,128)S(1)} %bitcast.27, s32[16,16]{1,0:T(8,128)S(1)} %bitcast.28), custom_call_target="tpu_custom_call" | custom-call | tf_op jit(solution)/shard_map/pallas_call | solution.py:440
  70.9 10.1 %all-to-all-start = ((f32[16,24,128]{2,1,0:T(8,128)}), f32[16,24,128]{2,1,0:T(8,128)S(1)}, u32[]{:S(2)}, u32[]{:S(2)}) async-start(f32[16,24,128]{2,1,0:T(8,128)} %shard_map.96), calls=%async_computation | async-start | bytes 393216 | tf_op jit(solution)/shard_map/all_to_all | solution.py:448
  81.0 0.0 collective-permute-done.6
  81.0 0.0 collective-permute-done.7
  81.1 0.7 collective-permute-start.8
  81.8 8.9 %all-to-all-done.packed_ref = f32[16,24,128]{2,1,0:T(8,128)S(1)} async-done(((f32[16,24,128]{2,1,0:T(8,128)}), f32[16,24,128]{2,1,0:T(8,128)S(1)}, u32[]{:S(2)}, u32[]{:S(2)}) %all-to-all-start) | async-done | bytes 196640 | tf_op jit(solution)/shard_map/all_to_all | solution.py:448
  90.6 1.4 %shard_map.97 = f32[16,8,512]{2,1,0:T(8,128)} custom-call(f32[16,24,128]{2,1,0:T(8,128)S(1)} %all-to-all-done.packed_ref), custom_call_target="tpu_custom_call" | custom-call | tf_op jit(solution)/shard_map/pallas_call | solution.py:450
  92.0 12.8 %all-to-all-start.1 = ((f32[16,8,512]{2,1,0:T(8,128)}), f32[16,8,512]{2,1,0:T(8,128)S(1)}, u32[]{:S(2)}, u32[]{:S(2)}) async-start(f32[16,8,512]{2,1,0:T(8,128)} %shard_map.97), calls=%async_computation.1 | async-start | bytes 524288 | tf_op jit(solution)/shard_map/all_to_all | solution.py:453
  104.9 0.0 collective-permute-done.8
  104.9 0.2 collective-permute-start.9
  105.1 0.0 copy-done.7
  105.1 0.0 copy-done.8
  105.1 0.8 shard_map.94
  105.9 0.0 collective-permute-done.4.other_ref
  105.9 0.0 copy-done
  105.9 0.0 copy-start.1
  106.0 1.6 %copy-done.1 = f32[4,8,8,2048]{3,2,1,0:T(8,128)S(1)} copy-done((f32[4,8,8,2048]{3,2,1,0:T(8,128)S(1)}, f32[4,8,8,2048]{3,2,1,0:T(8,128)}, u32[]{:S(2)}) %copy-start.1) | copy-done | bytes 2097176
  107.5 2.5 %shard_map.95 = f32[4,64,2048]{2,1,0:T(8,128)S(1)} custom-call(s32[1]{0:T(128)} %bitcast.lev_ref, f32[4,8,8,2048]{3,2,1,0:T(8,128)S(1)} %copy-done.1, f32[4,8,8,2048]{3,2,1,0:T(8,128)} %collective-permute-done.4.other_ref, s32[2,4,2048]{2,1,0:T(4,128)S(1)} %copy-done.2, f32[4,2048]{1,0:T(4,128)S(1)} %copy-done.8, ...), custom_call_target="tpu_custom_call" | custom-call | tf_op jit(solution)/shard_map/pallas_call | solution.py:496
  110.1 3.5 %all-to-all-done.1.forcing_ref = f32[16,8,512]{2,1,0:T(8,128)S(1)} async-done(((f32[16,8,512]{2,1,0:T(8,128)}), f32[16,8,512]{2,1,0:T(8,128)S(1)}, u32[]{:S(2)}, u32[]{:S(2)}) %all-to-all-start.1) | async-done | bytes 262176 | tf_op jit(solution)/shard_map/all_to_all | solution.py:453
  113.5 0.0 collective-permute-done.9.other_ref
  113.6 1.5 %shard_map.98 = f32[8,512,128]{2,1,0:T(8,128)} custom-call(s32[1]{0:T(128)} %bitcast.lev_ref, f32[4,8,8,2048]{3,2,1,0:T(8,128)S(1)} %bitcast.26, f32[4,8,2048]{2,1,0:T(8,128)S(1)} %get-tuple-element.24.gain_ref, f32[2,8,2048]{2,1,0:T(8,128)S(1)} %add.15.own_ref, f32[2,8,2048]{2,1,0:T(8,128)S(1)} %collective-permute-done.9.other_ref, ...), custom_call_target="tpu_custom_call" | custom-call | tf_op jit(solution)/shard_map/pallas_call | solution.py:504
  (3 shorter events, 0.1 us)
Async XLA Ops:
  0.0 57.7 %copy-start.2 = (s32[2,4,2048]{2,1,0:T(4,128)S(1)}, s32[2,4,2048]{2,1,0:T(4,128)}, u32[]{:S(2)}) copy-start(s32[2,4,2048]{2,1,0:T(4,128)} %band_ref.5) | copy-start | bytes 196612
  4.2 53.5 %collective-permute-start.3 = (f32[9,8,2048]{2,1,0:T(8,128)}, f32[9,8,2048]{2,1,0:T(8,128)S(1)}, u32[]{:S(2)}, u32[]{:S(2)}) collective-permute-start(f32[9,8,2048]{2,1,0:T(8,128)} %get-tuple-element.19.own_face_hbm), channel_id=1, source_target_pairs={{1,0},{2,1},{3,2},{4,3},{5,4},{6,5},{7,6},{8,7},{9,8},{10,9},{11,1... | collective-permute-start | bytes 1769480 | tf_op jit(solution)/shard_map/ppermute | solution.py:438
  5.5 39.4 %collective-permute-start.1 = (f32[8,8,2048]{2,1,0:T(8,128)}, f32[8,8,2048]{2,1,0:T(8,128)S(1)}, u32[]{:S(2)}, u32[]{:S(2)}) collective-permute-start(f32[8,8,2048]{2,1,0:T(8,128)} %get-tuple-element.20), channel_id=1, source_target_pairs={{0,1},{1,2},{2,3},{3,4},{4,5},{5,6},{6,7},{7,8},{8,9},{9,10},{10,1... | collective-permute-start | bytes 1572872 | tf_op jit(solution)/shard_map/ppermute | solution.py:437
  12.5 43.6 %collective-permute-start = (f32[8,8,2048]{2,1,0:T(8,128)}, f32[8,8,2048]{2,1,0:T(8,128)S(1)}, u32[]{:S(2)}, u32[]{:S(2)}) collective-permute-start(f32[8,8,2048]{2,1,0:T(8,128)} %get-tuple-element.17.own_last_hbm), channel_id=1, source_target_pairs={{0,1},{1,2},{2,3},{3,4},{4,5},{5,6},{6,7},{7,8},{8,9},{9,10},{10,1... | collective-permute-start | bytes 1572872 | tf_op jit(solution)/shard_map/ppermute | solution.py:435
  16.7 40.1 %collective-permute-start.2 = (f32[8,8,2048]{2,1,0:T(8,128)}, f32[8,8,2048]{2,1,0:T(8,128)S(1)}, u32[]{:S(2)}, u32[]{:S(2)}) collective-permute-start(f32[8,8,2048]{2,1,0:T(8,128)} %get-tuple-element.18.own_first_hbm), channel_id=1, source_target_pairs={{1,0},{2,1},{3,2},{4,3},{5,4},{6,5},{7,6},{8,7},{9,8},{10,9},{11,1... | collective-permute-start | bytes 1572872 | tf_op jit(solution)/shard_map/ppermute | solution.py:436
  56.0 0.8 copy-start.3
  56.8 0.8 copy-start.5
  57.7 1.0 copy-start.4
  58.7 1.0 copy-start.6
  59.7 9.9 %copy-start.9 = (f32[1,1,16,16,128]{4,3,2,1,0:T(8,128)S(1)}, f32[1,1,16,16,128]{4,3,2,1,0:T(8,128)}, u32[]{:S(2)}) copy-start(f32[1,1,16,16,128]{4,3,2,1,0:T(8,128)} %param.15) | copy-start | bytes 393220
  59.7 9.9 %copy-start.10 = (s32[1,1,16,16]{3,2,1,0:T(8,128)S(1)}, s32[1,1,16,16]{3,2,1,0:T(8,128)}, u32[]{:S(2)}) copy-start(s32[1,1,16,16]{3,2,1,0:T(8,128)} %param.16) | copy-start | bytes 3076
  59.7 9.9 %copy-start.11 = (s32[1,1,16]{2,1,0:T(1,128)S(1)}, s32[1,1,16]{2,1,0:T(1,128)}, u32[]{:S(2)}) copy-start(s32[1,1,16]{2,1,0:T(1,128)} %param.17) | copy-start | bytes 196
  63.6 42.3 %copy-start = (f32[4,8,8,2048]{3,2,1,0:T(8,128)}, f32[4,8,8,2048]{3,2,1,0:T(8,128)S(1)}, u32[]{:S(2)}) copy-start(f32[4,8,8,2048]{3,2,1,0:T(8,128)S(1)} %get-tuple-element.22.adv_ref) | copy-start | bytes 6291460
  63.6 41.4 %copy-start.7 = (f32[4,8,16,16]{3,2,1,0:T(8,128)S(1)}, f32[4,8,16,16]{3,2,1,0:T(8,128)}, u32[]{:S(2)}) copy-start(f32[4,8,16,16]{3,2,1,0:T(8,128)} %inv_ref.1) | copy-start | bytes 98308
  63.6 41.4 %copy-start.8 = (f32[4,2048]{1,0:T(4,128)S(1)}, f32[4,2048]{1,0:T(4,128)}, u32[]{:S(2)}) copy-start(f32[4,2048]{1,0:T(4,128)} %flux_ref.3) | copy-start | bytes 98308
  63.7 42.3 %collective-permute-start.4 = (f32[4,8,8,2048]{3,2,1,0:T(8,128)S(1)}, f32[4,8,8,2048]{3,2,1,0:T(8,128)}, u32[]{:S(2)}, u32[]{:S(2)}) collective-permute-start(f32[4,8,8,2048]{3,2,1,0:T(8,128)S(1)} %get-tuple-element.22.adv_ref), channel_id=1, source_target_pairs={{0,16},{16,0},{32,48},{48,32},{64,80},{80,64},{96,112},{112,96},{1... | collective-permute-start | bytes 6291464 | tf_op jit(solution)/shard_map/ppermute | solution.py:491
  64.2 4.0 %collective-permute-start.5 = (f32[2,8,2048]{2,1,0:T(8,128)S(1)}, f32[2,8,2048]{2,1,0:T(8,128)S(1)}, u32[]{:S(2)}, u32[]{:S(2)}) collective-permute-start(f32[2,8,2048]{2,1,0:T(8,128)S(1)} %get-tuple-element.26), channel_id=1, source_target_pairs={{0,16},{16,0},{32,48},{48,32},{64,80},{80,64},{96,112},{112,96},{1... | collective-permute-start | bytes 393224 | tf_op jit(solution)/shard_map/ppermute | solution.py:479
  68.2 12.8 %collective-permute-start.6 = (f32[2,8,2048]{2,1,0:T(8,128)S(1)}, f32[2,8,2048]{2,1,0:T(8,128)S(1)}, u32[]{:S(2)}, u32[]{:S(2)}) collective-permute-start(f32[2,8,2048]{2,1,0:T(8,128)S(1)} %add.12), channel_id=1, source_target_pairs={{64,128},{80,144},{96,160},{112,176},{128,192},{144,208},{160,224}... | collective-permute-start | bytes 393224 | tf_op jit(solution)/shard_map/ppermute | solution.py:489
  68.9 12.1 %collective-permute-start.7 = (f32[2,8,2048]{2,1,0:T(8,128)S(1)}, f32[2,8,2048]{2,1,0:T(8,128)S(1)}, u32[]{:S(2)}, u32[]{:S(2)}) collective-permute-start(f32[2,8,2048]{2,1,0:T(8,128)S(1)} %add.12), channel_id=1, source_target_pairs={{64,192},{80,208},{96,224},{112,240},{128,64},{144,80},{160,96},{1... | collective-permute-start | bytes 393224 | tf_op jit(solution)/shard_map/ppermute | solution.py:489
  70.9 19.7 %all-to-all-start = ((f32[16,24,128]{2,1,0:T(8,128)}), f32[16,24,128]{2,1,0:T(8,128)S(1)}, u32[]{:S(2)}, u32[]{:S(2)}) async-start(f32[16,24,128]{2,1,0:T(8,128)} %shard_map.96), calls=%async_computation | async-start | bytes 393216 | tf_op jit(solution)/shard_map/all_to_all | solution.py:448
  81.1 23.8 %collective-permute-start.8 = (f32[2,8,2048]{2,1,0:T(8,128)S(1)}, f32[2,8,2048]{2,1,0:T(8,128)S(1)}, u32[]{:S(2)}, u32[]{:S(2)}) collective-permute-start(f32[2,8,2048]{2,1,0:T(8,128)S(1)} %add_add_fusion), channel_id=1, source_target_pairs={{64,96},{80,112},{96,64},{112,80},{128,160},{144,176},{160,128},{1... | collective-permute-start | bytes 393224 | tf_op jit(solution)/shard_map/ppermute | solution.py:493
  92.0 21.5 %all-to-all-start.1 = ((f32[16,8,512]{2,1,0:T(8,128)}), f32[16,8,512]{2,1,0:T(8,128)S(1)}, u32[]{:S(2)}, u32[]{:S(2)}) async-start(f32[16,8,512]{2,1,0:T(8,128)} %shard_map.97), calls=%async_computation.1 | async-start | bytes 524288 | tf_op jit(solution)/shard_map/all_to_all | solution.py:453
  104.9 8.7 %collective-permute-start.9 = (f32[2,8,2048]{2,1,0:T(8,128)S(1)}, f32[2,8,2048]{2,1,0:T(8,128)S(1)}, u32[]{:S(2)}, u32[]{:S(2)}) collective-permute-start(f32[2,8,2048]{2,1,0:T(8,128)S(1)} %add.15.own_ref), channel_id=1, source_target_pairs={{0,16},{16,0},{32,48},{48,32},{64,80},{80,64},{96,112},{112,96},{1... | collective-permute-start | bytes 393224 | tf_op jit(solution)/shard_map/ppermute | solution.py:494
  105.9 1.6 %copy-start.1 = (f32[4,8,8,2048]{3,2,1,0:T(8,128)S(1)}, f32[4,8,8,2048]{3,2,1,0:T(8,128)}, u32[]{:S(2)}) copy-start(f32[4,8,8,2048]{3,2,1,0:T(8,128)} %copy-done) | copy-start | bytes 6291460

commit v4 on v3

--- a/solution.py
+++ b/solution.py
@@ -93,7 +93,7 @@
             coef_ref[4, r, :, s] = center
 
 
-def edge_kernel(a_hbm, last_hbm, first_hbm, a_ref, last_ref, first_ref, sems):
+def edge_kernel(a_hbm, v_hbm, last_hbm, first_hbm, a_ref, v_ref, last_ref, first_ref, sems):
     def incoming(t):
         return pltpu.make_async_copy(a_hbm.at[t], a_ref.at[t], sems.at[t, 0])
 
@@ -103,9 +103,20 @@
             pltpu.make_async_copy(first_ref.at[t], first_hbm.at[t], sems.at[t, 2]),
         ]
 
+    faces_in = pltpu.make_async_copy(v_hbm, v_ref, sems.at[8, 0])
+    faces_out = pltpu.make_async_copy(first_ref.at[8], first_hbm.at[8], sems.at[8, 1])
+    faces_in.start()
+
     @pl.loop(0, 8)
     def _(t):
         incoming(t).start()
+
+    faces_in.wait()
+    for k in range(8):
+        tiles = swap_axes8([v_ref[pl.ds(level * 64 + k * 8, 8), :] for level in range(8)])
+        for half in range(2):
+            first_ref[8, :, lane_slice(2 * k + half)] = tiles[4 * half]
+    faces_out.start()
 
     @pl.loop(0, 8)
     def _(t):
@@ -122,6 +133,8 @@
     def _(t):
         for copy in outgoing(t):
             copy.wait()
+
+    faces_out.wait()
 
 
 def prep_kernel(
@@ -153,9 +166,7 @@
         copy.wait()
     flow_coefficients(u_ref, v_ref, rows_ref, v_rows, coef_ref)
     coef_copy = pltpu.make_async_copy(coef_ref, coef_hbm, sems.at[8, 0])
-    face_copy = pltpu.make_async_copy(v_rows.at[0], south_hbm.at[8], sems.at[8, 1])
     coef_copy.start()
-    face_copy.start()
 
     @pl.loop(0, 8)
     def _(t):
@@ -182,88 +193,128 @@
             copy.wait()
 
     coef_copy.wait()
-    face_copy.wait()
-
-
-def advect_kernel(
-    lev_ref, part_hbm, own_last_hbm, own_first_hbm, own_face_hbm, south_row_ref, south_part_ref, north_row_ref, north_part_ref,
-    coef_hbm, band_ref, adv_ref, keep_ref, send_ref,
-    edge_ref, sum_ref, inside_ref, part_ref, own_last_ref, own_first_ref, coef_ref, sems,
+
+
+def inside_band(lev_ref, band_ref, r):
+    level = lax.broadcasted_iota(jnp.int32, (8, 2048), 0) + lev_ref[0] * 8
+    first = band_ref[0, r : r + 1, :]
+    last = band_ref[1, r : r + 1, :]
+    return jnp.where((level >= first) & (level < last), 1.0, 0.0).astype(F32)
+
+
+def mid_kernel(
+    lev_ref, part_hbm, own_last_hbm, south_row_ref, north_row_ref, coef_hbm, band_ref,
+    mid_hbm, edge_hbm, flow_hbm, sum_out_ref,
+    part_ref, own_last_ref, coef_ref, flow_ref, center_ref, inside_ref, mid_ref, edge_ref, sems,
 ):
     tiles = range(16)
 
-    def copies(t):
+    def incoming(t):
         return [
             pltpu.make_async_copy(part_hbm.at[t], part_ref.at[t], sems.at[t, 0]),
             pltpu.make_async_copy(own_last_hbm.at[t], own_last_ref.at[t], sems.at[t, 1]),
-            pltpu.make_async_copy(own_first_hbm.at[t], own_first_ref.at[t], sems.at[t, 2]),
         ]
 
-    fixed = [
-        pltpu.make_async_copy(coef_hbm, coef_ref, sems.at[8, 0]),
-        pltpu.make_async_copy(own_face_hbm.at[8], own_first_ref.at[8], sems.at[8, 1]),
-    ]
-    for copy in fixed:
-        copy.start()
-
-    @pl.loop(0, 8)
-    def _(t):
-        for copy in copies(t):
+    def outgoing(t):
+        return [
+            pltpu.make_async_copy(mid_ref.at[:, t], mid_hbm.at[:, t], sems.at[t, 2]),
+            pltpu.make_async_copy(edge_ref.at[:, t], edge_hbm.at[:, t], sems.at[t, 3]),
+        ]
+
+    coef_copy = pltpu.make_async_copy(coef_hbm, coef_ref, sems.at[8, 0])
+    flow_copy = pltpu.make_async_copy(flow_ref, flow_hbm, sems.at[8, 1])
+    coef_copy.start()
+
+    @pl.loop(0, 8)
+    def _(t):
+        for copy in incoming(t):
             copy.start()
 
-    level = lax.broadcasted_iota(jnp.int32, (8, 2048), 0) + lev_ref[0] * 8
-    for r in range(4):
-        first = band_ref[0, r : r + 1, :]
-        last = band_ref[1, r : r + 1, :]
-        inside_ref[r] = jnp.where((level >= first) & (level < last), 1.0, 0.0).astype(F32)
-
-    for copy in fixed:
-        copy.wait()
-    north_face = jnp.maximum(north_part_ref[8], 0.0)
-    edge_ref[0] = jnp.maximum(own_first_ref[8], 0.0)
-    edge_ref[1] = jnp.minimum(north_part_ref[8], 0.0)
-    edge_ref[2] = north_face
-    edge_ref[3] = coef_ref[4, 3] - north_face
-
-    @pl.loop(0, 8)
-    def _(t):
-        for copy in copies(t):
+    for q in range(2):
+        inside_ref[q] = inside_band(lev_ref, band_ref, q + 1)
+    coef_copy.wait()
+    north = jnp.maximum(north_row_ref[8], 0.0)
+    flow_ref[0] = coef_ref[3, 0]
+    flow_ref[1] = north
+    center_ref[...] = coef_ref[4, 3] - north
+    flow_copy.start()
+
+    @pl.loop(0, 8)
+    def _(t):
+        for copy in incoming(t):
             copy.wait()
-        rows = [[] for _ in range(6)]
+        rows = [[] for _ in range(4)]
         for j in tiles:
             s = lane_slice(j)
-            a_south = south_row_ref[t, :, s]
-            a_last = own_last_ref[t, :, s]
-            a_first = own_first_ref[t, :, s]
-            rows[0].append(south_part_ref[t, :, s] + edge_ref[0, :, s] * (a_first - a_south))
-            rows[1].append(part_ref[t, 0, :, s] - coef_ref[3, 0, :, s] * a_south)
-            rows[2].append(part_ref[t, 1, :, s])
-            rows[3].append(part_ref[t, 2, :, s])
-            rows[4].append(part_ref[t, 3, :, s] + edge_ref[2, :, s] * (north_row_ref[t, :, s] - a_last))
-            rows[5].append(north_part_ref[t, :, s] - edge_ref[1, :, s] * a_last)
+            rows[0].append(part_ref[t, 0, :, s] - flow_ref[0, :, s] * south_row_ref[t, :, s])
+            rows[1].append(part_ref[t, 1, :, s])
+            rows[2].append(part_ref[t, 2, :, s])
+            gap = north_row_ref[t, :, s] - own_last_ref[t, :, s]
+            rows[3].append(part_ref[t, 3, :, s] + flow_ref[1, :, s] * gap)
         for r in range(4):
-            x = rows[r + 1]
+            x = rows[r]
             e = east_tiles(x)
             w = west_tiles(x)
             for j in tiles:
                 s = lane_slice(j)
-                center = coef_ref[4, r, :, s] if r < 3 else edge_ref[3, :, s]
-                north = coef_ref[2, r, :, s] if r < 3 else edge_ref[2, :, s]
-                out = (
-                    x[j] * center
-                    + e[j] * coef_ref[0, r, :, s]
-                    - w[j] * coef_ref[1, r, :, s]
-                    + rows[r + 2][j] * north
-                    - rows[r][j] * coef_ref[3, r, :, s]
-                )
-                adv_ref[r, t, :, s] = out
-
-    @pl.loop(0, 4)
-    def _(r):
+                center = coef_ref[4, r, :, s] if r < 3 else center_ref[:, s]
+                out = x[j] * center + e[j] * coef_ref[0, r, :, s] - w[j] * coef_ref[1, r, :, s]
+                if r < 3:
+                    out = out + rows[r + 1][j] * coef_ref[2, r, :, s]
+                if r > 0:
+                    out = out - rows[r - 1][j] * coef_ref[3, r, :, s]
+                if r in (1, 2):
+                    mid_ref[r - 1, t, :, s] = out
+                else:
+                    edge_ref[r // 3, t, :, s] = out
+        for copy in outgoing(t):
+            copy.start()
+
+    for q in range(2):
         for j in tiles:
             s = lane_slice(j)
-            inside = inside_ref[r, :, s]
-            sum_ref[r, :, s] = level_sums([adv_ref[r, t, :, s] * inside for t in range(8)])
+            inside = inside_ref[q, :, s]
+            sum_out_ref[q, :, s] = level_sums([mid_ref[q, t, :, s] * inside for t in range(8)])
+
+    @pl.loop(0, 8)
+    def _(t):
+        for copy in outgoing(t):
+            copy.wait()
+
+    flow_copy.wait()
+
+
+def close_kernel(
+    lev_ref, edge_hbm, flow_hbm, south_part_ref, north_part_ref, sum_mid_ref, band_ref, adv_ref, keep_ref, send_ref,
+    edge_ref, flow_ref, inside_ref, sum_ref, sems,
+):
+    def incoming(t):
+        return pltpu.make_async_copy(edge_hbm.at[:, t], edge_ref.at[:, t], sems.at[t])
+
+    flow_copy = pltpu.make_async_copy(flow_hbm, flow_ref, sems.at[8])
+    flow_copy.start()
+
+    @pl.loop(0, 8)
+    def _(t):
+        incoming(t).start()
+
+    for q in range(2):
+        inside_ref[q] = inside_band(lev_ref, band_ref, 3 * q)
+    sum_ref[1] = sum_mid_ref[0]
+    sum_ref[2] = sum_mid_ref[1]
+    flow_copy.wait()
+
+    @pl.loop(0, 8)
+    def _(t):
+        incoming(t).wait()
+        adv_ref[0, t] = edge_ref[0, t] - flow_ref[0] * south_part_ref[t]
+        adv_ref[1, t] = edge_ref[1, t] + flow_ref[1] * north_part_ref[t]
+
+    for q in range(2):
+        for j in range(16):
+            s = lane_slice(j)
+            inside = inside_ref[q, :, s]
+            sum_ref[3 * q, :, s] = level_sums([adv_ref[q, t, :, s] * inside for t in range(8)])
 
     core = lax.rem(lev_ref[0], 2)
     keep_ref[...] = sum_ref[pl.ds(2 * core, 2)]
@@ -307,12 +358,12 @@
         matrix_ref[r, 64:128, 128:256] = jnp.zeros_like(low)
 
 
-def diffuse_kernel(lev_ref, adv_ref, other_ref, band_ref, flux_ref, matrix_ref, out_ref):
+def diffuse_rows(rows, lev_ref, adv_ref, other_ref, band_ref, flux_ref, matrix_ref, out_ref, ready):
     lev = lev_ref[0]
     level = lax.broadcasted_iota(jnp.int32, (8, 2048), 0)
     own_level = level + lev * 8
     other_level = level + (lev + 1 - 2 * lax.rem(lev, 2)) * 8
-    for r in range(4):
+    for q, r in enumerate(rows):
         first = band_ref[0, r : r + 1, :]
         last = band_ref[1, r : r + 1, :]
         flux = flux_ref[r : r + 1, :]
@@ -321,14 +372,52 @@
             kept = 1.0 - jnp.where((levels >= first) & (levels < last), flux, 0.0)
             return halves_of((values * kept[None]).reshape(64, 2048))
 
-        own_high, own_low = rest(adv_ref[r], own_level)
-        other_high, other_low = rest(other_ref[r], other_level)
+        ready(q)
+        own_high, own_low = rest(adv_ref[q], own_level)
+        other_high, other_low = rest(other_ref[q], other_level)
         stacked = jnp.concatenate([own_high, other_high, own_low, other_low], axis=0)
         both = lax.dot(matrix_ref[r], stacked, preferred_element_type=F32)
-        out_ref[r] = both[:64] + both[64:]
-
-
-def finish_kernel(lev_ref, base_ref, gain_ref, own_ref, other_ref, forcing_ref, out_ref, sum_ref, done_ref, sems):
+        out_ref[q] = (both[:64] + both[64:]).reshape(8, 8, 2048)
+
+
+def diffuse_mid_kernel(
+    lev_ref, adv_hbm, other_hbm, band_ref, flux_ref, matrix_ref, out_hbm, adv_ref, other_ref, out_ref, sems
+):
+    copies = [
+        [
+            pltpu.make_async_copy(adv_hbm.at[q], adv_ref.at[q], sems.at[q, 0]),
+            pltpu.make_async_copy(other_hbm.at[q], other_ref.at[q], sems.at[q, 1]),
+        ]
+        for q in range(2)
+    ]
+    for pair in copies:
+        for copy in pair:
+            copy.start()
+
+    def ready(q):
+        for copy in copies[q]:
+            copy.wait()
+
+    diffuse_rows((1, 2), lev_ref, adv_ref, other_ref, band_ref, flux_ref, matrix_ref, out_ref, ready)
+    result = pltpu.make_async_copy(out_ref, out_hbm, sems.at[2, 0])
+    result.start()
+    result.wait()
+
+
+def diffuse_edge_kernel(lev_ref, adv_ref, other_ref, band_ref, flux_ref, matrix_ref, out_ref):
+    diffuse_rows((0, 3), lev_ref, adv_ref, other_ref, band_ref, flux_ref, matrix_ref, out_ref, lambda q: None)
+
+
+def finish_kernel(
+    lev_ref, mid_hbm, edge_ref, gain_ref, own_ref, other_ref, forcing_ref, out_ref, sum_ref, done_ref, mid_ref, sems, mid_sems
+):
+    def incoming(t):
+        return pltpu.make_async_copy(mid_hbm.at[:, t], mid_ref.at[:, t], mid_sems.at[t])
+
+    @pl.loop(0, 8)
+    def _(t):
+        incoming(t).start()
+
     core = lax.rem(lev_ref[0], 2)
     for q in range(2):
         for j in range(16):
@@ -337,6 +426,7 @@
 
     @pl.loop(0, 8)
     def _(t):
+        incoming(t).wait()
         for k in range(8):
             tiles = []
             for j in (2 * k, 2 * k + 1):
@@ -344,7 +434,8 @@
                 for r in range(4):
                     total = sum_ref[r, j, pl.ds(t, 8, stride=0), :]
                     forcing = forcing_ref[4 * r + j // 4, :, lane_slice(j % 4)]
-                    tiles.append(base_ref[r, t, :, s] + gain_ref[r, :, s] * total + forcing)
+                    base = mid_ref[r - 1, t, :, s] if r in (1, 2) else edge_ref[r // 3, t, :, s]
+                    tiles.append(base + gain_ref[r, :, s] * total + forcing)
             tiles = swap_axes8(tiles)
             for level in range(8):
                 done_ref[t, pl.ds(level * 64 + k * 8, 8), :] = tiles[level]
@@ -409,20 +500,20 @@
 
     last_row, first_row = pl.pallas_call(
         edge_kernel,
-        in_specs=[hbm],
+        in_specs=[hbm] * 2,
         out_specs=[hbm] * 2,
-        out_shape=[far(8, 8, lons), far(8, 8, lons)],
+        out_shape=[far(8, 8, lons), far(9, 8, lons)],
         scratch_shapes=[
-            pltpu.VMEM((8, 512, LANES), F32), pltpu.VMEM((8, 8, lons), F32), pltpu.VMEM((8, 8, lons), F32),
-            pltpu.SemaphoreType.DMA((8, 3)),
+            pltpu.VMEM((8, 512, LANES), F32), pltpu.VMEM((512, LANES), F32), pltpu.VMEM((8, 8, lons), F32),
+            pltpu.VMEM((9, 8, lons), F32), pltpu.SemaphoreType.DMA((9, 3)),
         ],
         compiler_params=small,
-    )(keep_far(a_view))
+    )(keep_far(a_view), keep_far(v_view))
     part, to_north, to_south, coef = pl.pallas_call(
         prep_kernel,
         in_specs=[hbm] * 3,
         out_specs=[hbm] * 4,
-        out_shape=[far(8, 4, 8, lons), far(8, 8, lons), far(9, 8, lons), far(5, 4, 8, lons)],
+        out_shape=[far(8, 4, 8, lons), far(8, 8, lons), far(8, 8, lons), far(5, 4, 8, lons)],
         scratch_shapes=[
             pltpu.VMEM((8, 512, LANES), F32), pltpu.VMEM((512, LANES), F32), pltpu.VMEM((512, LANES), F32),
             row_scratch, row_scratch, pltpu.VMEM((8, 4, 8, lons), F32), pltpu.VMEM((5, 4, 8, lons), F32),
@@ -460,22 +551,39 @@
         compiler_params=small,
     )(lev, conv_band, mass_flux, diff_inverse)
 
+    two_rows = pltpu.VMEM((2, 8, 8, lons), F32)
+    one_row = pltpu.VMEM((2, 8, lons), F32)
+    swap = [(i, i ^ 1) for i in range(lev_count)]
+    mid, edge, flow, sum_mid = pl.pallas_call(
+        mid_kernel,
+        in_specs=[smem] + [hbm] * 2 + [vmem] * 2 + [hbm, vmem],
+        out_specs=[hbm] * 3 + [vmem],
+        out_shape=[far(2, 8, 8, lons), far(2, 8, 8, lons), far(2, 8, lons), shape(2, 8, lons)],
+        scratch_shapes=[
+            pltpu.VMEM((8, 4, 8, lons), F32), pltpu.VMEM((8, 8, lons), F32), pltpu.VMEM((5, 4, 8, lons), F32),
+            one_row, pltpu.VMEM((8, lons), F32), one_row, two_rows, two_rows, pltpu.SemaphoreType.DMA((9, 4)),
+        ],
+        compiler_params=small,
+    )(lev, keep_far(part), keep_far(last_row), south_row, north_row, keep_far(coef), conv_band)
+    mid_other = lax.ppermute(mid, "lev", swap)
+    base_mid = pl.pallas_call(
+        diffuse_mid_kernel,
+        in_specs=[smem] + [hbm] * 2 + [vmem] * 3,
+        out_specs=hbm,
+        out_shape=far(2, 8, 8, lons),
+        scratch_shapes=[two_rows] * 3 + [pltpu.SemaphoreType.DMA((3, 2))],
+        compiler_params=small,
+    )(lev, keep_far(mid), mid_other, conv_band, mass_flux, matrix)
+
     adv, keep, send = pl.pallas_call(
-        advect_kernel,
-        in_specs=[smem] + [hbm] * 4 + [vmem] * 4 + [hbm, vmem],
+        close_kernel,
+        in_specs=[smem] + [hbm] * 2 + [vmem] * 4,
         out_specs=[vmem] * 3,
-        out_shape=[shape(4, 8, 8, lons), shape(2, 8, lons), shape(2, 8, lons)],
-        scratch_shapes=[
-            row_scratch, row_scratch, row_scratch, pltpu.VMEM((8, 4, 8, lons), F32), pltpu.VMEM((8, 8, lons), F32),
-            pltpu.VMEM((9, 8, lons), F32), pltpu.VMEM((5, 4, 8, lons), F32), pltpu.SemaphoreType.DMA((9, 3)),
-        ],
-        compiler_params=small,
-    )(
-        lev, keep_far(part), keep_far(last_row), keep_far(first_row), keep_far(to_south),
-        south_row, south_part, north_row, north_part, keep_far(coef), conv_band,
-    )
-
-    swap = [(i, i ^ 1) for i in range(lev_count)]
+        out_shape=[shape(2, 8, 8, lons), shape(2, 8, lons), shape(2, 8, lons)],
+        scratch_shapes=[two_rows, one_row, one_row, row_scratch, pltpu.SemaphoreType.DMA((9,))],
+        compiler_params=small,
+    )(lev, keep_far(edge), keep_far(flow), south_part, north_part, sum_mid, conv_band)
+
     swapped = lax.ppermute(send, "lev", swap)
     chip_sum = keep + swapped
     blocks = lev_count // 2
@@ -493,24 +601,25 @@
     total = total + lax.ppermute(total, "lev", pairs)
     total_other = lax.ppermute(total, "lev", swap)
 
-    base = pl.pallas_call(
-        diffuse_kernel,
+    base_edge = pl.pallas_call(
+        diffuse_edge_kernel,
         in_specs=[smem] + [vmem] * 5,
         out_specs=vmem,
-        out_shape=shape(4, 64, lons),
+        out_shape=shape(2, 8, 8, lons),
         compiler_params=small,
     )(lev, adv, adv_other, conv_band, mass_flux, matrix)
 
     out = pl.pallas_call(
         finish_kernel,
-        in_specs=[smem] + [vmem] * 5,
+        in_specs=[smem, hbm] + [vmem] * 5,
         out_specs=hbm,
         out_shape=shape(tracers, 512, LANES),
         scratch_shapes=[
-            pltpu.VMEM((4, 16, 8, LANES), F32), pltpu.VMEM((8, 512, LANES), F32), pltpu.SemaphoreType.DMA((8,))
+            pltpu.VMEM((4, 16, 8, LANES), F32), pltpu.VMEM((8, 512, LANES), F32), two_rows,
+            pltpu.SemaphoreType.DMA((8,)), pltpu.SemaphoreType.DMA((8,)),
         ],
         compiler_params=small,
-    )(lev, base.reshape(4, 8, 8, lons), gain, total, total_other, forcing)
+    )(lev, keep_far(base_mid), base_edge, gain, total, total_other, forcing)
     return join_rows(out.reshape(tracers, levels, 64, LANES), rows, lons)
 
 

time: 116 us -> 112 us (0.966)
  waiting for transfers between devices: 54.2 us -> 42.3 us
  Pallas kernels: 18 us -> 22 us
  other arithmetic: 0.06 us -> 3.99 us
    ppermute x1, waiting for transfers between devices: 26.8 us -> 7.14 us  [body(): south_part = lax.ppermute(to_north, 'lat', north)]
    ppermute x1, waiting for transfers between devices: 11.2 us -> 25.1 us  [body(): south_row = lax.ppermute(last_row, 'lat', north)]
    pallas_call x4 -> x6, Pallas kernels: 10.3 us -> 15 us  [the longest x1 4.04 us: body(): pl.pallas_call(mid_kernel, in_specs=[smem] + [hbm] * 2 + [vmem] * 2 + [hb...]
    all_to_all x1, waiting for transfers between devices: 3.46 us -> 0.01 us  [body(): lax.all_to_all(forcing, 'lev', split_axis=0, concat_axis=0, tiled=True)]
    all_to_all x1, waiting for transfers between devices: 8.87 us -> 6.57 us  [body(): lax.all_to_all(packed, 'lat', split_axis=0, concat_axis=0, tiled=True)]
    add x1, other arithmetic: 0.02 us -> 1.7 us  [body(): total = sum(moved, chip_sum)]
    add x1, other arithmetic: 0.02 us -> 1.63 us  [body(): total = total + lax.ppermute(total, 'lev', pairs)]
    ppermute x2, starting transfers between devices: 1.34 us -> 2.61 us  [body(): moved.append(lax.ppermute(chip_sum, 'lev', pairs))]
  transfers between devices with their start and end apart: 12 -> 13, of which waited for: 5 -> 4; matrix products, arithmetic and copies ran while one was open for 0% -> 4% of each run, Pallas kernels for 7% -> 13%
where the time goes in v4:
time: 112 us; the launch traced here: 111 us
  waiting for transfers between devices  42.3 us (38%)
  starting transfers between devices  38.2 us (34%)
  Pallas kernels  22 us (20%)
  local copies, waits for them, and re-layouts  4.55 us (4%)
  other arithmetic  3.99 us (4%)
    ppermute x1, waiting for transfers between devices, body(): south_row = lax.ppermute(last_row, 'lat', north)  25.1 us
    all_to_all x1, starting transfers between devices, body(): lax.all_to_all(forcing, 'lev', split_axis=0, concat_axis=0, tiled=True)  11.6 us
    all_to_all x1, starting transfers between devices, body(): lax.all_to_all(packed, 'lat', split_axis=0, concat_axis=0, tiled=True)  10.1 us
    ppermute x1, waiting for transfers between devices, body(): south_part = lax.ppermute(to_north, 'lat', north)  7.14 us
    all_to_all x1, waiting for transfers between devices, body(): lax.all_to_all(packed, 'lat', split_axis=0, concat_axis=0, tiled=True)  6.57 us
    ppermute x1, starting transfers between devices, body(): south_row = lax.ppermute(last_row, 'lat', north)  4.59 us
    unnamed x22, local copies, waits for them, and re-layouts  4.55 us
    ppermute x1, starting transfers between devices, body(): south_part = lax.ppermute(to_north, 'lat', north)  4.26 us
  transfers between devices with their start and end apart: 13, of which 4 were waited for; matrix products, arithmetic and copies ran while one was open for 4% of the time, Pallas kernels for 13%

profile of v4, /device:TPU:1, one launch (start us, length us, event | category | flops | bytes accessed | tf_op | source)
XLA Modules:
  0.0 111.3 jit_solution(16392085648806395010)
XLA Ops:
  0.0 0.0 copy-start
  0.0 2.6 %shard_map.92 = (f32[8,8,2048]{2,1,0:T(8,128)}, f32[9,8,2048]{2,1,0:T(8,128)}) custom-call(f32[8,512,128]{2,1,0:T(8,128)} %bitcast.28, f32[512,128]{1,0:T(8,128)} %bitcast.30), custom_call_target="tpu_custom_call" | custom-call | tf_op jit(solution)/shard_map/pallas_call | solution.py:501
  2.6 1.3 %collective-permute-start.1 = (f32[9,8,2048]{2,1,0:T(8,128)}, f32[9,8,2048]{2,1,0:T(8,128)S(1)}, u32[]{:S(2)}, u32[]{:S(2)}) collective-permute-start(f32[9,8,2048]{2,1,0:T(8,128)} %get-tuple-element.22), channel_id=1, source_target_pairs={{1,0},{2,1},{3,2},{4,3},{5,4},{6,5},{7,6},{8,7},{9,8},{10,9},{11,1... | collective-permute-start | bytes 1769480 | tf_op jit(solution)/shard_map/ppermute | solution.py:527
  3.9 4.6 %collective-permute-start = (f32[8,8,2048]{2,1,0:T(8,128)}, f32[8,8,2048]{2,1,0:T(8,128)S(1)}, u32[]{:S(2)}, u32[]{:S(2)}) collective-permute-start(f32[8,8,2048]{2,1,0:T(8,128)} %get-tuple-element.21.own_last_hbm), channel_id=1, source_target_pairs={{0,1},{1,2},{2,3},{3,4},{4,5},{5,6},{6,7},{7,8},{8,9},{9,10},{10,1... | collective-permute-start | bytes 1572872 | tf_op jit(solution)/shard_map/ppermute | solution.py:526
  8.5 4.1 %shard_map.91 = (f32[8,4,8,2048]{3,2,1,0:T(8,128)}, f32[8,8,2048]{2,1,0:T(8,128)}, f32[8,8,2048]{2,1,0:T(8,128)}, f32[5,4,8,2048]{3,2,1,0:T(8,128)}) custom-call(f32[8,512,128]{2,1,0:T(8,128)} %bitcast.29, f32[512,128]{1,0:T(8,128)} %bitcast.32, f32[512,128]{1,0:T(8,128)} %bitcast.31), custom_call_target="tpu_custom_call" | custom-call | tf_op jit(solution)/shard_map/pallas_call | solution.py:512
  12.6 4.3 %collective-permute-start.3 = (f32[8,8,2048]{2,1,0:T(8,128)}, f32[8,8,2048]{2,1,0:T(8,128)S(1)}, u32[]{:S(2)}, u32[]{:S(2)}) collective-permute-start(f32[8,8,2048]{2,1,0:T(8,128)} %get-tuple-element.28), channel_id=1, source_target_pairs={{0,1},{1,2},{2,3},{3,4},{4,5},{5,6},{6,7},{7,8},{8,9},{9,10},{10,1... | collective-permute-start | bytes 1572872 | tf_op jit(solution)/shard_map/ppermute | solution.py:528
  16.8 1.3 %collective-permute-start.4 = (f32[8,8,2048]{2,1,0:T(8,128)}, f32[8,8,2048]{2,1,0:T(8,128)S(1)}, u32[]{:S(2)}, u32[]{:S(2)}) collective-permute-start(f32[8,8,2048]{2,1,0:T(8,128)} %get-tuple-element.29), channel_id=1, source_target_pairs={{1,0},{2,1},{3,2},{4,3},{5,4},{6,5},{7,6},{8,7},{9,8},{10,9},{11,1... | collective-permute-start | bytes 1572872 | tf_op jit(solution)/shard_map/ppermute | solution.py:529
  18.2 25.1 %collective-permute-done.south_row_ref = f32[8,8,2048]{2,1,0:T(8,128)S(1)} collective-permute-done((f32[8,8,2048]{2,1,0:T(8,128)}, f32[8,8,2048]{2,1,0:T(8,128)S(1)}, u32[]{:S(2)}, u32[]{:S(2)}) %collective-permute-start) | collective-permute-done | bytes 524320 | tf_op jit(solution)/shard_map/ppermute | solution.py:526
  43.2 0.0 collective-permute-done.1.north_row_ref
  43.2 0.0 copy-done
  43.2 4.0 %shard_map.93 = (f32[2,8,8,2048]{3,2,1,0:T(8,128)}, f32[2,8,8,2048]{3,2,1,0:T(8,128)}, f32[2,8,2048]{2,1,0:T(8,128)}, f32[2,8,2048]{2,1,0:T(8,128)S(1)}) custom-call(s32[1]{0:T(128)} %bitcast.lev_ref, f32[8,4,8,2048]{3,2,1,0:T(8,128)} %get-tuple-element.20.part_hbm, f32[8,8,2048]{2,1,0:T(8,128)} %get-tuple-element.21.own_last_hbm, ...), custom_call_target="tpu_custom_call" | custom-call | tf_op jit(solution)/shard_map/pallas_call | solution.py:557
  47.3 0.0 copy-start.8
  47.3 0.0 copy-start.9
  47.3 0.0 copy-start.10
  47.3 7.1 %collective-permute-done.3.south_part_ref = f32[8,8,2048]{2,1,0:T(8,128)S(1)} collective-permute-done((f32[8,8,2048]{2,1,0:T(8,128)}, f32[8,8,2048]{2,1,0:T(8,128)S(1)}, u32[]{:S(2)}, u32[]{:S(2)}) %collective-permute-start.3) | collective-permute-done | bytes 524320 | tf_op jit(solution)/shard_map/ppermute | solution.py:528
  54.5 0.0 collective-permute-done.4.north_part_ref
  54.5 1.6 %shard_map.96 = (f32[2,8,8,2048]{3,2,1,0:T(8,128)S(1)}, f32[2,8,2048]{2,1,0:T(8,128)S(1)}, f32[2,8,2048]{2,1,0:T(8,128)S(1)}) custom-call(s32[1]{0:T(128)} %bitcast.lev_ref, f32[2,8,8,2048]{3,2,1,0:T(8,128)} %get-tuple-element.26.edge_hbm, f32[2,8,2048]{2,1,0:T(8,128)} %get-tuple-element.27.flow_hbm, ...), custom_call_target="tpu_custom_call" | custom-call | tf_op jit(solution)/shard_map/pallas_call | solution.py:578
  56.1 0.0 copy-start.4
  56.1 0.6 collective-permute-start.5
  56.7 0.1 collective-permute-start.2
  56.8 0.4 collective-permute-start.6
  57.2 3.5 %collective-permute-done.6 = f32[2,8,2048]{2,1,0:T(8,128)S(1)} collective-permute-done((f32[2,8,2048]{2,1,0:T(8,128)S(1)}, f32[2,8,2048]{2,1,0:T(8,128)S(1)}, u32[]{:S(2)}, u32[]{:S(2)}) %collective-permute-start.6) | collective-permute-done | bytes 131104 | tf_op jit(solution)/shard_map/ppermute | solution.py:587
  60.6 0.7 add.12
  61.3 1.3 %collective-permute-start.7 = (f32[2,8,2048]{2,1,0:T(8,128)}, f32[2,8,2048]{2,1,0:T(8,128)}, u32[]{:S(2)}, u32[]{:S(2)}) collective-permute-start(f32[2,8,2048]{2,1,0:T(8,128)} %add.12), channel_id=1, source_target_pairs={{64,128},{80,144},{96,160},{112,176},{128,192},{144,208},{160,224}... | collective-permute-start | bytes 393224 | tf_op jit(solution)/shard_map/ppermute | solution.py:597
  62.6 1.3 %collective-permute-start.8 = (f32[2,8,2048]{2,1,0:T(8,128)}, f32[2,8,2048]{2,1,0:T(8,128)}, u32[]{:S(2)}, u32[]{:S(2)}) collective-permute-start(f32[2,8,2048]{2,1,0:T(8,128)} %add.12), channel_id=1, source_target_pairs={{64,192},{80,208},{96,224},{112,240},{128,64},{144,80},{160,96},{1... | collective-permute-start | bytes 393224 | tf_op jit(solution)/shard_map/ppermute | solution.py:597
  63.9 0.0 copy-done.8
  63.9 0.0 copy-done.9
  63.9 0.0 copy-done.10
  63.9 0.6 shard_map.98
  64.5 0.0 copy-start.3
  64.6 0.7 copy-done.3
  65.2 10.1 %all-to-all-start = ((f32[16,24,128]{2,1,0:T(8,128)}), f32[16,24,128]{2,1,0:T(8,128)S(1)}, u32[]{:S(2)}, u32[]{:S(2)}) async-start(f32[16,24,128]{2,1,0:T(8,128)} %copy-done.3), calls=%async_computation | async-start | bytes 393216 | tf_op jit(solution)/shard_map/all_to_all | solution.py:539
  75.3 0.0 collective-permute-done.7
  75.3 0.0 collective-permute-done.8
  75.4 1.7 %add_add_fusion = f32[2,8,2048]{2,1,0:T(8,128)} fusion(f32[2,8,2048]{2,1,0:T(8,128)} %collective-permute-done.8, f32[2,8,2048]{2,1,0:T(8,128)} %add.12, f32[2,8,2048]{2,1,0:T(8,128)} %collective-permute-done.7), kind=kLoop, calls=%fused_computation | loop fusion | flops 65536 | bytes 524288 | tf_op jit(solution)/shard_map/add | solution.py:598
  77.1 1.3 %collective-permute-start.9 = (f32[2,8,2048]{2,1,0:T(8,128)}, f32[2,8,2048]{2,1,0:T(8,128)}, u32[]{:S(2)}, u32[]{:S(2)}) collective-permute-start(f32[2,8,2048]{2,1,0:T(8,128)} %add_add_fusion), channel_id=1, source_target_pairs={{64,96},{80,112},{96,64},{112,80},{128,160},{144,176},{160,128},{1... | collective-permute-start | bytes 393224 | tf_op jit(solution)/shard_map/ppermute | solution.py:601
  78.4 6.6 %all-to-all-done.packed_ref = f32[16,24,128]{2,1,0:T(8,128)S(1)} async-done(((f32[16,24,128]{2,1,0:T(8,128)}), f32[16,24,128]{2,1,0:T(8,128)S(1)}, u32[]{:S(2)}, u32[]{:S(2)}) %all-to-all-start) | async-done | bytes 196640 | tf_op jit(solution)/shard_map/all_to_all | solution.py:539
  84.9 1.4 %shard_map.99 = f32[16,8,512]{2,1,0:T(8,128)} custom-call(f32[16,24,128]{2,1,0:T(8,128)S(1)} %all-to-all-done.packed_ref), custom_call_target="tpu_custom_call" | custom-call | tf_op jit(solution)/shard_map/pallas_call | solution.py:541
  86.4 11.6 %all-to-all-start.1 = ((f32[16,8,512]{2,1,0:T(8,128)}), f32[16,8,512]{2,1,0:T(8,128)S(1)}, u32[]{:S(2)}, u32[]{:S(2)}) async-start(f32[16,8,512]{2,1,0:T(8,128)} %shard_map.99), calls=%async_computation.1 | async-start | bytes 524288 | tf_op jit(solution)/shard_map/all_to_all | solution.py:544
  97.9 0.0 collective-permute-done.9
  98.0 1.6 %add.15.own_ref = f32[2,8,2048]{2,1,0:T(8,128)} add(f32[2,8,2048]{2,1,0:T(8,128)} %add_add_fusion, f32[2,8,2048]{2,1,0:T(8,128)} %collective-permute-done.9) | non-fusion elementwise | flops 32768 | bytes 393216 | tf_op jit(solution)/shard_map/add | solution.py:601
  99.6 0.1 collective-permute-start.10
  99.7 0.0 copy-done.4
  99.7 0.0 copy-start.7
  99.7 0.9 copy-done.7
  100.6 0.8 shard_map.94
  101.5 0.0 copy-start.5
  101.5 0.7 copy-done.5
  102.2 0.0 collective-permute-done.5.other_ref
  102.2 0.0 copy-start.1
  102.2 1.0 copy-done.1
  103.2 0.0 copy-start.2
  103.2 1.2 %copy-done.2 = f32[2,8,8,2048]{3,2,1,0:T(8,128)S(1)} copy-done((f32[2,8,8,2048]{3,2,1,0:T(8,128)S(1)}, f32[2,8,8,2048]{3,2,1,0:T(8,128)}, u32[]{:S(2)}) %copy-start.2) | copy-done | bytes 1048600
  104.4 0.5 shard_map.97.edge_ref
  104.9 0.0 copy-start.6
  104.9 0.0 collective-permute-done.2.other_hbm
  105.0 2.9 %shard_map.95.mid_hbm = f32[2,8,8,2048]{3,2,1,0:T(8,128)} custom-call(s32[1]{0:T(128)} %bitcast.lev_ref, f32[2,8,8,2048]{3,2,1,0:T(8,128)} %get-tuple-element.24.adv_hbm, f32[2,8,8,2048]{3,2,1,0:T(8,128)S(1)} %collective-permute-done.2.other_hbm, s32[2,4,2048]{2,1,0:T(4,128)S(1)} %copy-done, f32[4,2048]{1,0:T(4,128)S(1)} %copy-done.4, ...), custom_call_target="tpu_custom_call" | custom-call | tf_op jit(solution)/shard_map/pallas_call | solution.py:569
  107.8 0.0 all-to-all-done.1.forcing_ref
  107.8 0.0 collective-permute-done.10.other_ref
  107.8 0.0 copy-done.6
  107.9 3.4 %shard_map.100 = f32[8,512,128]{2,1,0:T(8,128)} custom-call(s32[1]{0:T(128)} %bitcast.lev_ref, f32[2,8,8,2048]{3,2,1,0:T(8,128)} %shard_map.95.mid_hbm, f32[2,8,8,2048]{3,2,1,0:T(8,128)S(1)} %shard_map.97.edge_ref, f32[4,8,2048]{2,1,0:T(8,128)S(1)} %copy-done.6, f32[2,8,2048]{2,1,0:T(8,128)} %add.15.own_ref, ...), custom_call_target="tpu_custom_call" | custom-call | tf_op jit(solution)/shard_map/pallas_call | solution.py:612
Async XLA Ops:
  0.0 43.2 %copy-start = (s32[2,4,2048]{2,1,0:T(4,128)S(1)}, s32[2,4,2048]{2,1,0:T(4,128)}, u32[]{:S(2)}) copy-start(s32[2,4,2048]{2,1,0:T(4,128)} %band_ref.9) | copy-start | bytes 196612
  2.6 40.7 %collective-permute-start.1 = (f32[9,8,2048]{2,1,0:T(8,128)}, f32[9,8,2048]{2,1,0:T(8,128)S(1)}, u32[]{:S(2)}, u32[]{:S(2)}) collective-permute-start(f32[9,8,2048]{2,1,0:T(8,128)} %get-tuple-element.22), channel_id=1, source_target_pairs={{1,0},{2,1},{3,2},{4,3},{5,4},{6,5},{7,6},{8,7},{9,8},{10,9},{11,1... | collective-permute-start | bytes 1769480 | tf_op jit(solution)/shard_map/ppermute | solution.py:527
  3.9 39.4 %collective-permute-start = (f32[8,8,2048]{2,1,0:T(8,128)}, f32[8,8,2048]{2,1,0:T(8,128)S(1)}, u32[]{:S(2)}, u32[]{:S(2)}) collective-permute-start(f32[8,8,2048]{2,1,0:T(8,128)} %get-tuple-element.21.own_last_hbm), channel_id=1, source_target_pairs={{0,1},{1,2},{2,3},{3,4},{4,5},{5,6},{6,7},{7,8},{8,9},{9,10},{10,1... | collective-permute-start | bytes 1572872 | tf_op jit(solution)/shard_map/ppermute | solution.py:526
  12.6 41.9 %collective-permute-start.3 = (f32[8,8,2048]{2,1,0:T(8,128)}, f32[8,8,2048]{2,1,0:T(8,128)S(1)}, u32[]{:S(2)}, u32[]{:S(2)}) collective-permute-start(f32[8,8,2048]{2,1,0:T(8,128)} %get-tuple-element.28), channel_id=1, source_target_pairs={{0,1},{1,2},{2,3},{3,4},{4,5},{5,6},{6,7},{7,8},{8,9},{9,10},{10,1... | collective-permute-start | bytes 1572872 | tf_op jit(solution)/shard_map/ppermute | solution.py:528
  16.8 37.6 %collective-permute-start.4 = (f32[8,8,2048]{2,1,0:T(8,128)}, f32[8,8,2048]{2,1,0:T(8,128)S(1)}, u32[]{:S(2)}, u32[]{:S(2)}) collective-permute-start(f32[8,8,2048]{2,1,0:T(8,128)} %get-tuple-element.29), channel_id=1, source_target_pairs={{1,0},{2,1},{3,2},{4,3},{5,4},{6,5},{7,6},{8,7},{9,8},{10,9},{11,1... | collective-permute-start | bytes 1572872 | tf_op jit(solution)/shard_map/ppermute | solution.py:529
  47.3 16.6 %copy-start.8 = (f32[1,1,16,16,128]{4,3,2,1,0:T(8,128)S(1)}, f32[1,1,16,16,128]{4,3,2,1,0:T(8,128)}, u32[]{:S(2)}) copy-start(f32[1,1,16,16,128]{4,3,2,1,0:T(8,128)} %param.15) | copy-start | bytes 393220
  47.3 16.6 %copy-start.9 = (s32[1,1,16,16]{3,2,1,0:T(8,128)S(1)}, s32[1,1,16,16]{3,2,1,0:T(8,128)}, u32[]{:S(2)}) copy-start(s32[1,1,16,16]{3,2,1,0:T(8,128)} %param.16) | copy-start | bytes 3076
  47.3 16.6 %copy-start.10 = (s32[1,1,16]{2,1,0:T(1,128)S(1)}, s32[1,1,16]{2,1,0:T(1,128)}, u32[]{:S(2)}) copy-start(s32[1,1,16]{2,1,0:T(1,128)} %param.17) | copy-start | bytes 196
  56.1 43.6 %copy-start.4 = (f32[4,2048]{1,0:T(4,128)S(1)}, f32[4,2048]{1,0:T(4,128)}, u32[]{:S(2)}) copy-start(f32[4,2048]{1,0:T(4,128)} %flux_ref.5) | copy-start | bytes 98308
  56.1 46.1 %collective-permute-start.5 = (f32[2,8,8,2048]{3,2,1,0:T(8,128)S(1)}, f32[2,8,8,2048]{3,2,1,0:T(8,128)S(1)}, u32[]{:S(2)}, u32[]{:S(2)}) collective-permute-start(f32[2,8,8,2048]{3,2,1,0:T(8,128)S(1)} %get-tuple-element.31.adv_ref), channel_id=1, source_target_pairs={{0,16},{16,0},{32,48},{48,32},{64,80},{80,64},{96,112},{112,96},{1... | collective-permute-start | bytes 3145736 | tf_op jit(solution)/shard_map/ppermute | solution.py:599
  56.7 48.3 %collective-permute-start.2 = (f32[2,8,8,2048]{3,2,1,0:T(8,128)}, f32[2,8,8,2048]{3,2,1,0:T(8,128)S(1)}, u32[]{:S(2)}, u32[]{:S(2)}) collective-permute-start(f32[2,8,8,2048]{3,2,1,0:T(8,128)} %get-tuple-element.24.adv_hbm), channel_id=1, source_target_pairs={{0,16},{16,0},{32,48},{48,32},{64,80},{80,64},{96,112},{112,96},{1... | collective-permute-start | bytes 3145736 | tf_op jit(solution)/shard_map/ppermute | solution.py:568
  56.8 3.9 %collective-permute-start.6 = (f32[2,8,2048]{2,1,0:T(8,128)S(1)}, f32[2,8,2048]{2,1,0:T(8,128)S(1)}, u32[]{:S(2)}, u32[]{:S(2)}) collective-permute-start(f32[2,8,2048]{2,1,0:T(8,128)S(1)} %get-tuple-element.34), channel_id=1, source_target_pairs={{0,16},{16,0},{32,48},{48,32},{64,80},{80,64},{96,112},{112,96},{1... | collective-permute-start | bytes 393224 | tf_op jit(solution)/shard_map/ppermute | solution.py:587
  61.3 14.0 %collective-permute-start.7 = (f32[2,8,2048]{2,1,0:T(8,128)}, f32[2,8,2048]{2,1,0:T(8,128)}, u32[]{:S(2)}, u32[]{:S(2)}) collective-permute-start(f32[2,8,2048]{2,1,0:T(8,128)} %add.12), channel_id=1, source_target_pairs={{64,128},{80,144},{96,160},{112,176},{128,192},{144,208},{160,224}... | collective-permute-start | bytes 393224 | tf_op jit(solution)/shard_map/ppermute | solution.py:597
  62.6 12.7 %collective-permute-start.8 = (f32[2,8,2048]{2,1,0:T(8,128)}, f32[2,8,2048]{2,1,0:T(8,128)}, u32[]{:S(2)}, u32[]{:S(2)}) collective-permute-start(f32[2,8,2048]{2,1,0:T(8,128)} %add.12), channel_id=1, source_target_pairs={{64,192},{80,208},{96,224},{112,240},{128,64},{144,80},{160,96},{1... | collective-permute-start | bytes 393224 | tf_op jit(solution)/shard_map/ppermute | solution.py:597
  64.5 0.7 copy-start.3
  65.2 19.7 %all-to-all-start = ((f32[16,24,128]{2,1,0:T(8,128)}), f32[16,24,128]{2,1,0:T(8,128)S(1)}, u32[]{:S(2)}, u32[]{:S(2)}) async-start(f32[16,24,128]{2,1,0:T(8,128)} %copy-done.3), calls=%async_computation | async-start | bytes 393216 | tf_op jit(solution)/shard_map/all_to_all | solution.py:539
  77.1 20.9 %collective-permute-start.9 = (f32[2,8,2048]{2,1,0:T(8,128)}, f32[2,8,2048]{2,1,0:T(8,128)}, u32[]{:S(2)}, u32[]{:S(2)}) collective-permute-start(f32[2,8,2048]{2,1,0:T(8,128)} %add_add_fusion), channel_id=1, source_target_pairs={{64,96},{80,112},{96,64},{112,80},{128,160},{144,176},{160,128},{1... | collective-permute-start | bytes 393224 | tf_op jit(solution)/shard_map/ppermute | solution.py:601
  86.4 21.5 %all-to-all-start.1 = ((f32[16,8,512]{2,1,0:T(8,128)}), f32[16,8,512]{2,1,0:T(8,128)S(1)}, u32[]{:S(2)}, u32[]{:S(2)}) async-start(f32[16,8,512]{2,1,0:T(8,128)} %shard_map.99), calls=%async_computation.1 | async-start | bytes 524288 | tf_op jit(solution)/shard_map/all_to_all | solution.py:544
  99.6 8.3 %collective-permute-start.10 = (f32[2,8,2048]{2,1,0:T(8,128)}, f32[2,8,2048]{2,1,0:T(8,128)}, u32[]{:S(2)}, u32[]{:S(2)}) collective-permute-start(f32[2,8,2048]{2,1,0:T(8,128)} %add.15.own_ref), channel_id=1, source_target_pairs={{0,16},{16,0},{32,48},{48,32},{64,80},{80,64},{96,112},{112,96},{1... | collective-permute-start | bytes 393224 | tf_op jit(solution)/shard_map/ppermute | solution.py:602
  99.7 1.0 copy-start.7
  101.5 0.7 copy-start.5
  102.2 1.0 copy-start.1
  103.2 1.2 %copy-start.2 = (f32[2,8,8,2048]{3,2,1,0:T(8,128)S(1)}, f32[2,8,8,2048]{3,2,1,0:T(8,128)}, u32[]{:S(2)}) copy-start(f32[2,8,8,2048]{3,2,1,0:T(8,128)} %copy-done.1) | copy-start | bytes 3145732
  104.9 2.9 %copy-start.6 = (f32[4,8,2048]{2,1,0:T(8,128)S(1)}, f32[4,8,2048]{2,1,0:T(8,128)}, u32[]{:S(2)}) copy-start(f32[4,8,2048]{2,1,0:T(8,128)} %copy-done.5) | copy-start | bytes 786436

commit v5 on v4

--- a/solution.py
+++ b/solution.py
@@ -204,8 +204,8 @@
 
 def mid_kernel(
     lev_ref, part_hbm, own_last_hbm, south_row_ref, north_row_ref, coef_hbm, band_ref,
-    mid_hbm, edge_hbm, flow_hbm, sum_out_ref,
-    part_ref, own_last_ref, coef_ref, flow_ref, center_ref, inside_ref, mid_ref, edge_ref, sems,
+    mid_hbm, edge_hbm, flow_hbm, keep_ref, send_ref,
+    part_ref, own_last_ref, coef_ref, flow_ref, center_ref, inside_ref, mid_ref, edge_ref, sum_ref, sems,
 ):
     tiles = range(16)
 
@@ -274,7 +274,11 @@
         for j in tiles:
             s = lane_slice(j)
             inside = inside_ref[q, :, s]
-            sum_out_ref[q, :, s] = level_sums([mid_ref[q, t, :, s] * inside for t in range(8)])
+            sum_ref[q, :, s] = level_sums([mid_ref[q, t, :, s] * inside for t in range(8)])
+
+    core = lax.rem(lev_ref[0], 2)
+    keep_ref[...] = sum_ref[pl.ds(core, 1)]
+    send_ref[...] = sum_ref[pl.ds(1 - core, 1)]
 
     @pl.loop(0, 8)
     def _(t):
@@ -285,28 +289,32 @@
 
 
 def close_kernel(
-    lev_ref, edge_hbm, flow_hbm, south_part_ref, north_part_ref, sum_mid_ref, band_ref, adv_ref, keep_ref, send_ref,
-    edge_ref, flow_ref, inside_ref, sum_ref, sems,
+    lev_ref, edge_hbm, flow_hbm, south_part_hbm, north_part_hbm, band_ref, adv_ref, keep_ref, send_ref,
+    edge_ref, south_part_ref, north_part_ref, flow_ref, inside_ref, sum_ref, sems,
 ):
     def incoming(t):
-        return pltpu.make_async_copy(edge_hbm.at[:, t], edge_ref.at[:, t], sems.at[t])
-
-    flow_copy = pltpu.make_async_copy(flow_hbm, flow_ref, sems.at[8])
+        return [
+            pltpu.make_async_copy(edge_hbm.at[:, t], edge_ref.at[:, t], sems.at[t, 0]),
+            pltpu.make_async_copy(south_part_hbm.at[t], south_part_ref.at[t], sems.at[t, 1]),
+            pltpu.make_async_copy(north_part_hbm.at[t], north_part_ref.at[t], sems.at[t, 2]),
+        ]
+
+    flow_copy = pltpu.make_async_copy(flow_hbm, flow_ref, sems.at[8, 0])
     flow_copy.start()
 
     @pl.loop(0, 8)
     def _(t):
-        incoming(t).start()
+        for copy in incoming(t):
+            copy.start()
 
     for q in range(2):
         inside_ref[q] = inside_band(lev_ref, band_ref, 3 * q)
-    sum_ref[1] = sum_mid_ref[0]
-    sum_ref[2] = sum_mid_ref[1]
     flow_copy.wait()
 
     @pl.loop(0, 8)
     def _(t):
-        incoming(t).wait()
+        for copy in incoming(t):
+            copy.wait()
         adv_ref[0, t] = edge_ref[0, t] - flow_ref[0] * south_part_ref[t]
         adv_ref[1, t] = edge_ref[1, t] + flow_ref[1] * north_part_ref[t]
 
@@ -314,11 +322,11 @@
         for j in range(16):
             s = lane_slice(j)
             inside = inside_ref[q, :, s]
-            sum_ref[3 * q, :, s] = level_sums([adv_ref[q, t, :, s] * inside for t in range(8)])
+            sum_ref[q, :, s] = level_sums([adv_ref[q, t, :, s] * inside for t in range(8)])
 
     core = lax.rem(lev_ref[0], 2)
-    keep_ref[...] = sum_ref[pl.ds(2 * core, 2)]
-    send_ref[...] = sum_ref[pl.ds(2 - 2 * core, 2)]
+    keep_ref[...] = sum_ref[pl.ds(core, 1)]
+    send_ref[...] = sum_ref[pl.ds(1 - core, 1)]
 
 
 def halves_of(x):
@@ -381,7 +389,7 @@
 
 
 def diffuse_mid_kernel(
-    lev_ref, adv_hbm, other_hbm, band_ref, flux_ref, matrix_ref, out_hbm, adv_ref, other_ref, out_ref, sems
+    lev_ref, adv_hbm, other_hbm, band_ref, flux_ref, matrix_ref, out_ref, adv_ref, other_ref, sems
 ):
     copies = [
         [
@@ -399,34 +407,23 @@
             copy.wait()
 
     diffuse_rows((1, 2), lev_ref, adv_ref, other_ref, band_ref, flux_ref, matrix_ref, out_ref, ready)
-    result = pltpu.make_async_copy(out_ref, out_hbm, sems.at[2, 0])
-    result.start()
-    result.wait()
 
 
 def diffuse_edge_kernel(lev_ref, adv_ref, other_ref, band_ref, flux_ref, matrix_ref, out_ref):
     diffuse_rows((0, 3), lev_ref, adv_ref, other_ref, band_ref, flux_ref, matrix_ref, out_ref, lambda q: None)
 
 
-def finish_kernel(
-    lev_ref, mid_hbm, edge_ref, gain_ref, own_ref, other_ref, forcing_ref, out_ref, sum_ref, done_ref, mid_ref, sems, mid_sems
-):
-    def incoming(t):
-        return pltpu.make_async_copy(mid_hbm.at[:, t], mid_ref.at[:, t], mid_sems.at[t])
-
-    @pl.loop(0, 8)
-    def _(t):
-        incoming(t).start()
-
+def finish_kernel(lev_ref, mid_ref, edge_ref, gain_ref, own_ref, other_ref, forcing_ref, out_ref, sum_ref, done_ref, sems):
     core = lax.rem(lev_ref[0], 2)
-    for q in range(2):
-        for j in range(16):
-            sum_ref[2 * core + q, j] = own_ref[q, :, lane_slice(j)]
-            sum_ref[2 - 2 * core + q, j] = other_ref[q, :, lane_slice(j)]
-
-    @pl.loop(0, 8)
-    def _(t):
-        incoming(t).wait()
+    for j in range(16):
+        s = lane_slice(j)
+        sum_ref[1 + core, j] = own_ref[0, :, s]
+        sum_ref[3 * core, j] = own_ref[1, :, s]
+        sum_ref[2 - core, j] = other_ref[0, :, s]
+        sum_ref[3 - 3 * core, j] = other_ref[1, :, s]
+
+    @pl.loop(0, 8)
+    def _(t):
         for k in range(8):
             tiles = []
             for j in (2 * k, 2 * k + 1):
@@ -554,53 +551,62 @@
     two_rows = pltpu.VMEM((2, 8, 8, lons), F32)
     one_row = pltpu.VMEM((2, 8, lons), F32)
     swap = [(i, i ^ 1) for i in range(lev_count)]
-    mid, edge, flow, sum_mid = pl.pallas_call(
+    mid, edge, flow, keep_mid, send_mid = pl.pallas_call(
         mid_kernel,
         in_specs=[smem] + [hbm] * 2 + [vmem] * 2 + [hbm, vmem],
-        out_specs=[hbm] * 3 + [vmem],
-        out_shape=[far(2, 8, 8, lons), far(2, 8, 8, lons), far(2, 8, lons), shape(2, 8, lons)],
+        out_specs=[hbm] * 3 + [vmem] * 2,
+        out_shape=[
+            far(2, 8, 8, lons), far(2, 8, 8, lons), far(2, 8, lons), shape(1, 8, lons), shape(1, 8, lons)
+        ],
         scratch_shapes=[
             pltpu.VMEM((8, 4, 8, lons), F32), pltpu.VMEM((8, 8, lons), F32), pltpu.VMEM((5, 4, 8, lons), F32),
-            one_row, pltpu.VMEM((8, lons), F32), one_row, two_rows, two_rows, pltpu.SemaphoreType.DMA((9, 4)),
+            one_row, pltpu.VMEM((8, lons), F32), one_row, two_rows, two_rows, one_row, pltpu.SemaphoreType.DMA((9, 4)),
         ],
         compiler_params=small,
     )(lev, keep_far(part), keep_far(last_row), south_row, north_row, keep_far(coef), conv_band)
+
+    blocks = lev_count // 2
+    lines = blocks // 2 - 1
+
+    def summed(keep, send):
+        part_sum = keep + lax.ppermute(send, "lev", swap)
+        moved = []
+        for shift in range(1, lines):
+            pairs = []
+            for y in range(lines):
+                for n in range(4):
+                    pairs.append((4 * (y + 1) + n, 4 * ((y + shift) % lines + 1) + n))
+            moved.append(lax.ppermute(part_sum, "lev", pairs))
+        return sum(moved, part_sum)
+
+    total_mid = summed(keep_mid, send_mid)
+
+    adv, keep, send = pl.pallas_call(
+        close_kernel,
+        in_specs=[smem] + [hbm] * 4 + [vmem],
+        out_specs=[vmem] * 3,
+        out_shape=[shape(2, 8, 8, lons), shape(1, 8, lons), shape(1, 8, lons)],
+        scratch_shapes=[
+            two_rows, pltpu.VMEM((8, 8, lons), F32), pltpu.VMEM((8, 8, lons), F32), one_row, one_row, one_row,
+            pltpu.SemaphoreType.DMA((9, 3)),
+        ],
+        compiler_params=small,
+    )(lev, keep_far(edge), keep_far(flow), south_part, north_part, conv_band)
+    total_edge = summed(keep, send)
+    adv_other = lax.ppermute(adv, "lev", swap)
     mid_other = lax.ppermute(mid, "lev", swap)
+    pairs = [(2 * n + c, 2 * (n ^ 1) + c) for n in range(2, blocks) for c in range(2)]
+    total = jnp.concatenate([total_mid, total_edge], axis=0)
+    total = total + lax.ppermute(total, "lev", pairs)
+    total_other = lax.ppermute(total, "lev", swap)
     base_mid = pl.pallas_call(
         diffuse_mid_kernel,
         in_specs=[smem] + [hbm] * 2 + [vmem] * 3,
-        out_specs=hbm,
-        out_shape=far(2, 8, 8, lons),
-        scratch_shapes=[two_rows] * 3 + [pltpu.SemaphoreType.DMA((3, 2))],
+        out_specs=vmem,
+        out_shape=shape(2, 8, 8, lons),
+        scratch_shapes=[two_rows] * 2 + [pltpu.SemaphoreType.DMA((2, 2))],
         compiler_params=small,
     )(lev, keep_far(mid), mid_other, conv_band, mass_flux, matrix)
-
-    adv, keep, send = pl.pallas_call(
-        close_kernel,
-        in_specs=[smem] + [hbm] * 2 + [vmem] * 4,
-        out_specs=[vmem] * 3,
-        out_shape=[shape(2, 8, 8, lons), shape(2, 8, lons), shape(2, 8, lons)],
-        scratch_shapes=[two_rows, one_row, one_row, row_scratch, pltpu.SemaphoreType.DMA((9,))],
-        compiler_params=small,
-    )(lev, keep_far(edge), keep_far(flow), south_part, north_part, sum_mid, conv_band)
-
-    swapped = lax.ppermute(send, "lev", swap)
-    chip_sum = keep + swapped
-    blocks = lev_count // 2
-    lines = blocks // 2 - 1
-    moved = []
-    for shift in range(1, lines):
-        pairs = []
-        for y in range(lines):
-            for n in range(4):
-                pairs.append((4 * (y + 1) + n, 4 * ((y + shift) % lines + 1) + n))
-        moved.append(lax.ppermute(chip_sum, "lev", pairs))
-    total = sum(moved, chip_sum)
-    adv_other = lax.ppermute(adv, "lev", swap)
-    pairs = [(2 * n + c, 2 * (n ^ 1) + c) for n in range(2, blocks) for c in range(2)]
-    total = total + lax.ppermute(total, "lev", pairs)
-    total_other = lax.ppermute(total, "lev", swap)
-
     base_edge = pl.pallas_call(
         diffuse_edge_kernel,
         in_specs=[smem] + [vmem] * 5,
@@ -611,15 +617,14 @@
 
     out = pl.pallas_call(
         finish_kernel,
-        in_specs=[smem, hbm] + [vmem] * 5,
+        in_specs=[smem] + [vmem] * 6,
         out_specs=hbm,
         out_shape=shape(tracers, 512, LANES),
         scratch_shapes=[
-            pltpu.VMEM((4, 16, 8, LANES), F32), pltpu.VMEM((8, 512, LANES), F32), two_rows,
-            pltpu.SemaphoreType.DMA((8,)), pltpu.SemaphoreType.DMA((8,)),
+            pltpu.VMEM((4, 16, 8, LANES), F32), pltpu.VMEM((8, 512, LANES), F32), pltpu.SemaphoreType.DMA((8,))
         ],
         compiler_params=small,
-    )(lev, keep_far(base_mid), base_edge, gain, total, total_other, forcing)
+    )(lev, base_mid, base_edge, gain, total, total_other, forcing)
     return join_rows(out.reshape(tracers, levels, 64, LANES), rows, lons)
 
 

time: 112 us -> 115 us (1.027)
  starting transfers between devices: 38.2 us -> 45.8 us
  waiting for transfers between devices: 42.3 us -> 35.9 us
    all_to_all x1, starting transfers between devices: 11.6 us -> 17.2 us  [body(): lax.all_to_all(forcing, 'lev', split_axis=0, concat_axis=0, tiled=True)]
    ppermute x3 -> x6, waiting for transfers between devices: 3.47 us -> 0.02 us  [the longest x4 0.01 us: summed(): moved.append(lax.ppermute(part_sum, 'lev', pairs))]
    all_to_all x1, waiting for transfers between devices: 6.57 us -> 4.34 us  [body(): lax.all_to_all(packed, 'lat', split_axis=0, concat_axis=0, tiled=True)]
    ppermute x3 -> x6, starting transfers between devices: 3.02 us -> 5.04 us  [the longest x4 3.88 us: summed(): moved.append(lax.ppermute(part_sum, 'lev', pairs))]
    unnamed x22 -> x26, local copies, waits for them, and re-layouts: 4.55 us -> 5.42 us
    add x2 -> x4, other arithmetic: 2.36 us -> 1.79 us  [the longest x2 0.9 us: summed(): return sum(moved, part_sum)]
  transfers between devices with their start and end apart: 13 -> 16, of which waited for: 4 -> 3; matrix products, arithmetic and copies ran while one was open for 4% -> 4% of each run, Pallas kernels for 13% -> 15%
where the time goes in v5:
time: 115 us; the launch traced here: 114 us
  starting transfers between devices  45.8 us (40%)
  waiting for transfers between devices  35.9 us (31%)
  Pallas kernels  22.3 us (19%)
  local copies, waits for them, and re-layouts  5.42 us (5%)
  other arithmetic  4.07 us (4%)
    ppermute x1, waiting for transfers between devices, body(): south_row = lax.ppermute(last_row, 'lat', north)  25.1 us
    all_to_all x1, starting transfers between devices, body(): lax.all_to_all(forcing, 'lev', split_axis=0, concat_axis=0, tiled=True)  17.2 us
    all_to_all x1, starting transfers between devices, body(): lax.all_to_all(packed, 'lat', split_axis=0, concat_axis=0, tiled=True)  10.1 us
    ppermute x1, waiting for transfers between devices, body(): south_part = lax.ppermute(to_north, 'lat', north)  6.43 us
    unnamed x26, local copies, waits for them, and re-layouts  5.42 us
    ppermute x1, starting transfers between devices, body(): south_row = lax.ppermute(last_row, 'lat', north)  4.59 us
    all_to_all x1, waiting for transfers between devices, body(): lax.all_to_all(packed, 'lat', split_axis=0, concat_axis=0, tiled=True)  4.34 us
    ppermute x1, starting transfers between devices, body(): south_part = lax.ppermute(to_north, 'lat', north)  4.26 us
  transfers between devices with their start and end apart: 16, of which 3 were waited for; matrix products, arithmetic and copies ran while one was open for 4% of the time, Pallas kernels for 15%

profile of v5, /device:TPU:1, one launch (start us, length us, event | category | flops | bytes accessed | tf_op | source)
XLA Modules:
  0.0 113.7 jit_solution(1912479111130659736)
XLA Ops:
  0.0 2.5 %shard_map.92 = (f32[8,8,2048]{2,1,0:T(8,128)}, f32[9,8,2048]{2,1,0:T(8,128)}) custom-call(f32[8,512,128]{2,1,0:T(8,128)} %bitcast.28, f32[512,128]{1,0:T(8,128)} %bitcast.30), custom_call_target="tpu_custom_call" | custom-call | tf_op jit(solution)/shard_map/pallas_call | solution.py:498
  2.5 1.3 %collective-permute-start.1 = (f32[9,8,2048]{2,1,0:T(8,128)}, f32[9,8,2048]{2,1,0:T(8,128)S(1)}, u32[]{:S(2)}, u32[]{:S(2)}) collective-permute-start(f32[9,8,2048]{2,1,0:T(8,128)} %get-tuple-element.23), channel_id=1, source_target_pairs={{1,0},{2,1},{3,2},{4,3},{5,4},{6,5},{7,6},{8,7},{9,8},{10,9},{11,1... | collective-permute-start | bytes 1769480 | tf_op jit(solution)/shard_map/ppermute | solution.py:524
  3.8 4.6 %collective-permute-start = (f32[8,8,2048]{2,1,0:T(8,128)}, f32[8,8,2048]{2,1,0:T(8,128)S(1)}, u32[]{:S(2)}, u32[]{:S(2)}) collective-permute-start(f32[8,8,2048]{2,1,0:T(8,128)} %get-tuple-element.22.own_last_hbm), channel_id=1, source_target_pairs={{0,1},{1,2},{2,3},{3,4},{4,5},{5,6},{6,7},{7,8},{8,9},{9,10},{10,1... | collective-permute-start | bytes 1572872 | tf_op jit(solution)/shard_map/ppermute | solution.py:523
  8.4 4.1 %shard_map.91 = (f32[8,4,8,2048]{3,2,1,0:T(8,128)}, f32[8,8,2048]{2,1,0:T(8,128)}, f32[8,8,2048]{2,1,0:T(8,128)}, f32[5,4,8,2048]{3,2,1,0:T(8,128)}) custom-call(f32[8,512,128]{2,1,0:T(8,128)} %bitcast.29, f32[512,128]{1,0:T(8,128)} %bitcast.32, f32[512,128]{1,0:T(8,128)} %bitcast.31), custom_call_target="tpu_custom_call" | custom-call | tf_op jit(solution)/shard_map/pallas_call | solution.py:509
  12.5 4.3 %collective-permute-start.3 = (f32[8,8,2048]{2,1,0:T(8,128)}, f32[8,8,2048]{2,1,0:T(8,128)S(1)}, u32[]{:S(2)}, u32[]{:S(2)}) collective-permute-start(f32[8,8,2048]{2,1,0:T(8,128)} %get-tuple-element.29), channel_id=1, source_target_pairs={{0,1},{1,2},{2,3},{3,4},{4,5},{5,6},{6,7},{7,8},{8,9},{9,10},{10,1... | collective-permute-start | bytes 1572872 | tf_op jit(solution)/shard_map/ppermute | solution.py:525
  16.8 1.3 %collective-permute-start.4 = (f32[8,8,2048]{2,1,0:T(8,128)}, f32[8,8,2048]{2,1,0:T(8,128)S(1)}, u32[]{:S(2)}, u32[]{:S(2)}) collective-permute-start(f32[8,8,2048]{2,1,0:T(8,128)} %get-tuple-element.30), channel_id=1, source_target_pairs={{1,0},{2,1},{3,2},{4,3},{5,4},{6,5},{7,6},{8,7},{9,8},{10,9},{11,1... | collective-permute-start | bytes 1572872 | tf_op jit(solution)/shard_map/ppermute | solution.py:526
  18.1 25.1 %collective-permute-done.south_row_ref = f32[8,8,2048]{2,1,0:T(8,128)S(1)} collective-permute-done((f32[8,8,2048]{2,1,0:T(8,128)}, f32[8,8,2048]{2,1,0:T(8,128)S(1)}, u32[]{:S(2)}, u32[]{:S(2)}) %collective-permute-start) | collective-permute-done | bytes 524320 | tf_op jit(solution)/shard_map/ppermute | solution.py:523
  43.2 0.0 collective-permute-done.1.north_row_ref
  43.2 0.0 copy-done
  43.2 4.1 %shard_map.93 = (f32[2,8,8,2048]{3,2,1,0:T(8,128)}, f32[2,8,8,2048]{3,2,1,0:T(8,128)}, f32[2,8,2048]{2,1,0:T(8,128)}, f32[1,8,2048]{2,1,0:T(8,128)S(1)}, f32[1,8,2048]{2,1,0:T(8,128)S(1)}) custom-call(s32[1]{0:T(128)} %bitcast.lev_ref, f32[8,4,8,2048]{3,2,1,0:T(8,128)} %get-tuple-element.21.part_hbm, f32[8,8,2048]{2,1,0:T(8,128)} %get-tuple-element.22.own_last_hbm, ...), custom_call_target="tpu_custom_call" | custom-call | tf_op jit(solution)/shard_map/pallas_call | solution.py:554
  47.3 0.0 copy-start.7
  47.3 0.0 copy-start.9
  47.3 0.0 copy-start.10
  47.3 0.7 collective-permute-start.6
  48.0 6.4 %collective-permute-done.3.south_part_hbm = f32[8,8,2048]{2,1,0:T(8,128)S(1)} collective-permute-done((f32[8,8,2048]{2,1,0:T(8,128)}, f32[8,8,2048]{2,1,0:T(8,128)S(1)}, u32[]{:S(2)}, u32[]{:S(2)}) %collective-permute-start.3) | collective-permute-done | bytes 524320 | tf_op jit(solution)/shard_map/ppermute | solution.py:525
  54.4 0.0 collective-permute-done.4.north_part_hbm
  54.4 3.3 %shard_map.96 = (f32[2,8,8,2048]{3,2,1,0:T(8,128)S(1)}, f32[1,8,2048]{2,1,0:T(8,128)S(1)}, f32[1,8,2048]{2,1,0:T(8,128)}) custom-call(s32[1]{0:T(128)} %bitcast.lev_ref, f32[2,8,8,2048]{3,2,1,0:T(8,128)} %get-tuple-element.27.edge_hbm, f32[2,8,2048]{2,1,0:T(8,128)} %get-tuple-element.28.flow_hbm, f32[8,8,2048]{2,1,0:T(8,128)S(1)} %collective-permute-done.3.south_part_hbm, ...), custom_call_target="tpu_custom_call" | custom-call | tf_op jit(solution)/shard_map/pallas_call | solution.py:584
  57.7 0.0 copy-start.8
  57.7 0.6 copy-done.8
  58.3 0.5 collective-permute-start.9
  58.8 0.0 collective-permute-done.6
  58.8 1.3 %collective-permute-start.7 = (f32[1,8,2048]{2,1,0:T(8,128)S(1)}, f32[1,8,2048]{2,1,0:T(8,128)}, u32[]{:S(2)}, u32[]{:S(2)}) collective-permute-start(f32[1,8,2048]{2,1,0:T(8,128)S(1)} %add.21), channel_id=1, source_target_pairs={{64,128},{80,144},{96,160},{112,176},{128,192},{144,208},{160,224}... | collective-permute-start | bytes 196616 | tf_op jit(solution)/shard_map/ppermute | solution.py:579
  60.1 1.3 %collective-permute-start.8 = (f32[1,8,2048]{2,1,0:T(8,128)S(1)}, f32[1,8,2048]{2,1,0:T(8,128)}, u32[]{:S(2)}, u32[]{:S(2)}) collective-permute-start(f32[1,8,2048]{2,1,0:T(8,128)S(1)} %add.21), channel_id=1, source_target_pairs={{64,192},{80,208},{96,224},{112,240},{128,64},{144,80},{160,96},{1... | collective-permute-start | bytes 196616 | tf_op jit(solution)/shard_map/ppermute | solution.py:579
  61.4 0.0 copy-done.7
  61.4 0.0 copy-done.9
  61.4 0.0 copy-done.10
  61.4 1.3 %shard_map.98 = f32[16,24,128]{2,1,0:T(8,128)} custom-call(s32[1]{0:T(128)} %bitcast.14.lat_ref, s32[16]{0:T(128)S(1)} %bitcast.27, f32[16,16,128]{2,1,0:T(8,128)S(1)} %bitcast.25, s32[16,16]{1,0:T(8,128)S(1)} %bitcast.26), custom_call_target="tpu_custom_call" | custom-call | tf_op jit(solution)/shard_map/pallas_call | solution.py:528
  62.7 10.1 %all-to-all-start = ((f32[16,24,128]{2,1,0:T(8,128)}), f32[16,24,128]{2,1,0:T(8,128)S(1)}, u32[]{:S(2)}, u32[]{:S(2)}) async-start(f32[16,24,128]{2,1,0:T(8,128)} %shard_map.98), calls=%async_computation | async-start | bytes 393216 | tf_op jit(solution)/shard_map/all_to_all | solution.py:536
  72.8 0.4 collective-permute-start.5
  73.2 0.2 collective-permute-start.2
  73.4 0.0 collective-permute-done.9
  73.4 0.9 add.24
  74.3 0.7 collective-permute-start.10
  74.9 0.0 collective-permute-done.7
  75.0 0.7 collective-permute-start.11
  75.6 0.0 collective-permute-done.8
  75.6 0.9 add_add_fusion.1
  76.5 0.0 copy-start.11
  76.5 0.0 collective-permute-done.10
  76.6 0.0 collective-permute-done.11
  76.6 0.0 copy-start.12
  76.6 0.7 pad_maximum_fusion
  77.3 0.0 copy-done.11
  77.3 0.0 copy-done.12
  77.3 1.3 %collective-permute-start.12 = (f32[2,8,2048]{2,1,0:T(8,128)}, f32[2,8,2048]{2,1,0:T(8,128)}, u32[]{:S(2)}, u32[]{:S(2)}) collective-permute-start(f32[2,8,2048]{2,1,0:T(8,128)} %pad_maximum_fusion), channel_id=1, source_target_pairs={{64,96},{80,112},{96,64},{112,80},{128,160},{144,176},{160,128},{1... | collective-permute-start | bytes 393224 | tf_op jit(solution)/shard_map/ppermute | solution.py:600
  78.6 4.3 %all-to-all-done.packed_ref = f32[16,24,128]{2,1,0:T(8,128)S(1)} async-done(((f32[16,24,128]{2,1,0:T(8,128)}), f32[16,24,128]{2,1,0:T(8,128)S(1)}, u32[]{:S(2)}, u32[]{:S(2)}) %all-to-all-start) | async-done | bytes 196640 | tf_op jit(solution)/shard_map/all_to_all | solution.py:536
  82.9 1.4 %shard_map.99 = f32[16,8,512]{2,1,0:T(8,128)} custom-call(f32[16,24,128]{2,1,0:T(8,128)S(1)} %all-to-all-done.packed_ref), custom_call_target="tpu_custom_call" | custom-call | tf_op jit(solution)/shard_map/pallas_call | solution.py:538
  84.3 17.2 %all-to-all-start.1 = ((f32[16,8,512]{2,1,0:T(8,128)}), f32[16,8,512]{2,1,0:T(8,128)S(1)}, u32[]{:S(2)}, u32[]{:S(2)}) async-start(f32[16,8,512]{2,1,0:T(8,128)} %shard_map.99), calls=%async_computation.1 | async-start | bytes 524288 | tf_op jit(solution)/shard_map/all_to_all | solution.py:541
  101.5 0.0 collective-permute-done.12
  101.5 1.6 %fusion.own_ref = f32[2,8,2048]{2,1,0:T(8,128)} fusion(f32[2,8,2048]{2,1,0:T(8,128)} %collective-permute-done.12, f32[1,8,2048]{2,1,0:T(8,128)} %copy-done.12, f32[1,8,2048]{2,1,0:T(8,128)} %copy-done.11), kind=kLoop, calls=%fused_computation.3 | loop fusion | flops 65536 | bytes 393216 | tf_op jit(solution)/shard_map/add | solution.py:600
  103.1 0.1 collective-permute-start.13
  103.3 0.9 copy-done.6
  104.2 0.8 shard_map.94
  105.1 0.7 copy-done.4
  105.7 0.0 collective-permute-done.5.other_ref
  105.7 1.0 copy-done.1
  106.7 1.2 %copy-done.2 = f32[2,8,8,2048]{3,2,1,0:T(8,128)S(1)} copy-done((f32[2,8,8,2048]{3,2,1,0:T(8,128)S(1)}, f32[2,8,8,2048]{3,2,1,0:T(8,128)}, u32[]{:S(2)}) %copy-start.2) | copy-done | bytes 1048600
  107.9 0.5 shard_map.97.edge_ref
  108.5 0.0 collective-permute-done.2.other_hbm
  108.5 1.8 %shard_map.95.mid_ref = f32[2,8,8,2048]{3,2,1,0:T(8,128)S(1)} custom-call(s32[1]{0:T(128)} %bitcast.lev_ref, f32[2,8,8,2048]{3,2,1,0:T(8,128)} %get-tuple-element.25.adv_hbm, f32[2,8,8,2048]{3,2,1,0:T(8,128)S(1)} %collective-permute-done.2.other_hbm, s32[2,4,2048]{2,1,0:T(4,128)S(1)} %copy-done, f32[4,2048]{1,0:T(4,128)S(1)} %copy-done.3, ...), custom_call_target="tpu_custom_call" | custom-call | tf_op jit(solution)/shard_map/pallas_call | solution.py:602
  110.3 0.0 all-to-all-done.1.forcing_ref
  110.3 0.0 collective-permute-done.13.other_ref
  110.3 0.9 copy-done.5
  111.3 2.4 %shard_map.100 = f32[8,512,128]{2,1,0:T(8,128)} custom-call(s32[1]{0:T(128)} %bitcast.lev_ref, f32[2,8,8,2048]{3,2,1,0:T(8,128)S(1)} %shard_map.95.mid_ref, f32[2,8,8,2048]{3,2,1,0:T(8,128)S(1)} %shard_map.97.edge_ref, f32[4,8,2048]{2,1,0:T(8,128)S(1)} %copy-done.5, f32[2,8,2048]{2,1,0:T(8,128)} %fusion.own_ref, ...), custom_call_target="tpu_custom_call" | custom-call | tf_op jit(solution)/shard_map/pallas_call | solution.py:618
  (10 shorter events, 0.0 us)
Async XLA Ops:
  0.0 43.2 %copy-start = (s32[2,4,2048]{2,1,0:T(4,128)S(1)}, s32[2,4,2048]{2,1,0:T(4,128)}, u32[]{:S(2)}) copy-start(s32[2,4,2048]{2,1,0:T(4,128)} %band_ref.9) | copy-start | bytes 196612
  2.5 40.7 %collective-permute-start.1 = (f32[9,8,2048]{2,1,0:T(8,128)}, f32[9,8,2048]{2,1,0:T(8,128)S(1)}, u32[]{:S(2)}, u32[]{:S(2)}) collective-permute-start(f32[9,8,2048]{2,1,0:T(8,128)} %get-tuple-element.23), channel_id=1, source_target_pairs={{1,0},{2,1},{3,2},{4,3},{5,4},{6,5},{7,6},{8,7},{9,8},{10,9},{11,1... | collective-permute-start | bytes 1769480 | tf_op jit(solution)/shard_map/ppermute | solution.py:524
  3.8 39.4 %collective-permute-start = (f32[8,8,2048]{2,1,0:T(8,128)}, f32[8,8,2048]{2,1,0:T(8,128)S(1)}, u32[]{:S(2)}, u32[]{:S(2)}) collective-permute-start(f32[8,8,2048]{2,1,0:T(8,128)} %get-tuple-element.22.own_last_hbm), channel_id=1, source_target_pairs={{0,1},{1,2},{2,3},{3,4},{4,5},{5,6},{6,7},{7,8},{8,9},{9,10},{10,1... | collective-permute-start | bytes 1572872 | tf_op jit(solution)/shard_map/ppermute | solution.py:523
  12.5 41.9 %collective-permute-start.3 = (f32[8,8,2048]{2,1,0:T(8,128)}, f32[8,8,2048]{2,1,0:T(8,128)S(1)}, u32[]{:S(2)}, u32[]{:S(2)}) collective-permute-start(f32[8,8,2048]{2,1,0:T(8,128)} %get-tuple-element.29), channel_id=1, source_target_pairs={{0,1},{1,2},{2,3},{3,4},{4,5},{5,6},{6,7},{7,8},{8,9},{9,10},{10,1... | collective-permute-start | bytes 1572872 | tf_op jit(solution)/shard_map/ppermute | solution.py:525
  16.8 37.6 %collective-permute-start.4 = (f32[8,8,2048]{2,1,0:T(8,128)}, f32[8,8,2048]{2,1,0:T(8,128)S(1)}, u32[]{:S(2)}, u32[]{:S(2)}) collective-permute-start(f32[8,8,2048]{2,1,0:T(8,128)} %get-tuple-element.30), channel_id=1, source_target_pairs={{1,0},{2,1},{3,2},{4,3},{5,4},{6,5},{7,6},{8,7},{9,8},{10,9},{11,1... | collective-permute-start | bytes 1572872 | tf_op jit(solution)/shard_map/ppermute | solution.py:526
  47.3 14.1 %copy-start.7 = (f32[1,1,16,16,128]{4,3,2,1,0:T(8,128)S(1)}, f32[1,1,16,16,128]{4,3,2,1,0:T(8,128)}, u32[]{:S(2)}) copy-start(f32[1,1,16,16,128]{4,3,2,1,0:T(8,128)} %param.15) | copy-start | bytes 393220
  47.3 14.1 %copy-start.9 = (s32[1,1,16,16]{3,2,1,0:T(8,128)S(1)}, s32[1,1,16,16]{3,2,1,0:T(8,128)}, u32[]{:S(2)}) copy-start(s32[1,1,16,16]{3,2,1,0:T(8,128)} %param.16) | copy-start | bytes 3076
  47.3 14.1 %copy-start.10 = (s32[1,1,16]{2,1,0:T(1,128)S(1)}, s32[1,1,16]{2,1,0:T(1,128)}, u32[]{:S(2)}) copy-start(s32[1,1,16]{2,1,0:T(1,128)} %param.17) | copy-start | bytes 196
  47.3 11.5 %collective-permute-start.6 = (f32[1,8,2048]{2,1,0:T(8,128)S(1)}, f32[1,8,2048]{2,1,0:T(8,128)S(1)}, u32[]{:S(2)}, u32[]{:S(2)}) collective-permute-start(f32[1,8,2048]{2,1,0:T(8,128)S(1)} %get-tuple-element.34), channel_id=1, source_target_pairs={{0,16},{16,0},{32,48},{48,32},{64,80},{80,64},{96,112},{112,96},{1... | collective-permute-start | bytes 196616 | tf_op jit(solution)/shard_map/ppermute | solution.py:572
  57.7 0.6 copy-start.8
  58.3 44.9 %copy-start.3 = (f32[4,2048]{1,0:T(4,128)S(1)}, f32[4,2048]{1,0:T(4,128)}, u32[]{:S(2)}) copy-start(f32[4,2048]{1,0:T(4,128)} %flux_ref.5) | copy-start | bytes 98308
  58.3 15.1 %collective-permute-start.9 = (f32[1,8,2048]{2,1,0:T(8,128)}, f32[1,8,2048]{2,1,0:T(8,128)}, u32[]{:S(2)}, u32[]{:S(2)}) collective-permute-start(f32[1,8,2048]{2,1,0:T(8,128)} %get-tuple-element.36), channel_id=1, source_target_pairs={{0,16},{16,0},{32,48},{48,32},{64,80},{80,64},{96,112},{112,96},{1... | collective-permute-start | bytes 196616 | tf_op jit(solution)/shard_map/ppermute | solution.py:572
  58.8 16.1 %collective-permute-start.7 = (f32[1,8,2048]{2,1,0:T(8,128)S(1)}, f32[1,8,2048]{2,1,0:T(8,128)}, u32[]{:S(2)}, u32[]{:S(2)}) collective-permute-start(f32[1,8,2048]{2,1,0:T(8,128)S(1)} %add.21), channel_id=1, source_target_pairs={{64,128},{80,144},{96,160},{112,176},{128,192},{144,208},{160,224}... | collective-permute-start | bytes 196616 | tf_op jit(solution)/shard_map/ppermute | solution.py:579
  60.1 15.5 %collective-permute-start.8 = (f32[1,8,2048]{2,1,0:T(8,128)S(1)}, f32[1,8,2048]{2,1,0:T(8,128)}, u32[]{:S(2)}, u32[]{:S(2)}) collective-permute-start(f32[1,8,2048]{2,1,0:T(8,128)S(1)} %add.21), channel_id=1, source_target_pairs={{64,192},{80,208},{96,224},{112,240},{128,64},{144,80},{160,96},{1... | collective-permute-start | bytes 196616 | tf_op jit(solution)/shard_map/ppermute | solution.py:579
  62.7 20.2 %all-to-all-start = ((f32[16,24,128]{2,1,0:T(8,128)}), f32[16,24,128]{2,1,0:T(8,128)S(1)}, u32[]{:S(2)}, u32[]{:S(2)}) async-start(f32[16,24,128]{2,1,0:T(8,128)} %shard_map.98), calls=%async_computation | async-start | bytes 393216 | tf_op jit(solution)/shard_map/all_to_all | solution.py:536
  72.8 33.0 %collective-permute-start.5 = (f32[2,8,8,2048]{3,2,1,0:T(8,128)S(1)}, f32[2,8,8,2048]{3,2,1,0:T(8,128)S(1)}, u32[]{:S(2)}, u32[]{:S(2)}) collective-permute-start(f32[2,8,8,2048]{3,2,1,0:T(8,128)S(1)} %get-tuple-element.31.adv_ref), channel_id=1, source_target_pairs={{0,16},{16,0},{32,48},{48,32},{64,80},{80,64},{96,112},{112,96},{1... | collective-permute-start | bytes 3145736 | tf_op jit(solution)/shard_map/ppermute | solution.py:596
  73.2 35.3 %collective-permute-start.2 = (f32[2,8,8,2048]{3,2,1,0:T(8,128)}, f32[2,8,8,2048]{3,2,1,0:T(8,128)S(1)}, u32[]{:S(2)}, u32[]{:S(2)}) collective-permute-start(f32[2,8,8,2048]{3,2,1,0:T(8,128)} %get-tuple-element.25.adv_hbm), channel_id=1, source_target_pairs={{0,16},{16,0},{32,48},{48,32},{64,80},{80,64},{96,112},{112,96},{1... | collective-permute-start | bytes 3145736 | tf_op jit(solution)/shard_map/ppermute | solution.py:597
  74.3 2.3 %collective-permute-start.10 = (f32[1,8,2048]{2,1,0:T(8,128)S(1)}, f32[1,8,2048]{2,1,0:T(8,128)S(1)}, u32[]{:S(2)}, u32[]{:S(2)}) collective-permute-start(f32[1,8,2048]{2,1,0:T(8,128)S(1)} %add.24), channel_id=1, source_target_pairs={{64,128},{80,144},{96,160},{112,176},{128,192},{144,208},{160,224}... | collective-permute-start | bytes 196616 | tf_op jit(solution)/shard_map/ppermute | solution.py:579
  75.0 1.6 %collective-permute-start.11 = (f32[1,8,2048]{2,1,0:T(8,128)S(1)}, f32[1,8,2048]{2,1,0:T(8,128)S(1)}, u32[]{:S(2)}, u32[]{:S(2)}) collective-permute-start(f32[1,8,2048]{2,1,0:T(8,128)S(1)} %add.24), channel_id=1, source_target_pairs={{64,192},{80,208},{96,224},{112,240},{128,64},{144,80},{160,96},{1... | collective-permute-start | bytes 196616 | tf_op jit(solution)/shard_map/ppermute | solution.py:579
  76.5 0.7 copy-start.11
  76.6 0.7 copy-start.12
  77.3 24.3 %collective-permute-start.12 = (f32[2,8,2048]{2,1,0:T(8,128)}, f32[2,8,2048]{2,1,0:T(8,128)}, u32[]{:S(2)}, u32[]{:S(2)}) collective-permute-start(f32[2,8,2048]{2,1,0:T(8,128)} %pad_maximum_fusion), channel_id=1, source_target_pairs={{64,96},{80,112},{96,64},{112,80},{128,160},{144,176},{160,128},{1... | collective-permute-start | bytes 393224 | tf_op jit(solution)/shard_map/ppermute | solution.py:600
  84.3 26.0 %all-to-all-start.1 = ((f32[16,8,512]{2,1,0:T(8,128)}), f32[16,8,512]{2,1,0:T(8,128)S(1)}, u32[]{:S(2)}, u32[]{:S(2)}) async-start(f32[16,8,512]{2,1,0:T(8,128)} %shard_map.99), calls=%async_computation.1 | async-start | bytes 524288 | tf_op jit(solution)/shard_map/all_to_all | solution.py:541
  103.1 7.2 %collective-permute-start.13 = (f32[2,8,2048]{2,1,0:T(8,128)}, f32[2,8,2048]{2,1,0:T(8,128)}, u32[]{:S(2)}, u32[]{:S(2)}) collective-permute-start(f32[2,8,2048]{2,1,0:T(8,128)} %fusion.own_ref), channel_id=1, source_target_pairs={{0,16},{16,0},{32,48},{48,32},{64,80},{80,64},{96,112},{112,96},{1... | collective-permute-start | bytes 393224 | tf_op jit(solution)/shard_map/ppermute | solution.py:601
  103.3 1.0 copy-start.6
  105.0 0.7 copy-start.4
  105.7 1.0 copy-start.1
  106.7 1.2 %copy-start.2 = (f32[2,8,8,2048]{3,2,1,0:T(8,128)S(1)}, f32[2,8,8,2048]{3,2,1,0:T(8,128)}, u32[]{:S(2)}) copy-start(f32[2,8,8,2048]{3,2,1,0:T(8,128)} %copy-done.1) | copy-start | bytes 3145732
  110.3 1.0 copy-start.5

commit v6 on v3

--- a/solution.py
+++ b/solution.py
@@ -93,15 +93,9 @@
             coef_ref[4, r, :, s] = center
 
 
-def edge_kernel(a_hbm, last_hbm, first_hbm, a_ref, last_ref, first_ref, sems):
+def edge_kernel(a_hbm, last_ref, first_ref, a_ref, sems):
     def incoming(t):
-        return pltpu.make_async_copy(a_hbm.at[t], a_ref.at[t], sems.at[t, 0])
-
-    def outgoing(t):
-        return [
-            pltpu.make_async_copy(last_ref.at[t], last_hbm.at[t], sems.at[t, 1]),
-            pltpu.make_async_copy(first_ref.at[t], first_hbm.at[t], sems.at[t, 2]),
-        ]
+        return pltpu.make_async_copy(a_hbm.at[t], a_ref.at[t], sems.at[t])
 
     @pl.loop(0, 8)
     def _(t):
@@ -115,13 +109,6 @@
             for half in range(2):
                 first_ref[t, :, lane_slice(2 * k + half)] = tiles[4 * half]
                 last_ref[t, :, lane_slice(2 * k + half)] = tiles[4 * half + 3]
-        for copy in outgoing(t):
-            copy.start()
-
-    @pl.loop(0, 8)
-    def _(t):
-        for copy in outgoing(t):
-            copy.wait()
 
 
 def prep_kernel(
@@ -186,22 +173,23 @@
 
 
 def advect_kernel(
-    lev_ref, part_hbm, own_last_hbm, own_first_hbm, own_face_hbm, south_row_ref, south_part_ref, north_row_ref, north_part_ref,
-    coef_hbm, band_ref, adv_ref, keep_ref, send_ref,
-    edge_ref, sum_ref, inside_ref, part_ref, own_last_ref, own_first_ref, coef_ref, sems,
+    lev_ref, part_hbm, own_last_ref, own_first_ref, own_face_hbm, south_row_ref, south_part_hbm, north_row_ref, north_part_ref,
+    coef_hbm, band_hbm, adv_ref, keep_ref, send_ref,
+    edge_ref, sum_ref, inside_ref, part_ref, south_part_ref, own_face_ref, coef_ref, band_ref, sems,
 ):
     tiles = range(16)
 
     def copies(t):
         return [
             pltpu.make_async_copy(part_hbm.at[t], part_ref.at[t], sems.at[t, 0]),
-            pltpu.make_async_copy(own_last_hbm.at[t], own_last_ref.at[t], sems.at[t, 1]),
-            pltpu.make_async_copy(own_first_hbm.at[t], own_first_ref.at[t], sems.at[t, 2]),
+            pltpu.make_async_copy(south_part_hbm.at[t], south_part_ref.at[t], sems.at[t, 1]),
         ]
 
+    band_copy = pltpu.make_async_copy(band_hbm, band_ref, sems.at[8, 2])
+    band_copy.start()
     fixed = [
         pltpu.make_async_copy(coef_hbm, coef_ref, sems.at[8, 0]),
-        pltpu.make_async_copy(own_face_hbm.at[8], own_first_ref.at[8], sems.at[8, 1]),
+        pltpu.make_async_copy(own_face_hbm.at[8], own_face_ref, sems.at[8, 1]),
     ]
     for copy in fixed:
         copy.start()
@@ -211,6 +199,7 @@
         for copy in copies(t):
             copy.start()
 
+    band_copy.wait()
     level = lax.broadcasted_iota(jnp.int32, (8, 2048), 0) + lev_ref[0] * 8
     for r in range(4):
         first = band_ref[0, r : r + 1, :]
@@ -220,7 +209,7 @@
     for copy in fixed:
         copy.wait()
     north_face = jnp.maximum(north_part_ref[8], 0.0)
-    edge_ref[0] = jnp.maximum(own_first_ref[8], 0.0)
+    edge_ref[0] = jnp.maximum(own_face_ref[...], 0.0)
     edge_ref[1] = jnp.minimum(north_part_ref[8], 0.0)
     edge_ref[2] = north_face
     edge_ref[3] = coef_ref[4, 3] - north_face
@@ -410,12 +399,9 @@
     last_row, first_row = pl.pallas_call(
         edge_kernel,
         in_specs=[hbm],
-        out_specs=[hbm] * 2,
-        out_shape=[far(8, 8, lons), far(8, 8, lons)],
-        scratch_shapes=[
-            pltpu.VMEM((8, 512, LANES), F32), pltpu.VMEM((8, 8, lons), F32), pltpu.VMEM((8, 8, lons), F32),
-            pltpu.SemaphoreType.DMA((8, 3)),
-        ],
+        out_specs=[vmem] * 2,
+        out_shape=[shape(8, 8, lons), shape(8, 8, lons)],
+        scratch_shapes=[pltpu.VMEM((8, 512, LANES), F32), pltpu.SemaphoreType.DMA((8,))],
         compiler_params=small,
     )(keep_far(a_view))
     part, to_north, to_south, coef = pl.pallas_call(
@@ -462,17 +448,18 @@
 
     adv, keep, send = pl.pallas_call(
         advect_kernel,
-        in_specs=[smem] + [hbm] * 4 + [vmem] * 4 + [hbm, vmem],
+        in_specs=[smem, hbm, vmem, vmem, hbm, vmem, hbm, vmem, vmem, hbm, hbm],
         out_specs=[vmem] * 3,
         out_shape=[shape(4, 8, 8, lons), shape(2, 8, lons), shape(2, 8, lons)],
         scratch_shapes=[
             row_scratch, row_scratch, row_scratch, pltpu.VMEM((8, 4, 8, lons), F32), pltpu.VMEM((8, 8, lons), F32),
-            pltpu.VMEM((9, 8, lons), F32), pltpu.VMEM((5, 4, 8, lons), F32), pltpu.SemaphoreType.DMA((9, 3)),
+            pltpu.VMEM((8, lons), F32), pltpu.VMEM((5, 4, 8, lons), F32), pltpu.VMEM((2, 4, lons), jnp.int32),
+            pltpu.SemaphoreType.DMA((9, 3)),
         ],
         compiler_params=small,
     )(
-        lev, keep_far(part), keep_far(last_row), keep_far(first_row), keep_far(to_south),
-        south_row, south_part, north_row, north_part, keep_far(coef), conv_band,
+        lev, keep_far(part), last_row, first_row, keep_far(to_south),
+        south_row, south_part, north_row, north_part, keep_far(coef), keep_far(conv_band),
     )
 
     swap = [(i, i ^ 1) for i in range(lev_count)]

time: 116 us -> 118 us (1.017)
  local copies, waits for them, and re-layouts: 5.3 us -> 8.93 us
    unnamed x24 -> x32, local copies, waits for them, and re-layouts: 5.3 us -> 8.93 us
where the time goes in v6:
time: 118 us; the launch traced here: 117 us
  waiting for transfers between devices  53.3 us (45%)
  starting transfers between devices  37.3 us (32%)
  Pallas kernels  17.2 us (15%)
  local copies, waits for them, and re-layouts  8.93 us (8%)
    ppermute x1, waiting for transfers between devices, body(): south_part = lax.ppermute(to_north, 'lat', north)  26 us
    all_to_all x1, starting transfers between devices, body(): lax.all_to_all(forcing, 'lev', split_axis=0, concat_axis=0, tiled=True)  12.8 us
    ppermute x1, waiting for transfers between devices, body(): south_row = lax.ppermute(last_row, 'lat', north)  11.1 us
    all_to_all x1, starting transfers between devices, body(): lax.all_to_all(packed, 'lat', split_axis=0, concat_axis=0, tiled=True)  10.2 us
    unnamed x32, local copies, waits for them, and re-layouts  8.93 us
    all_to_all x1, waiting for transfers between devices, body(): lax.all_to_all(packed, 'lat', split_axis=0, concat_axis=0, tiled=True)  8.87 us
    ppermute x1, starting transfers between devices, body(): south_part = lax.ppermute(to_north, 'lat', north)  4.59 us
    ppermute x1, starting transfers between devices, body(): south_row = lax.ppermute(last_row, 'lat', north)  4.26 us
  transfers between devices with their start and end apart: 12, of which 5 were waited for; matrix products, arithmetic and copies ran while one was open for 0% of the time, Pallas kernels for 7%

profile of v6, /device:TPU:1, one launch (start us, length us, event | category | flops | bytes accessed | tf_op | source)
XLA Modules:
  0.0 117.1 jit_solution(14931333601441654490)
XLA Ops:
  0.0 4.1 %shard_map.91 = (f32[8,4,8,2048]{3,2,1,0:T(8,128)}, f32[8,8,2048]{2,1,0:T(8,128)}, f32[9,8,2048]{2,1,0:T(8,128)}, f32[5,4,8,2048]{3,2,1,0:T(8,128)}) custom-call(f32[8,512,128]{2,1,0:T(8,128)} %bitcast.30, f32[512,128]{1,0:T(8,128)} %bitcast.32, f32[512,128]{1,0:T(8,128)} %bitcast.33), custom_call_target="tpu_custom_call" | custom-call | tf_op jit(solution)/shard_map/pallas_call | solution.py:407
  4.1 1.3 %collective-permute-start.3 = (f32[9,8,2048]{2,1,0:T(8,128)}, f32[9,8,2048]{2,1,0:T(8,128)S(1)}, u32[]{:S(2)}, u32[]{:S(2)}) collective-permute-start(f32[9,8,2048]{2,1,0:T(8,128)} %get-tuple-element.19.own_face_hbm), channel_id=1, source_target_pairs={{1,0},{2,1},{3,2},{4,3},{5,4},{6,5},{7,6},{8,7},{9,8},{10,9},{11,1... | collective-permute-start | bytes 1769480 | tf_op jit(solution)/shard_map/ppermute | solution.py:424
  5.4 4.6 %collective-permute-start.1 = (f32[8,8,2048]{2,1,0:T(8,128)}, f32[8,8,2048]{2,1,0:T(8,128)S(1)}, u32[]{:S(2)}, u32[]{:S(2)}) collective-permute-start(f32[8,8,2048]{2,1,0:T(8,128)} %get-tuple-element.20), channel_id=1, source_target_pairs={{0,1},{1,2},{2,3},{3,4},{4,5},{5,6},{6,7},{7,8},{8,9},{9,10},{10,1... | collective-permute-start | bytes 1572872 | tf_op jit(solution)/shard_map/ppermute | solution.py:423
  10.0 1.6 %shard_map.92 = (f32[8,8,2048]{2,1,0:T(8,128)S(1)}, f32[8,8,2048]{2,1,0:T(8,128)S(1)}) custom-call(f32[8,512,128]{2,1,0:T(8,128)} %bitcast.31), custom_call_target="tpu_custom_call" | custom-call | tf_op jit(solution)/shard_map/pallas_call | solution.py:399
  11.7 4.3 %collective-permute-start = (f32[8,8,2048]{2,1,0:T(8,128)S(1)}, f32[8,8,2048]{2,1,0:T(8,128)S(1)}, u32[]{:S(2)}, u32[]{:S(2)}) collective-permute-start(f32[8,8,2048]{2,1,0:T(8,128)S(1)} %get-tuple-element.17.own_last_ref), channel_id=1, source_target_pairs={{0,1},{1,2},{2,3},{3,4},{4,5},{5,6},{6,7},{7,8},{8,9},{9,10},{10,1... | collective-permute-start | bytes 1572872 | tf_op jit(solution)/shard_map/ppermute | solution.py:421
  15.9 0.0 copy-start.3
  15.9 0.8 copy-done.3
  16.7 1.3 %collective-permute-start.2 = (f32[8,8,2048]{2,1,0:T(8,128)S(1)}, f32[8,8,2048]{2,1,0:T(8,128)S(1)}, u32[]{:S(2)}, u32[]{:S(2)}) collective-permute-start(f32[8,8,2048]{2,1,0:T(8,128)S(1)} %get-tuple-element.18.own_first_ref), channel_id=1, source_target_pairs={{1,0},{2,1},{3,2},{4,3},{5,4},{6,5},{7,6},{8,7},{9,8},{10,9},{11,1... | collective-permute-start | bytes 1572872 | tf_op jit(solution)/shard_map/ppermute | solution.py:422
  18.0 0.0 copy-start.5
  18.0 0.8 copy-done.5
  18.8 26.0 %collective-permute-done.1.south_part_hbm = f32[8,8,2048]{2,1,0:T(8,128)S(1)} collective-permute-done((f32[8,8,2048]{2,1,0:T(8,128)}, f32[8,8,2048]{2,1,0:T(8,128)S(1)}, u32[]{:S(2)}, u32[]{:S(2)}) %collective-permute-start.1) | collective-permute-done | bytes 524320 | tf_op jit(solution)/shard_map/ppermute | solution.py:423
  44.8 11.1 %collective-permute-done.south_row_ref = f32[8,8,2048]{2,1,0:T(8,128)S(1)} collective-permute-done((f32[8,8,2048]{2,1,0:T(8,128)S(1)}, f32[8,8,2048]{2,1,0:T(8,128)S(1)}, u32[]{:S(2)}, u32[]{:S(2)}) %collective-permute-start) | collective-permute-done | bytes 524320 | tf_op jit(solution)/shard_map/ppermute | solution.py:421
  55.9 0.0 copy-start.7
  55.9 0.8 copy-done.7
  56.7 0.0 collective-permute-done.2.north_row_ref
  56.7 0.0 copy-start.9
  56.7 0.8 copy-done.9
  57.5 0.0 collective-permute-done.3.north_part_ref
  57.5 0.0 copy-start.4
  57.5 1.0 copy-done.4
  58.5 0.0 copy-start.6
  58.5 1.0 copy-done.6
  59.6 0.0 copy-start.8
  59.6 1.0 copy-done.8
  60.6 0.0 copy-start.10
  60.6 1.0 copy-done.10
  61.7 0.0 copy-start.13
  61.7 0.0 copy-start.14
  61.7 0.0 copy-start.15
  61.7 3.9 %shard_map.93 = (f32[4,8,8,2048]{3,2,1,0:T(8,128)S(1)}, f32[2,8,2048]{2,1,0:T(8,128)S(1)}, f32[2,8,2048]{2,1,0:T(8,128)S(1)}) custom-call(s32[1]{0:T(128)} %bitcast.lev_ref, f32[8,4,8,2048]{3,2,1,0:T(8,128)} %get-tuple-element.16.part_hbm, f32[8,8,2048]{2,1,0:T(8,128)S(1)} %copy-done.4, f32[8,8,2048]{2,1,0:T(8,128)S(1)} %copy-done.6, ...), custom_call_target="tpu_custom_call" | custom-call | tf_op jit(solution)/shard_map/pallas_call | solution.py:449
  65.6 0.0 copy-start
  65.6 0.0 copy-start.2
  65.6 0.0 copy-start.11
  65.6 0.0 copy-start.12
  65.6 0.6 collective-permute-start.4
  66.2 0.1 collective-permute-start.5
  66.3 3.9 %collective-permute-done.5 = f32[2,8,2048]{2,1,0:T(8,128)S(1)} collective-permute-done((f32[2,8,2048]{2,1,0:T(8,128)S(1)}, f32[2,8,2048]{2,1,0:T(8,128)S(1)}, u32[]{:S(2)}, u32[]{:S(2)}) %collective-permute-start.5) | collective-permute-done | bytes 131104 | tf_op jit(solution)/shard_map/ppermute | solution.py:466
  70.2 0.7 collective-permute-start.6
  70.9 0.7 collective-permute-start.7
  71.5 0.0 copy-done.13
  71.5 0.0 copy-done.14
  71.6 0.0 copy-done.15
  71.6 1.3 %shard_map.96 = f32[16,24,128]{2,1,0:T(8,128)} custom-call(s32[1]{0:T(128)} %bitcast.13.lat_ref, s32[16]{0:T(128)S(1)} %bitcast.29, f32[16,16,128]{2,1,0:T(8,128)S(1)} %bitcast.27, s32[16,16]{1,0:T(8,128)S(1)} %bitcast.28), custom_call_target="tpu_custom_call" | custom-call | tf_op jit(solution)/shard_map/pallas_call | solution.py:426
  72.9 10.2 %all-to-all-start = ((f32[16,24,128]{2,1,0:T(8,128)}), f32[16,24,128]{2,1,0:T(8,128)S(1)}, u32[]{:S(2)}, u32[]{:S(2)}) async-start(f32[16,24,128]{2,1,0:T(8,128)} %shard_map.96), calls=%async_computation | async-start | bytes 393216 | tf_op jit(solution)/shard_map/all_to_all | solution.py:434
  83.1 0.0 collective-permute-done.6
  83.1 0.0 collective-permute-done.7
  83.1 0.7 collective-permute-start.8
  83.8 8.9 %all-to-all-done.packed_ref = f32[16,24,128]{2,1,0:T(8,128)S(1)} async-done(((f32[16,24,128]{2,1,0:T(8,128)}), f32[16,24,128]{2,1,0:T(8,128)S(1)}, u32[]{:S(2)}, u32[]{:S(2)}) %all-to-all-start) | async-done | bytes 196640 | tf_op jit(solution)/shard_map/all_to_all | solution.py:434
  92.7 1.4 %shard_map.97 = f32[16,8,512]{2,1,0:T(8,128)} custom-call(f32[16,24,128]{2,1,0:T(8,128)S(1)} %all-to-all-done.packed_ref), custom_call_target="tpu_custom_call" | custom-call | tf_op jit(solution)/shard_map/pallas_call | solution.py:436
  94.1 12.8 %all-to-all-start.1 = ((f32[16,8,512]{2,1,0:T(8,128)}), f32[16,8,512]{2,1,0:T(8,128)S(1)}, u32[]{:S(2)}, u32[]{:S(2)}) async-start(f32[16,8,512]{2,1,0:T(8,128)} %shard_map.97), calls=%async_computation.1 | async-start | bytes 524288 | tf_op jit(solution)/shard_map/all_to_all | solution.py:439
  106.9 0.0 collective-permute-done.8
  107.0 0.2 collective-permute-start.9
  107.1 0.0 copy-done.2
  107.1 0.0 copy-done.11
  107.1 0.0 copy-done.12
  107.2 0.8 shard_map.94
  108.0 0.0 collective-permute-done.4.other_ref
  108.0 0.0 copy-done
  108.0 0.0 copy-start.1
  108.0 1.6 %copy-done.1 = f32[4,8,8,2048]{3,2,1,0:T(8,128)S(1)} copy-done((f32[4,8,8,2048]{3,2,1,0:T(8,128)S(1)}, f32[4,8,8,2048]{3,2,1,0:T(8,128)}, u32[]{:S(2)}) %copy-start.1) | copy-done | bytes 2097176
  109.6 2.5 %shard_map.95 = f32[4,64,2048]{2,1,0:T(8,128)S(1)} custom-call(s32[1]{0:T(128)} %bitcast.lev_ref, f32[4,8,8,2048]{3,2,1,0:T(8,128)S(1)} %copy-done.1, f32[4,8,8,2048]{3,2,1,0:T(8,128)} %collective-permute-done.4.other_ref, s32[2,4,2048]{2,1,0:T(4,128)S(1)} %copy-done.2, f32[4,2048]{1,0:T(4,128)S(1)} %copy-done.12, ...), custom_call_target="tpu_custom_call" | custom-call | tf_op jit(solution)/shard_map/pallas_call | solution.py:483
  112.2 3.5 %all-to-all-done.1.forcing_ref = f32[16,8,512]{2,1,0:T(8,128)S(1)} async-done(((f32[16,8,512]{2,1,0:T(8,128)}), f32[16,8,512]{2,1,0:T(8,128)S(1)}, u32[]{:S(2)}, u32[]{:S(2)}) %all-to-all-start.1) | async-done | bytes 262176 | tf_op jit(solution)/shard_map/all_to_all | solution.py:439
  115.6 0.0 collective-permute-done.9.other_ref
  115.6 1.5 %shard_map.98 = f32[8,512,128]{2,1,0:T(8,128)} custom-call(s32[1]{0:T(128)} %bitcast.lev_ref, f32[4,8,8,2048]{3,2,1,0:T(8,128)S(1)} %bitcast.26, f32[4,8,2048]{2,1,0:T(8,128)S(1)} %get-tuple-element.24.gain_ref, f32[2,8,2048]{2,1,0:T(8,128)S(1)} %add.15.own_ref, f32[2,8,2048]{2,1,0:T(8,128)S(1)} %collective-permute-done.9.other_ref, ...), custom_call_target="tpu_custom_call" | custom-call | tf_op jit(solution)/shard_map/pallas_call | solution.py:491
  (3 shorter events, 0.1 us)
Async XLA Ops:
  4.1 53.4 %collective-permute-start.3 = (f32[9,8,2048]{2,1,0:T(8,128)}, f32[9,8,2048]{2,1,0:T(8,128)S(1)}, u32[]{:S(2)}, u32[]{:S(2)}) collective-permute-start(f32[9,8,2048]{2,1,0:T(8,128)} %get-tuple-element.19.own_face_hbm), channel_id=1, source_target_pairs={{1,0},{2,1},{3,2},{4,3},{5,4},{6,5},{7,6},{8,7},{9,8},{10,9},{11,1... | collective-permute-start | bytes 1769480 | tf_op jit(solution)/shard_map/ppermute | solution.py:424
  5.4 39.4 %collective-permute-start.1 = (f32[8,8,2048]{2,1,0:T(8,128)}, f32[8,8,2048]{2,1,0:T(8,128)S(1)}, u32[]{:S(2)}, u32[]{:S(2)}) collective-permute-start(f32[8,8,2048]{2,1,0:T(8,128)} %get-tuple-element.20), channel_id=1, source_target_pairs={{0,1},{1,2},{2,3},{3,4},{4,5},{5,6},{6,7},{7,8},{8,9},{9,10},{10,1... | collective-permute-start | bytes 1572872 | tf_op jit(solution)/shard_map/ppermute | solution.py:423
  11.7 44.2 %collective-permute-start = (f32[8,8,2048]{2,1,0:T(8,128)S(1)}, f32[8,8,2048]{2,1,0:T(8,128)S(1)}, u32[]{:S(2)}, u32[]{:S(2)}) collective-permute-start(f32[8,8,2048]{2,1,0:T(8,128)S(1)} %get-tuple-element.17.own_last_ref), channel_id=1, source_target_pairs={{0,1},{1,2},{2,3},{3,4},{4,5},{5,6},{6,7},{7,8},{8,9},{9,10},{10,1... | collective-permute-start | bytes 1572872 | tf_op jit(solution)/shard_map/ppermute | solution.py:421
  15.9 0.8 copy-start.3
  16.7 40.0 %collective-permute-start.2 = (f32[8,8,2048]{2,1,0:T(8,128)S(1)}, f32[8,8,2048]{2,1,0:T(8,128)S(1)}, u32[]{:S(2)}, u32[]{:S(2)}) collective-permute-start(f32[8,8,2048]{2,1,0:T(8,128)S(1)} %get-tuple-element.18.own_first_ref), channel_id=1, source_target_pairs={{1,0},{2,1},{3,2},{4,3},{5,4},{6,5},{7,6},{8,7},{9,8},{10,9},{11,1... | collective-permute-start | bytes 1572872 | tf_op jit(solution)/shard_map/ppermute | solution.py:422
  18.0 0.8 copy-start.5
  55.9 0.8 copy-start.7
  56.7 0.8 copy-start.9
  57.5 1.0 copy-start.4
  58.5 1.0 copy-start.6
  59.6 1.0 copy-start.8
  60.6 1.0 copy-start.10
  61.7 9.9 %copy-start.13 = (f32[1,1,16,16,128]{4,3,2,1,0:T(8,128)S(1)}, f32[1,1,16,16,128]{4,3,2,1,0:T(8,128)}, u32[]{:S(2)}) copy-start(f32[1,1,16,16,128]{4,3,2,1,0:T(8,128)} %param.15) | copy-start | bytes 393220
  61.7 9.9 %copy-start.14 = (s32[1,1,16,16]{3,2,1,0:T(8,128)S(1)}, s32[1,1,16,16]{3,2,1,0:T(8,128)}, u32[]{:S(2)}) copy-start(s32[1,1,16,16]{3,2,1,0:T(8,128)} %param.16) | copy-start | bytes 3076
  61.7 9.9 %copy-start.15 = (s32[1,1,16]{2,1,0:T(1,128)S(1)}, s32[1,1,16]{2,1,0:T(1,128)}, u32[]{:S(2)}) copy-start(s32[1,1,16]{2,1,0:T(1,128)} %param.17) | copy-start | bytes 196
  65.6 42.5 %copy-start = (f32[4,8,8,2048]{3,2,1,0:T(8,128)}, f32[4,8,8,2048]{3,2,1,0:T(8,128)S(1)}, u32[]{:S(2)}) copy-start(f32[4,8,8,2048]{3,2,1,0:T(8,128)S(1)} %get-tuple-element.22.adv_ref) | copy-start | bytes 6291460
  65.6 41.6 %copy-start.2 = (s32[2,4,2048]{2,1,0:T(4,128)S(1)}, s32[2,4,2048]{2,1,0:T(4,128)}, u32[]{:S(2)}) copy-start(s32[2,4,2048]{2,1,0:T(4,128)} %band_ref.3) | copy-start | bytes 196612
  65.6 41.6 %copy-start.11 = (f32[4,8,16,16]{3,2,1,0:T(8,128)S(1)}, f32[4,8,16,16]{3,2,1,0:T(8,128)}, u32[]{:S(2)}) copy-start(f32[4,8,16,16]{3,2,1,0:T(8,128)} %inv_ref.1) | copy-start | bytes 98308
  65.6 41.6 %copy-start.12 = (f32[4,2048]{1,0:T(4,128)S(1)}, f32[4,2048]{1,0:T(4,128)}, u32[]{:S(2)}) copy-start(f32[4,2048]{1,0:T(4,128)} %flux_ref.3) | copy-start | bytes 98308
  65.6 42.4 %collective-permute-start.4 = (f32[4,8,8,2048]{3,2,1,0:T(8,128)S(1)}, f32[4,8,8,2048]{3,2,1,0:T(8,128)}, u32[]{:S(2)}, u32[]{:S(2)}) collective-permute-start(f32[4,8,8,2048]{3,2,1,0:T(8,128)S(1)} %get-tuple-element.22.adv_ref), channel_id=1, source_target_pairs={{0,16},{16,0},{32,48},{48,32},{64,80},{80,64},{96,112},{112,96},{1... | collective-permute-start | bytes 6291464 | tf_op jit(solution)/shard_map/ppermute | solution.py:478
  66.2 4.0 %collective-permute-start.5 = (f32[2,8,2048]{2,1,0:T(8,128)S(1)}, f32[2,8,2048]{2,1,0:T(8,128)S(1)}, u32[]{:S(2)}, u32[]{:S(2)}) collective-permute-start(f32[2,8,2048]{2,1,0:T(8,128)S(1)} %get-tuple-element.26), channel_id=1, source_target_pairs={{0,16},{16,0},{32,48},{48,32},{64,80},{80,64},{96,112},{112,96},{1... | collective-permute-start | bytes 393224 | tf_op jit(solution)/shard_map/ppermute | solution.py:466
  70.2 12.9 %collective-permute-start.6 = (f32[2,8,2048]{2,1,0:T(8,128)S(1)}, f32[2,8,2048]{2,1,0:T(8,128)S(1)}, u32[]{:S(2)}, u32[]{:S(2)}) collective-permute-start(f32[2,8,2048]{2,1,0:T(8,128)S(1)} %add.12), channel_id=1, source_target_pairs={{64,128},{80,144},{96,160},{112,176},{128,192},{144,208},{160,224}... | collective-permute-start | bytes 393224 | tf_op jit(solution)/shard_map/ppermute | solution.py:476
  70.9 12.2 %collective-permute-start.7 = (f32[2,8,2048]{2,1,0:T(8,128)S(1)}, f32[2,8,2048]{2,1,0:T(8,128)S(1)}, u32[]{:S(2)}, u32[]{:S(2)}) collective-permute-start(f32[2,8,2048]{2,1,0:T(8,128)S(1)} %add.12), channel_id=1, source_target_pairs={{64,192},{80,208},{96,224},{112,240},{128,64},{144,80},{160,96},{1... | collective-permute-start | bytes 393224 | tf_op jit(solution)/shard_map/ppermute | solution.py:476
  72.9 19.8 %all-to-all-start = ((f32[16,24,128]{2,1,0:T(8,128)}), f32[16,24,128]{2,1,0:T(8,128)S(1)}, u32[]{:S(2)}, u32[]{:S(2)}) async-start(f32[16,24,128]{2,1,0:T(8,128)} %shard_map.96), calls=%async_computation | async-start | bytes 393216 | tf_op jit(solution)/shard_map/all_to_all | solution.py:434
  83.1 23.8 %collective-permute-start.8 = (f32[2,8,2048]{2,1,0:T(8,128)S(1)}, f32[2,8,2048]{2,1,0:T(8,128)S(1)}, u32[]{:S(2)}, u32[]{:S(2)}) collective-permute-start(f32[2,8,2048]{2,1,0:T(8,128)S(1)} %add_add_fusion), channel_id=1, source_target_pairs={{64,96},{80,112},{96,64},{112,80},{128,160},{144,176},{160,128},{1... | collective-permute-start | bytes 393224 | tf_op jit(solution)/shard_map/ppermute | solution.py:480
  94.1 21.5 %all-to-all-start.1 = ((f32[16,8,512]{2,1,0:T(8,128)}), f32[16,8,512]{2,1,0:T(8,128)S(1)}, u32[]{:S(2)}, u32[]{:S(2)}) async-start(f32[16,8,512]{2,1,0:T(8,128)} %shard_map.97), calls=%async_computation.1 | async-start | bytes 524288 | tf_op jit(solution)/shard_map/all_to_all | solution.py:439
  107.0 8.7 %collective-permute-start.9 = (f32[2,8,2048]{2,1,0:T(8,128)S(1)}, f32[2,8,2048]{2,1,0:T(8,128)S(1)}, u32[]{:S(2)}, u32[]{:S(2)}) collective-permute-start(f32[2,8,2048]{2,1,0:T(8,128)S(1)} %add.15.own_ref), channel_id=1, source_target_pairs={{0,16},{16,0},{32,48},{48,32},{64,80},{80,64},{96,112},{112,96},{1... | collective-permute-start | bytes 393224 | tf_op jit(solution)/shard_map/ppermute | solution.py:481
  108.0 1.6 %copy-start.1 = (f32[4,8,8,2048]{3,2,1,0:T(8,128)S(1)}, f32[4,8,8,2048]{3,2,1,0:T(8,128)}, u32[]{:S(2)}) copy-start(f32[4,8,8,2048]{3,2,1,0:T(8,128)} %copy-done) | copy-start | bytes 6291460
